TPU v7x, 32 devices: a whole 2x2x4 slice. The times are simulated.
32 devices in a mesh: seq: 8 (over z, y), head: 4 (over x, core).
Axes of the slice: x: 2, y: 2, z: 4, core: 2. Of those that a mesh axis runs over, the one named last changes fastest.
Arguments:
- queries: bfloat16 [8192, 1024], P('seq', 'head'), may hold values from -0.69921875 to 0.69921875
- key_vectors: bfloat16 [8192, 1024], P('seq', 'head'), may hold values from -0.69921875 to 0.69921875
- values: bfloat16 [8192, 1024], P('seq', 'head'), may hold values from -0.69921875 to 0.69921875
- out_grad: bfloat16 [8192, 1024], P('seq', 'head'), may hold values from -6 to 6
- level_coef: float32 [17, 8192], P(None, 'seq'), may hold values from 0.25 to 4
- saved_states: bfloat16 [8, 6, 8, 128, 128], P('seq', None, 'head'), may hold values from -0.079589844 to 0.079589844
Outputs:
- query_grad: bfloat16 [8192, 1024], P('seq', 'head')
- key_grad: bfloat16 [8192, 1024], P('seq', 'head')
- value_grad: bfloat16 [8192, 1024], P('seq', 'head')
- coef_grad: float32 [17, 8192], P(None, 'seq')
All inputs are finite; a program needn't handle non-finite values.
Results may differ from a plain program's by a relative error of at most 0.0053.
Values sent between devices are 32-bit elements; how exact they have to be, the bound alone decides.
No kernel may reach another device: no remote copies, remote signals or barrier semaphores. Data moves between devices by JAX's collectives and lax.ppermute only.
A program may use at most 128 MiB of HBM per device.

v0:
```python
import jax
import jax.numpy as jnp
from jax import lax
from jax.sharding import PartitionSpec as P


def partner(value, axis, stride):
    mask = 2**stride
    pairs = [(source, source ^ mask) for source in range(lax.axis_size(axis))]
    return lax.ppermute(value, axis, pairs)


def level_weight(level_idx):
    if level_idx == 0:
        return 1.0
    return 2.0 ** (-(level_idx - 1) / 2.0)


def level_table(row_pos, col_pos, local_levels):
    mixed = jnp.bitwise_xor(row_pos[:, None], col_pos[None, :])
    levels = jnp.zeros(mixed.shape, jnp.int32)
    for bit_pos in range(local_levels - 1):
        levels = levels + (jnp.right_shift(mixed, bit_pos) > 0).astype(jnp.int32)
    return levels


def coef_table(levels, gate_rows, local_levels):
    level_mix = jnp.zeros(levels.shape, jnp.float32)
    for level_idx in range(local_levels):
        level_mix = jnp.where(
            levels == level_idx, gate_rows[level_idx][:, None] * level_weight(level_idx), level_mix
        )
    return level_mix


def level_sums(products, row_pos, local_levels):
    row_total = products.shape[0]
    column_ids = jnp.arange(products.shape[1], dtype=jnp.int32)
    per_level = [jnp.sum(jnp.where(column_ids[None, :] == row_pos[:, None], products, 0.0), axis=1)]
    blocked = products
    for level_idx in range(1, local_levels):
        if level_idx > 1:
            blocked = blocked.reshape(row_total, blocked.shape[1] // 2, 2).sum(axis=2)
        sibling = jnp.bitwise_xor(jnp.right_shift(row_pos, level_idx - 1), 1)
        block_ids = jnp.arange(blocked.shape[1], dtype=jnp.int32)
        picked = jnp.sum(jnp.where(block_ids[None, :] == sibling[:, None], blocked, 0.0), axis=1)
        per_level.append(picked * level_weight(level_idx))
    return jnp.stack(per_level)


def shards(queries, key_vectors, values, out_grad, level_coef, saved_states):
    tokens = queries.shape[0]
    cross_levels = saved_states.shape[1]
    head_count = saved_states.shape[2]
    key_width = saved_states.shape[3]
    value_width = saved_states.shape[4]
    local_levels = level_coef.shape[0] - cross_levels
    query_heads = queries.reshape(tokens, head_count, key_width)
    key_heads = key_vectors.reshape(tokens, head_count, key_width)
    value_heads = values.reshape(tokens, head_count, value_width)
    grad_heads = out_grad.reshape(tokens, head_count, value_width)
    states = saved_states[0]
    shard_idx = lax.axis_index("seq")
    level_ids = jnp.arange(cross_levels, dtype=jnp.int32)
    bit_flags = jnp.bitwise_and(jnp.right_shift(shard_idx, level_ids), 1).astype(jnp.float32)
    cross_gates = level_coef[local_levels:]
    scaled = (cross_gates[:, :, None, None] * grad_heads).astype(jnp.bfloat16)
    state_grads = jnp.einsum(
        "thd,jthe->jhde", query_heads, scaled, preferred_element_type=jnp.float32
    )
    weight_list = jnp.array(
        [level_weight(local_levels + level_idx) for level_idx in range(cross_levels)], jnp.float32
    )
    contrib = state_grads * (weight_list * bit_flags)[:, None, None, None]
    bit_count = lax.axis_size("seq").bit_length() - 1
    grad_state = jnp.zeros((head_count, key_width, value_width), jnp.float32)
    for level_idx in range(bit_count):
        partial_value = contrib[level_idx]
        for bit_pos in range(level_idx):
            partial_value = partial_value + partner(partial_value, "seq", bit_pos)
        received = partner(partial_value, "seq", level_idx)
        own_bit = jnp.bitwise_and(jnp.right_shift(shard_idx, level_idx), 1)
        grad_state = grad_state + jnp.where(own_bit == 0, received, 0.0)
    projected = jnp.einsum("the,jhde->jthd", grad_heads, states, preferred_element_type=jnp.float32)
    gate_rows = cross_gates * bit_flags[:, None]
    query_cross = jnp.sum(gate_rows[:, :, None, None] * projected, axis=0)
    cross_grads = bit_flags[:, None] * jnp.sum(projected * query_heads[None], axis=(2, 3))
    block_rows = min(512, tokens)
    query_parts = []
    coef_parts = []
    key_local = jnp.zeros((tokens, head_count, key_width), jnp.float32)
    value_local = jnp.zeros((tokens, head_count, value_width), jnp.float32)
    for row_start in range(0, tokens, block_rows):
        key_end = row_start + block_rows
        row_pos = row_start + jnp.arange(block_rows, dtype=jnp.int32)
        col_pos = jnp.arange(key_end, dtype=jnp.int32)
        levels = level_table(row_pos, col_pos, local_levels)
        causal = col_pos[None, :] <= row_pos[:, None]
        level_mix = jnp.where(
            causal,
            coef_table(levels, level_coef[:local_levels, row_start:key_end], local_levels),
            0.0,
        )
        query_rows = query_heads[row_start:key_end]
        grad_rows = grad_heads[row_start:key_end]
        key_cols = key_heads[:key_end]
        value_cols = value_heads[:key_end]
        scores = jnp.einsum(
            "thd,shd->hts", query_rows, key_cols, preferred_element_type=jnp.float32
        )
        grad_scores = jnp.einsum(
            "the,she->hts", grad_rows, value_cols, preferred_element_type=jnp.float32
        )
        grad_weights = (level_mix[None] * grad_scores).astype(jnp.bfloat16)
        weights = (level_mix[None] * scores).astype(jnp.bfloat16)
        query_parts.append(
            jnp.einsum("hts,shd->thd", grad_weights, key_cols, preferred_element_type=jnp.float32)
        )
        key_local = key_local.at[:key_end].add(
            jnp.einsum("hts,thd->shd", grad_weights, query_rows, preferred_element_type=jnp.float32)
        )
        value_local = value_local.at[:key_end].add(
            jnp.einsum("hts,the->she", weights, grad_rows, preferred_element_type=jnp.float32)
        )
        products = jnp.where(causal, jnp.sum(scores * grad_scores, axis=0), 0.0)
        coef_parts.append(level_sums(products, row_pos, local_levels))
    local_grads = jnp.concatenate(coef_parts, axis=1)
    coef_local = jnp.concatenate([local_grads, cross_grads], axis=0)
    coef_grad = lax.psum(coef_local, "head")
    state_data = grad_state.astype(jnp.bfloat16)
    query_total = jnp.concatenate(query_parts, axis=0) + query_cross
    key_total = key_local + jnp.einsum(
        "she,hde->shd", value_heads, state_data, preferred_element_type=jnp.float32
    )
    value_total = value_local + jnp.einsum(
        "shd,hde->she", key_heads, state_data, preferred_element_type=jnp.float32
    )
    query_grad = query_total.astype(jnp.bfloat16).reshape(tokens, head_count * key_width)
    key_grad = key_total.astype(jnp.bfloat16).reshape(tokens, head_count * key_width)
    value_grad = value_total.astype(jnp.bfloat16).reshape(tokens, head_count * value_width)
    return (query_grad, key_grad, value_grad, coef_grad)


def solution(mesh):
    in_specs = (
        P("seq", "head"),
        P("seq", "head"),
        P("seq", "head"),
        P("seq", "head"),
        P(None, "seq"),
        P("seq", None, "head", None, None),
    )
    out_specs = (P("seq", "head"), P("seq", "head"), P("seq", "head"), P(None, "seq"))
    return jax.shard_map(shards, mesh=mesh, in_specs=in_specs, out_specs=out_specs, check_vma=False)
```

profile of v0, /device:TPU:0, one launch (start us, length us, event | category | flops | bytes accessed | tf_op | source)
XLA Modules:
  0.0 119.2 jit_solution(2505414521914661350)
XLA Ops:
  7.3 0.7 fusion.42
  8.0 1.2 reshape.1156
  9.1 1.2 reshape.1155
  10.8 0.7 fusion.48
  11.4 1.0 fusion.17
  12.5 0.7 slice_bitcast_fusion.2
  13.5 3.0 %collective-permute-start = (f32[2,128,128]{1,2,0:T(8,128)}, f32[2,128,128]{1,2,0:T(8,128)}, u32[]{:S(2)}, u32[]{:S(2)}) collective-permute-start(f32[2,128,128]{1,2,0:T(8,128)} %get-tuple-element.91), channel_id=1, source_target_pairs={{0,4},{4,0},{8,12},{12,8},{16,20},{20,16},{24,28},{28,24},{1,5},{5... | collective-permute-start | bytes 393224 | tf_op jit(solution)/shard_map/ppermute | solution.py:10
  16.5 2.0 %collective-permute-start.1 = (f32[2,128,128]{1,2,0:T(8,128)}, f32[2,128,128]{1,2,0:T(8,128)}, u32[]{:S(2)}, u32[]{:S(2)}) collective-permute-start(f32[2,128,128]{1,2,0:T(8,128)} %get-tuple-element.93), channel_id=1, source_target_pairs={{0,4},{4,0},{8,12},{12,8},{16,20},{20,16},{24,28},{28,24},{1,5},{5... | collective-permute-start | bytes 393224 | tf_op jit(solution)/shard_map/ppermute | solution.py:10
  19.7 0.6 shift-right-arithmetic_xor_fusion.16
  20.3 0.6 shift-right-arithmetic_xor_fusion.15
  22.0 0.6 shift-right-arithmetic_xor_fusion.12
  22.6 0.6 shift-right-arithmetic_xor_fusion.11
  23.2 0.6 shift-right-arithmetic_xor_fusion.10
  26.1 0.6 shift-right-arithmetic_xor_fusion.4
  26.7 0.6 shift-right-arithmetic_xor_fusion.3
  27.3 0.6 shift-right-arithmetic_xor_fusion.2
  27.9 0.6 shift-right-arithmetic_xor_fusion.1
  29.1 0.6 shift-right-arithmetic_xor_fusion.9
  29.7 0.6 slice_multiply_fusion.16
  30.3 0.7 slice_multiply_fusion.17
  30.9 0.7 multiply_add_fusion.1
  31.6 0.7 multiply_add_fusion
  32.3 1.1 copy.130
  33.4 0.7 fusion.46
  34.2 0.7 fusion.47
  34.9 0.9 copy.115
  35.9 0.8 fusion.28
  37.1 3.1 %multiply_reduce_fusion = (f32[512,1024]{1,0:T(8,128)S(1)}, f32[2,512,1024]{2,1,0:T(8,128)}) fusion(f32[2,512,1024]{2,1,0:T(8,128)S(1)} %fusion.28, bf16[512,2,128]{0,2,1:T(8,128)(2,1)S(1)} %bitcast.192, bf16[1024,256]{1,0:T(8,128)(2,1)S(1)} %copy-done.8), kind=kOutput, calls=%fused_computation.5 | convolution fusion | flops 270008320 | bytes 11272192 | tf_op jit(solution)/shard_map/thd,shd->hts/dot_general | solution.py:108
  40.3 2.1 %copy.128 = f32[512,1024]{0,1:T(8,128)} copy(f32[512,1024]{1,0:T(8,128)S(1)} %get-tuple-element.125) | data formatting | bytes 4194304 | tf_op jit(solution)/shard_map/reduce_sum | solution.py:125
  42.3 3.5 %reduce_sum.426 = f32[512,512,2]{0,2,1:T(2,128)} reshape(f32[512,1024]{0,1:T(8,128)} %copy.128) | data formatting | bytes 4194304 | tf_op jit(solution)/shard_map/reduce_sum | solution.py:125
  45.8 4.4 %fusion.5 = f32[512,512]{0,1:T(8,128)S(1)} fusion(f32[512,512,2]{0,2,1:T(2,128)} %reduce_sum.426, s32[512]{0:T(512)S(1)} %get-tuple-element.130, s32[512,2]{1,0:T(8,128)S(1)} %copy-done.31), kind=kLoop, calls=%fused_computation.12 | loop fusion | flops 1310720 | bytes 3151872 | tf_op jit(solution)/shard_map/reduce_sum | solution.py:43
  50.3 1.6 %reshape.1166 = f32[512,256,2]{0,2,1:T(2,128)} reshape(f32[512,512]{0,1:T(8,128)S(1)} %fusion.5) | data formatting | bytes 2097152 | tf_op jit(solution)/shard_map/reshape | solution.py:43
  51.9 1.3 %copy.129 = f32[512,512]{1,0:T(8,128)} copy(f32[512,512]{0,1:T(8,128)S(1)} %fusion.5) | data formatting | bytes 2097152 | tf_op jit(solution)/shard_map/reduce_sum | solution.py:43
  53.9 2.2 %fusion.1 = (f32[6,1024]{1,0:T(8,128)S(1)}, f32[1024,2,128]{0,2,1:T(8,128)}) fusion(f32[1024,2,128]{0,2,1:T(8,128)S(1)} %convert_element_type.621, f32[6,1024]{1,0:T(8,128)S(1)} %copy-done.37, bf16[1024,2,128,1]{2,1,0,3:T(2,128)(2,1)S(1)} %bitcast.201, bf16[1,6,2,128,128]{4,3,2,1,0:T(8,128)(2,1)S(1)} %copy-done), kind=kOutput, calls=%fused_computation.3 | convolution fusion | flops 408676352 | bytes 3063808 | tf_op jit(solution)/shard_map/the,jhde->jthd/dot_general | solution.py:84
  56.1 0.7 broadcast_multiply_fusion
  57.8 2.0 %multiply_reduce_fusion.1 = (f32[512,512]{1,0:T(8,128)S(1)}, f32[2,512,512]{2,1,0:T(8,128)}) fusion(f32[2,512,512]{2,1,0:T(8,128)S(1)} %fusion.49, bf16[512,2,128]{0,2,1:T(8,128)(2,1)S(1)} %bitcast.196, bf16[512,2,128]{0,2,1:T(8,128)(2,1)S(1)} %bitcast.194), kind=kOutput, calls=%fused_computation.18 | convolution fusion | flops 135004160 | bytes 5767168 | tf_op jit(solution)/shard_map/thd,shd->hts/dot_general | solution.py:108
  60.2 0.6 reduce_sum.404
  60.9 2.7 %fusion.18 = f32[512,256]{0,1:T(8,128)S(1)} fusion(f32[512,256,2]{0,2,1:T(2,128)S(1)} %reduce_sum.404, s32[256,2]{1,0:T(8,128)} %multiply_add_fusion.1), kind=kLoop, calls=%fused_computation.52 | loop fusion | flops 655360 | bytes 1574912 | tf_op jit(solution)/shard_map/reduce_sum | solution.py:43
  64.1 0.6 reduce_sum.407
  66.5 1.2 %reduce_sum.429 = f32[512,256]{0,1:T(8,128)S(1)} reduce(f32[512,256,2]{0,2,1:T(2,128)S(1)} %copy-done.11, f32[]{:T(128)} %constant.198.clone.1), dimensions={2}, to_apply=%region_26.27 | reduce | flops 131072 | bytes 1572868 | tf_op jit(solution)/shard_map/reduce_sum | solution.py:43
  68.4 0.6 reduce_sum.431
  71.0 7.0 %select_reduce_fusion = (f32[512]{0:T(512)S(1)}, f32[512]{0:T(512)S(1)}, f32[512,1024]{1,0:T(8,128)S(1)}) fusion(f32[512,1024]{1,0:T(8,128)} %copy-done.5, s32[512]{0:T(512)S(1)} %copy-done.55, s32[512]{0:T(512)S(1)} %get-tuple-element.130, f32[512]{0:T(512)S(1)} %bitcast.234, f32[512]{0:T(512)S(1)} %bitcast.221, f32[512]{0:T(512)S(1)} %bitcast.222, ...), kind=kLoop, calls=%fused_computation.14 | loop fusion | flops 37223424 | bytes 4225024 | tf_op jit(solution)/shard_map/reduce_sum | solution.py:46
  78.0 0.7 pad_maximum_fusion
  78.8 1.5 %select_select_fusion.1 = f32[512,512]{1,0:T(8,128)S(1)} fusion(f32[512]{0:T(512)S(1)} %bitcast.213, f32[512]{0:T(512)S(1)} %bitcast.214, f32[512]{0:T(512)S(1)} %bitcast.215, f32[512]{0:T(512)S(1)} %bitcast.216, f32[512]{0:T(512)S(1)} %bitcast.217, f32[512]{0:T(512)S(1)} %bitcast.218, f32[512]{0:T(512)S(1)} %bitcast.219, f32[512]{0:T(512)S(1)} %bitcast.220, ...), kind=kLoop, calls=%fused_computation.64 | loop fusion | flops 16777216 | bytes 1071104 | tf_op jit(solution)/shard_map/jit(_where)/select_n | solution.py:99
  80.3 2.2 %convolution_bitcast_fusion.4 = f32[512,2,128]{0,2,1:T(8,128)S(1)} fusion(bf16[512,2,128]{0,2,1:T(8,128)(2,1)S(1)} %bitcast.197, f32[2,512,512]{2,1,0:T(8,128)} %copy-done.3, f32[512,512]{1,0:T(8,128)S(1)} %select_select_fusion.1), kind=kOutput, calls=%fused_computation.51 | convolution fusion | flops 135266304 | bytes 3932160 | tf_op jit(solution)/shard_map/hts,thd->shd/dot_general | solution.py:120
  83.7 1.8 %fusion.13 = f32[1024,2,128]{0,2,1:T(8,128)} fusion(bf16[512,2,128]{0,2,1:T(8,128)(2,1)S(1)} %bitcast.193, f32[512,2,128]{0,2,1:T(8,128)S(1)} %convolution_bitcast_fusion.4, f32[2,512,1024]{2,1,0:T(8,128)S(1)} %copy-done.2, f32[512,1024]{1,0:T(8,128)S(1)} %get-tuple-element.124), kind=kOutput, calls=%fused_computation.45 | convolution fusion | flops 270794752 | bytes 8126464 | tf_op jit(solution)/shard_map/hts,thd->shd/dot_general | solution.py:120
  85.4 0.8 copy-done.6
  86.3 1.8 %fusion.10 = f32[1024,2,128]{0,2,1:T(8,128)} fusion(bf16[512,2,128]{0,2,1:T(8,128)(2,1)S(1)} %bitcast.191, f32[2,512,1024]{2,1,0:T(8,128)S(1)} %copy-done.6, f32[512,1024]{1,0:T(8,128)S(1)} %get-tuple-element.124, f32[512,2,128]{0,2,1:T(8,128)S(1)} %convolution_bitcast_fusion.3), kind=kOutput, calls=%fused_computation.42 | convolution fusion | flops 270794752 | bytes 8126464 | tf_op jit(solution)/shard_map/hts,the->she/dot_general | solution.py:123
  88.0 0.9 fusion.22
  89.0 1.8 %fusion.43 = (f32[2,128,128]{1,2,0:T(8,128)}, f32[2,128,128]{1,2,0:T(8,128)S(1)}) fusion(f32[2,128,128]{1,2,0:T(8,128)} %collective-permute-done.1, f32[6,2,128,128]{2,3,0,1:T(8,128)} %copy-done.34, f32[2,128,128]{1,2,0:T(8,128)} %collective-permute-done.3), kind=kLoop, calls=%fused_computation.196 | loop fusion | flops 65536 | bytes 786432 | tf_op jit(solution)/shard_map/add | solution.py:80
  90.8 1.6 %collective-permute-start.4 = (f32[2,128,128]{1,2,0:T(8,128)S(1)}, f32[2,128,128]{1,2,0:T(8,128)S(1)}, u32[]{:S(2)}, u32[]{:S(2)}) collective-permute-start(f32[2,128,128]{1,2,0:T(8,128)S(1)} %get-tuple-element.95), channel_id=1, source_target_pairs={{0,8},{4,12},{8,0},{12,4},{16,24},{20,28},{24,16},{28,20},{1,9},{5... | collective-permute-start | bytes 393224 | tf_op jit(solution)/shard_map/ppermute | solution.py:10
  92.9 1.6 %copy.113 = f32[1024,256]{1,0:T(8,128)S(1)} copy(f32[1024,256]{0,1:T(8,128)} %bitcast.207) | data formatting | bytes 2097152 | tf_op jit(solution)/shard_map/reduce_sum | solution.py:86
  94.4 1.0 copy.109
  95.4 1.0 copy.110
  96.9 0.7 add.673
  97.6 2.6 %collective-permute-start.5 = (f32[2,128,128]{1,2,0:T(8,128)}, f32[2,128,128]{1,2,0:T(8,128)}, u32[]{:S(2)}, u32[]{:S(2)}) collective-permute-start(f32[2,128,128]{1,2,0:T(8,128)} %add.673), channel_id=1, source_target_pairs={{0,16},{4,20},{8,24},{12,28},{16,0},{20,4},{24,8},{28,12},{1,17},{... | collective-permute-start | bytes 393224 | tf_op jit(solution)/shard_map/ppermute | solution.py:10
  100.1 2.1 %fusion.19 = bf16[1024,256]{1,0:T(8,128)(2,1)} fusion(f32[1024,256]{1,0:T(8,128)S(1)} %copy.113, f32[512,256]{1,0:T(8,128)} %copy.110, f32[512,256]{1,0:T(8,128)} %copy.109), kind=kLoop, calls=%fused_computation.54 | loop fusion | flops 786432 | bytes 2621440 | tf_op jit(solution)/shard_map/convert_element_type | solution.py:138
  102.8 1.4 %collective-permute-done.5 = f32[2,128,128]{1,2,0:T(8,128)} collective-permute-done((f32[2,128,128]{1,2,0:T(8,128)}, f32[2,128,128]{1,2,0:T(8,128)}, u32[]{:S(2)}, u32[]{:S(2)}) %collective-permute-start.5) | collective-permute-done | bytes 131104 | tf_op jit(solution)/shard_map/ppermute | solution.py:10
  104.3 1.1 add_convert_fusion
  105.3 1.5 %fusion.14 = bf16[1024,2,128]{0,2,1:T(8,128)(2,1)S(1)} fusion(f32[1024,2,128]{0,2,1:T(8,128)} %fusion.10, bf16[2,128,128]{1,2,0:T(8,128)(2,1)S(1)} %add_convert_fusion, bf16[1024,256]{1,0:T(8,128)(2,1)S(1)} %copy-done.9), kind=kOutput, calls=%fused_computation.46 | convolution fusion | flops 67633152 | bytes 2162688 | tf_op jit(solution)/shard_map/shd,hde->she/dot_general | solution.py:135
  107.2 1.0 copy.132
  108.2 1.0 copy.131
  109.2 1.6 %all-reduce.4.cloned.1.call-done = f32[17,1024]{1,0:T(8,128)} async-done(((f32[17,1024]{1,0:T(8,128)}), f32[17,1024]{1,0:T(8,128)}) %all-reduce.4.cloned.1.call-update) | async-done | bytes 69648 | tf_op jit(solution)/shard_map/psum | solution.py:129
  110.9 1.5 %copy.186 = f32[17,1024]{1,0:T(8,128)} copy(f32[17,1024]{1,0:T(8,128)} %all-reduce.4.cloned.1.call-done) | data formatting | bytes 139264
  (257 shorter events, 15.6 us)
Async XLA Ops:
  7.2 46.7 %copy-start = (bf16[1,6,2,128,128]{4,3,2,1,0:T(8,128)(2,1)S(1)}, bf16[1,6,2,128,128]{4,3,2,1,0:T(8,128)(2,1)}, u32[]{:S(2)}) copy-start(bf16[1,6,2,128,128]{4,3,2,1,0:T(8,128)(2,1)} %param.24) | copy-start | bytes 1179652
  7.2 3.6 %copy-start.36 = (f32[17,1024]{1,0:T(8,128)S(1)}, f32[17,1024]{1,0:T(8,128)}, u32[]{:S(2)}) copy-start(f32[17,1024]{1,0:T(8,128)} %param.23) | copy-start | bytes 208900
  7.2 103.7 %all-reduce.4.cloned.1.call-start = ((), (), s32[]{:S(2)}) async-start(), calls=%async_computation | async-start | bytes 196608 | tf_op jit(solution)/shard_map/psum | solution.py:129
  7.3 5.2 %copy-start.77 = (f32[6]{0:T(128)}, f32[6]{0:T(128)S(1)}, u32[]{:S(2)}) copy-start(f32[6]{0:T(128)S(1)} %and_convert_fusion) | copy-start | bytes 76
  12.5 21.0 %copy-start.28 = (bf16[1024,256]{1,0:T(8,128)(2,1)S(1)}, bf16[1024,256]{1,0:T(8,128)(2,1)}, u32[]{:S(2)}) copy-start(bf16[1024,256]{1,0:T(8,128)(2,1)} %param.19) | copy-start | bytes 1572868
  12.5 21.7 %copy-start.29 = (bf16[1024,256]{1,0:T(8,128)(2,1)S(1)}, bf16[1024,256]{1,0:T(8,128)(2,1)}, u32[]{:S(2)}) copy-start(bf16[1024,256]{1,0:T(8,128)(2,1)} %param.22) | copy-start | bytes 1572868
  13.5 88.7 %collective-permute-start = (f32[2,128,128]{1,2,0:T(8,128)}, f32[2,128,128]{1,2,0:T(8,128)}, u32[]{:S(2)}, u32[]{:S(2)}) collective-permute-start(f32[2,128,128]{1,2,0:T(8,128)} %get-tuple-element.91), channel_id=1, source_target_pairs={{0,4},{4,0},{8,12},{12,8},{16,20},{20,16},{24,28},{28,24},{1,5},{5... | collective-permute-start | bytes 393224 | tf_op jit(solution)/shard_map/ppermute | solution.py:10
  16.5 72.5 %collective-permute-start.3 = (f32[2,128,128]{1,2,0:T(8,128)}, f32[2,128,128]{1,2,0:T(8,128)}, u32[]{:S(2)}, u32[]{:S(2)}) collective-permute-start(f32[2,128,128]{1,2,0:T(8,128)} %get-tuple-element.92), channel_id=1, source_target_pairs={{0,4},{4,0},{8,12},{12,8},{16,20},{20,16},{24,28},{28,24},{1,5},{5... | collective-permute-start | bytes 393224 | tf_op jit(solution)/shard_map/ppermute | solution.py:10
  16.5 72.5 %collective-permute-start.1 = (f32[2,128,128]{1,2,0:T(8,128)}, f32[2,128,128]{1,2,0:T(8,128)}, u32[]{:S(2)}, u32[]{:S(2)}) collective-permute-start(f32[2,128,128]{1,2,0:T(8,128)} %get-tuple-element.93), channel_id=1, source_target_pairs={{0,4},{4,0},{8,12},{12,8},{16,20},{20,16},{24,28},{28,24},{1,5},{5... | collective-permute-start | bytes 393224 | tf_op jit(solution)/shard_map/ppermute | solution.py:10
  33.4 2.5 %copy-start.13 = (bf16[1024,256]{1,0:T(8,128)(2,1)S(1)}, bf16[1024,256]{1,0:T(8,128)(2,1)}, u32[]{:S(2)}) copy-start(bf16[1024,256]{1,0:T(8,128)(2,1)} %param.21) | copy-start | bytes 1572868
  36.7 3.5 %copy-start.1 = (f32[2,512,1024]{2,1,0:T(8,128)}, f32[2,512,1024]{2,1,0:T(8,128)S(1)}, u32[]{:S(2)}) copy-start(f32[2,512,1024]{2,1,0:T(8,128)S(1)} %fusion.28) | copy-start | bytes 12582916
  42.3 3.5 %copy-start.31 = (s32[512,2]{1,0:T(8,128)S(1)}, s32[512,2]{1,0:T(8,128)}, u32[]{:S(2)}) copy-start(s32[512,2]{1,0:T(8,128)} %multiply_add_fusion) | copy-start | bytes 12292
  50.3 3.0 %copy-start.30 = (s32[256,2]{1,0:T(8,128)S(1)}, s32[256,2]{1,0:T(8,128)}, u32[]{:S(2)}) copy-start(s32[256,2]{1,0:T(8,128)} %multiply_add_fusion.1) | copy-start | bytes 6148
  50.3 3.1 %slice-start.1 = ((bf16[1024,256]{1,0:T(8,128)(2,1)}), bf16[512,256]{1,0:T(8,128)(2,1)S(1)}, s32[]{:S(2)}) async-start(bf16[1024,256]{1,0:T(8,128)(2,1)} %param.21), calls=%async_computation.2 | async-start | bytes 524288 | tf_op jit(solution)/shard_map/slice | solution.py:107
  50.3 3.3 %slice-start = ((bf16[1024,256]{1,0:T(8,128)(2,1)}), bf16[512,256]{1,0:T(8,128)(2,1)S(1)}, s32[]{:S(2)}) async-start(bf16[1024,256]{1,0:T(8,128)(2,1)} %param.20), calls=%async_computation.1 | async-start | bytes 524288 | tf_op jit(solution)/shard_map/slice | solution.py:106
  53.7 4.1 %copy-start.19 = (bf16[512,256]{0,1:T(8,128)(2,1)}, bf16[512,256]{0,1:T(8,128)(2,1)S(1)}, u32[]{:S(2)}) copy-start(bf16[512,256]{0,1:T(8,128)(2,1)S(1)} %copy.104) | copy-start | bytes 786436
  53.9 2.9 %copy-start.32 = (bf16[512,256]{1,0:T(8,128)(2,1)S(1)}, bf16[512,256]{1,0:T(8,128)(2,1)}, u32[]{:S(2)}) copy-start(bf16[512,256]{1,0:T(8,128)(2,1)} %get-tuple-element.96) | copy-start | bytes 786436
  53.9 3.1 %copy-start.33 = (bf16[512,256]{1,0:T(8,128)(2,1)S(1)}, bf16[512,256]{1,0:T(8,128)(2,1)}, u32[]{:S(2)}) copy-start(bf16[512,256]{1,0:T(8,128)(2,1)} %get-tuple-element.98) | copy-start | bytes 786436
  57.0 2.9 %copy-start.21 = (bf16[512,256]{0,1:T(8,128)(2,1)}, bf16[512,256]{0,1:T(8,128)(2,1)S(1)}, u32[]{:S(2)}) copy-start(bf16[512,256]{0,1:T(8,128)(2,1)S(1)} %copy.114) | copy-start | bytes 786436
  57.6 2.3 %copy-start.3 = (f32[2,512,512]{2,1,0:T(8,128)}, f32[2,512,512]{2,1,0:T(8,128)S(1)}, u32[]{:S(2)}) copy-start(f32[2,512,512]{2,1,0:T(8,128)S(1)} %fusion.49) | copy-start | bytes 6291460
  60.9 3.1 %copy-start.63 = (s32[512]{0:T(512)S(1)}, s32[512]{0:T(512)}, u32[]{:S(2)}) copy-start(s32[512]{0:T(512)} %shift-right-arithmetic_xor_fusion.17) | copy-start | bytes 6148
  63.6 2.3 %copy-start.76 = (s32[512]{0:T(512)S(1)}, s32[512]{0:T(512)}, u32[]{:S(2)}) copy-start(s32[512]{0:T(512)} %shift-right-arithmetic_xor_fusion.11) | copy-start | bytes 6148
  63.6 2.3 %copy-start.75 = (s32[512]{0:T(512)S(1)}, s32[512]{0:T(512)}, u32[]{:S(2)}) copy-start(s32[512]{0:T(512)} %shift-right-arithmetic_xor_fusion.10) | copy-start | bytes 6148
  64.1 2.5 %copy-start.11 = (f32[512,256,2]{0,2,1:T(2,128)S(1)}, f32[512,256,2]{0,2,1:T(2,128)}, u32[]{:S(2)}) copy-start(f32[512,256,2]{0,2,1:T(2,128)} %reshape.1166) | copy-start | bytes 3145732
  65.6 2.6 %copy-start.60 = (s32[512]{0:T(512)S(1)}, s32[512]{0:T(512)}, u32[]{:S(2)}) copy-start(s32[512]{0:T(512)} %shift-right-arithmetic_xor_fusion.7) | copy-start | bytes 6148
  66.5 2.7 %copy-start.58 = (s32[512]{0:T(512)S(1)}, s32[512]{0:T(512)}, u32[]{:S(2)}) copy-start(s32[512]{0:T(512)} %shift-right-arithmetic_xor_fusion.6) | copy-start | bytes 6148
  67.8 2.3 %copy-start.67 = (s32[512]{0:T(512)S(1)}, s32[512]{0:T(512)}, u32[]{:S(2)}) copy-start(s32[512]{0:T(512)} %shift-right-arithmetic_xor_fusion.2) | copy-start | bytes 6148
  67.8 2.4 %copy-start.74 = (s32[512]{0:T(512)S(1)}, s32[512]{0:T(512)}, u32[]{:S(2)}) copy-start(s32[512]{0:T(512)} %shift-right-arithmetic_xor_fusion.1) | copy-start | bytes 6148
  67.8 2.5 %copy-start.73 = (s32[512]{0:T(512)S(1)}, s32[512]{0:T(512)}, u32[]{:S(2)}) copy-start(s32[512]{0:T(512)} %shift-right-arithmetic_xor_fusion) | copy-start | bytes 6148
  68.3 2.5 %copy-start.45 = (f32[1,512]{1,0:T(1,128)S(1)}, f32[1,512]{1,0:T(1,128)}, u32[]{:S(2)}) copy-start(f32[1,512]{1,0:T(1,128)} %get-tuple-element.103) | copy-start | bytes 6148
  68.3 2.5 %copy-start.46 = (f32[1,512]{1,0:T(1,128)S(1)}, f32[1,512]{1,0:T(1,128)}, u32[]{:S(2)}) copy-start(f32[1,512]{1,0:T(1,128)} %get-tuple-element.104) | copy-start | bytes 6148
  68.3 2.5 %copy-start.47 = (f32[1,512]{1,0:T(1,128)S(1)}, f32[1,512]{1,0:T(1,128)}, u32[]{:S(2)}) copy-start(f32[1,512]{1,0:T(1,128)} %get-tuple-element.105) | copy-start | bytes 6148
  68.3 2.5 %copy-start.48 = (f32[1,512]{1,0:T(1,128)S(1)}, f32[1,512]{1,0:T(1,128)}, u32[]{:S(2)}) copy-start(f32[1,512]{1,0:T(1,128)} %get-tuple-element.106) | copy-start | bytes 6148
  68.3 2.5 %copy-start.49 = (f32[1,512]{1,0:T(1,128)S(1)}, f32[1,512]{1,0:T(1,128)}, u32[]{:S(2)}) copy-start(f32[1,512]{1,0:T(1,128)} %get-tuple-element.107) | copy-start | bytes 6148
  68.3 2.5 %copy-start.50 = (f32[1,512]{1,0:T(1,128)S(1)}, f32[1,512]{1,0:T(1,128)}, u32[]{:S(2)}) copy-start(f32[1,512]{1,0:T(1,128)} %get-tuple-element.108) | copy-start | bytes 6148
  68.4 2.5 %copy-start.51 = (f32[1,512]{1,0:T(1,128)S(1)}, f32[1,512]{1,0:T(1,128)}, u32[]{:S(2)}) copy-start(f32[1,512]{1,0:T(1,128)} %get-tuple-element.109) | copy-start | bytes 6148
  68.4 2.5 %copy-start.52 = (f32[1,512]{1,0:T(1,128)S(1)}, f32[1,512]{1,0:T(1,128)}, u32[]{:S(2)}) copy-start(f32[1,512]{1,0:T(1,128)} %get-tuple-element.110) | copy-start | bytes 6148
  68.4 2.5 %copy-start.53 = (f32[1,512]{1,0:T(1,128)S(1)}, f32[1,512]{1,0:T(1,128)}, u32[]{:S(2)}) copy-start(f32[1,512]{1,0:T(1,128)} %get-tuple-element.111) | copy-start | bytes 6148
  68.4 2.5 %copy-start.54 = (f32[1,512]{1,0:T(1,128)S(1)}, f32[1,512]{1,0:T(1,128)}, u32[]{:S(2)}) copy-start(f32[1,512]{1,0:T(1,128)} %get-tuple-element.112) | copy-start | bytes 6148
  68.4 2.5 %copy-start.55 = (s32[512]{0:T(512)S(1)}, s32[512]{0:T(512)}, u32[]{:S(2)}) copy-start(s32[512]{0:T(512)} %get-tuple-element.129) | copy-start | bytes 6148
  68.4 2.5 %copy-start.66 = (f32[1,512]{1,0:T(1,128)S(1)}, f32[1,512]{1,0:T(1,128)}, u32[]{:S(2)}) copy-start(f32[1,512]{1,0:T(1,128)} %get-tuple-element.123) | copy-start | bytes 6148
  70.9 7.1 %copy-start.35 = (f32[6,1024]{1,0:T(8,128)S(1)}, f32[6,1024]{1,0:T(8,128)}, u32[]{:S(2)}) copy-start(f32[6,1024]{1,0:T(8,128)} %broadcast_multiply_fusion) | copy-start | bytes 73732
  70.9 7.8 %copy-start.38 = (f32[1,512]{1,0:T(1,128)S(1)}, f32[1,512]{1,0:T(1,128)}, u32[]{:S(2)}) copy-start(f32[1,512]{1,0:T(1,128)} %get-tuple-element.114) | copy-start | bytes 6148
  70.9 7.8 %copy-start.39 = (f32[1,512]{1,0:T(1,128)S(1)}, f32[1,512]{1,0:T(1,128)}, u32[]{:S(2)}) copy-start(f32[1,512]{1,0:T(1,128)} %get-tuple-element.115) | copy-start | bytes 6148
  70.9 7.8 %copy-start.40 = (f32[1,512]{1,0:T(1,128)S(1)}, f32[1,512]{1,0:T(1,128)}, u32[]{:S(2)}) copy-start(f32[1,512]{1,0:T(1,128)} %get-tuple-element.116) | copy-start | bytes 6148
  70.9 7.8 %copy-start.41 = (f32[1,512]{1,0:T(1,128)S(1)}, f32[1,512]{1,0:T(1,128)}, u32[]{:S(2)}) copy-start(f32[1,512]{1,0:T(1,128)} %get-tuple-element.117) | copy-start | bytes 6148
  71.0 7.8 %copy-start.42 = (f32[1,512]{1,0:T(1,128)S(1)}, f32[1,512]{1,0:T(1,128)}, u32[]{:S(2)}) copy-start(f32[1,512]{1,0:T(1,128)} %get-tuple-element.118) | copy-start | bytes 6148
  71.0 7.8 %copy-start.43 = (f32[1,512]{1,0:T(1,128)S(1)}, f32[1,512]{1,0:T(1,128)}, u32[]{:S(2)}) copy-start(f32[1,512]{1,0:T(1,128)} %get-tuple-element.119) | copy-start | bytes 6148
  71.0 7.8 %copy-start.44 = (f32[1,512]{1,0:T(1,128)S(1)}, f32[1,512]{1,0:T(1,128)}, u32[]{:S(2)}) copy-start(f32[1,512]{1,0:T(1,128)} %get-tuple-element.120) | copy-start | bytes 6148
  71.0 7.8 %copy-start.64 = (f32[1,512]{1,0:T(1,128)S(1)}, f32[1,512]{1,0:T(1,128)}, u32[]{:S(2)}) copy-start(f32[1,512]{1,0:T(1,128)} %get-tuple-element.121) | copy-start | bytes 6148
  71.0 7.8 %copy-start.65 = (f32[1,512]{1,0:T(1,128)S(1)}, f32[1,512]{1,0:T(1,128)}, u32[]{:S(2)}) copy-start(f32[1,512]{1,0:T(1,128)} %get-tuple-element.122) | copy-start | bytes 6148
  71.0 9.3 %copy-start.22 = (bf16[512,256]{0,1:T(8,128)(2,1)S(1)}, bf16[512,256]{0,1:T(8,128)(2,1)}, u32[]{:S(2)}) copy-start(bf16[512,256]{0,1:T(8,128)(2,1)} %copy-done.21) | copy-start | bytes 786436
  78.8 3.7 %copy-start.7 = (f32[2,512,512]{2,1,0:T(8,128)S(1)}, f32[2,512,512]{2,1,0:T(8,128)}, u32[]{:S(2)}) copy-start(f32[2,512,512]{2,1,0:T(8,128)} %get-tuple-element.128) | copy-start | bytes 6291460
  78.8 3.7 %copy-start.24 = (bf16[512,256]{0,1:T(8,128)(2,1)S(1)}, bf16[512,256]{0,1:T(8,128)(2,1)}, u32[]{:S(2)}) copy-start(bf16[512,256]{0,1:T(8,128)(2,1)} %copy-done.23) | copy-start | bytes 786436
  80.3 2.9 %copy-start.2 = (f32[2,512,1024]{2,1,0:T(8,128)S(1)}, f32[2,512,1024]{2,1,0:T(8,128)}, u32[]{:S(2)}) copy-start(f32[2,512,1024]{2,1,0:T(8,128)} %copy-done.1) | copy-start | bytes 12582916
  83.7 2.6 %copy-start.6 = (f32[2,512,1024]{2,1,0:T(8,128)S(1)}, f32[2,512,1024]{2,1,0:T(8,128)}, u32[]{:S(2)}) copy-start(f32[2,512,1024]{2,1,0:T(8,128)} %get-tuple-element.126) | copy-start | bytes 12582916
  83.7 2.6 %copy-start.16 = (bf16[512,256]{0,1:T(8,128)(2,1)S(1)}, bf16[512,256]{0,1:T(8,128)(2,1)}, u32[]{:S(2)}) copy-start(bf16[512,256]{0,1:T(8,128)(2,1)} %copy-done.15) | copy-start | bytes 786436
  88.0 4.3 %copy-start.4 = (f32[2,512,512]{2,1,0:T(8,128)S(1)}, f32[2,512,512]{2,1,0:T(8,128)}, u32[]{:S(2)}) copy-start(f32[2,512,512]{2,1,0:T(8,128)} %copy-done.3) | copy-start | bytes 6291460
  88.0 4.3 %copy-start.20 = (bf16[512,256]{0,1:T(8,128)(2,1)S(1)}, bf16[512,256]{0,1:T(8,128)(2,1)}, u32[]{:S(2)}) copy-start(bf16[512,256]{0,1:T(8,128)(2,1)} %copy-done.19) | copy-start | bytes 786436
  90.8 6.1 %collective-permute-start.4 = (f32[2,128,128]{1,2,0:T(8,128)S(1)}, f32[2,128,128]{1,2,0:T(8,128)S(1)}, u32[]{:S(2)}, u32[]{:S(2)}) collective-permute-start(f32[2,128,128]{1,2,0:T(8,128)S(1)} %get-tuple-element.95), channel_id=1, source_target_pairs={{0,8},{4,12},{8,0},{12,4},{16,24},{20,28},{24,16},{28,20},{1,9},{5... | collective-permute-start | bytes 393224 | tf_op jit(solution)/shard_map/ppermute | solution.py:10
  96.4 6.4 %collective-permute-start.2 = (f32[2,128,128]{1,2,0:T(8,128)}, f32[2,128,128]{1,2,0:T(8,128)}, u32[]{:S(2)}, u32[]{:S(2)}) collective-permute-start(f32[2,128,128]{1,2,0:T(8,128)} %get-tuple-element.94), channel_id=1, source_target_pairs={{0,8},{4,12},{8,0},{12,4},{16,24},{20,28},{24,16},{28,20},{1,9},{5... | collective-permute-start | bytes 393224 | tf_op jit(solution)/shard_map/ppermute | solution.py:10
  97.5 9.3 %copy-start.12 = (f32[1024,2,128]{0,2,1:T(8,128)S(1)}, f32[1024,2,128]{0,2,1:T(8,128)}, u32[]{:S(2)}) copy-start(f32[1024,2,128]{0,2,1:T(8,128)} %fusion.13) | copy-start | bytes 3145732
  97.5 9.3 %copy-start.14 = (bf16[1024,256]{1,0:T(8,128)(2,1)S(1)}, bf16[1024,256]{1,0:T(8,128)(2,1)}, u32[]{:S(2)}) copy-start(bf16[1024,256]{1,0:T(8,128)(2,1)} %param.21) | copy-start | bytes 1572868
  97.6 6.7 %collective-permute-start.5 = (f32[2,128,128]{1,2,0:T(8,128)}, f32[2,128,128]{1,2,0:T(8,128)}, u32[]{:S(2)}, u32[]{:S(2)}) collective-permute-start(f32[2,128,128]{1,2,0:T(8,128)} %add.673), channel_id=1, source_target_pairs={{0,16},{4,20},{8,24},{12,28},{16,0},{20,4},{24,8},{28,12},{1,17},{... | collective-permute-start | bytes 393224 | tf_op jit(solution)/shard_map/ppermute | solution.py:10
  (24 other events, 42.1 us)
Sparse Core Ops, SparseCore 0:
  78.8 31.9 all-reduce.3
where the time goes:
time: 120 us; the launch traced here: 119 us
  other arithmetic  42.9 us (36%)
  local copies, waits for them, and re-layouts  28.4 us (24%)
  matrix products  19 us (16%)
  between operations  15.6 us (13%)
  starting transfers between devices  9.67 us (8%)
  waiting for transfers between devices  3.65 us (3%)
    reduce_sum x18, other arithmetic, level_sums(): blocked = blocked.reshape(row_total, blocked.shape[1] // 2, 2).sum(axis=2)  11.2 us
    xor x19, other arithmetic, level_sums(): sibling = jnp.bitwise_xor(jnp.right_shift(row_pos, level_idx - 1), 1)  11.1 us
    ppermute x6, starting transfers between devices, partner(): return lax.ppermute(value, axis, pairs)  9.63 us
    reduce_sum x18, other arithmetic, level_sums(): jnp.sum(jnp.where(block_ids[None, :] == sibling[:, None], blocked, 0.0),...  7.85 us
    unnamed x164, local copies, waits for them, and re-layouts  6.69 us
    reduce_sum x4, local copies, waits for them, and re-layouts, shards(): products = jnp.where(causal, jnp.sum(scores * grad_scores, axis=0), 0.0)  6.52 us
    dot_general x2, matrix products, shards(): jnp.einsum('thd,shd->hts', query_rows, key_cols, preferred_element_type=j...  5.18 us
    dot_general x2, matrix products, shards(): jnp.einsum('hts,thd->shd', grad_weights, query_rows, preferred_element_ty...  3.97 us
  transfers between devices with their start and end apart: 7, of which 3 were waited for; matrix products, arithmetic and copies ran while one was open for 67% of the time, Pallas kernels for 0%

commit v1 on v0

v1 whole, which is shorter than its diff:
```python
import functools

import jax
import jax.numpy as jnp
from jax import lax
from jax.experimental import pallas as pl
from jax.experimental.pallas import tpu as pltpu
from jax.sharding import PartitionSpec as P

LANES = 128


def level_weight(level_idx):
    if level_idx == 0:
        return 1.0
    return 2.0 ** (-(level_idx - 1) / 2.0)


def dot(lhs, rhs):
    return jnp.dot(lhs, rhs, preferred_element_type=jnp.float32)


def state_kernel(local_levels, query_ref, grad_ref, gates_ref, *out_refs):
    grad_t = grad_ref[...].T.astype(jnp.float32)
    query = query_ref[...]
    for level_idx, out_ref in enumerate(out_refs):
        row = local_levels + level_idx
        scaled = (gates_ref[row : row + 1, :] * grad_t).astype(jnp.bfloat16)
        out_ref[0] = dot(scaled, query) * level_weight(row)


def local_kernel(
    local_levels, cross_levels, flags_ref, query_ref, key_ref, value_ref, grad_ref, gates_ref, states_ref,
    query_out, key_out, value_out, coef_out,
    query_t, key_t, grad_t, mix, levels, sums, weights, grad_weights,
):
    head = pl.program_id(0)
    last = pl.num_programs(0) - 1
    tokens = query_ref.shape[0]
    block = LANES
    wide = 2 * block
    base = block.bit_length() - 1

    query_t[...] = query_ref[...].T
    key_t[...] = key_ref[...].T
    grad_t[...] = grad_ref[...].T

    @pl.when(head == 0)
    def _():
        col = lax.broadcasted_iota(jnp.int32, (block, block), 0)
        row = lax.broadcasted_iota(jnp.int32, (block, block), 1)
        mixed = jnp.bitwise_xor(row, col)
        level = jnp.zeros((block, block), jnp.int32)
        for bit_pos in range(base):
            level = level + (jnp.right_shift(mixed, bit_pos) > 0).astype(jnp.int32)
        level = jnp.where(col <= row, level, -1)
        levels[...] = level
        for idx in range(tokens // block):
            tile = jnp.zeros((block, block), jnp.float32)
            for level_idx in range(base + 1):
                gate = gates_ref[level_idx : level_idx + 1, idx * block : (idx + 1) * block]
                tile = jnp.where(level == level_idx, gate * level_weight(level_idx), tile)
            mix[idx] = tile
        sums[...] = jnp.zeros_like(sums)
        coef_out[...] = jnp.zeros_like(coef_out)

    key_acc = [None] * (tokens // block)
    key_out[...] = jnp.zeros_like(key_out)
    value_out[...] = jnp.zeros_like(value_out)
    for t_start in range(0, tokens, wide):
        t_slice = slice(t_start, t_start + wide)
        q_cols = query_t[:, t_slice]
        g_cols = grad_t[:, t_slice]
        level_totals = {}
        for s_start in range(0, t_start, block):
            s_slice = slice(s_start, s_start + block)
            level = ((s_start ^ t_start) // block).bit_length() + base
            gate = gates_ref[level : level + 1, t_slice] * level_weight(level)
            score = dot(key_ref[s_slice, :], q_cols)
            grad_score = dot(value_ref[s_slice, :], g_cols)
            total = jnp.sum(score * grad_score, axis=0, keepdims=True)
            level_totals[level] = level_totals.get(level, 0.0) + total
            weights[s_slice, :] = (gate * score).astype(jnp.bfloat16)
            grad_weights[s_slice, :] = (gate * grad_score).astype(jnp.bfloat16)
        for level, total in level_totals.items():
            coef_out[level : level + 1, t_slice] += total * level_weight(level)
        idx = t_start // block
        level = base + 1
        high = slice(t_start + block, t_start + wide)
        low = slice(t_start, t_start + block)
        score = dot(key_ref[low, :], q_cols)
        grad_score = dot(value_ref[low, :], g_cols)
        product = score * grad_score
        gate = jnp.broadcast_to(gates_ref[level : level + 1, high] * level_weight(level), (block, block))
        tile = jnp.concatenate([mix[idx], gate], axis=1)
        weights[low, :] = (tile * score).astype(jnp.bfloat16)
        grad_weights[low, :] = (tile * grad_score).astype(jnp.bfloat16)
        sums[idx] += product[:, :block]
        coef_out[level : level + 1, high] += (
            jnp.sum(product[:, block:], axis=0, keepdims=True) * level_weight(level)
        )
        score = dot(key_ref[high, :], q_cols[:, block:])
        grad_score = dot(value_ref[high, :], g_cols[:, block:])
        tile = mix[idx + 1]
        zeros = jnp.zeros((block, block), jnp.bfloat16)
        weights[high, :block] = zeros
        grad_weights[high, :block] = zeros
        weights[high, block:] = (tile * score).astype(jnp.bfloat16)
        grad_weights[high, block:] = (tile * grad_score).astype(jnp.bfloat16)
        sums[idx + 1] += score * grad_score

        s_all = slice(0, t_start + wide)
        query_total = dot(key_t[:, s_all], grad_weights[s_all, :])
        for level_idx in range(cross_levels):
            row = local_levels + level_idx
            projected = dot(states_ref[0, level_idx, 0], g_cols)
            flag = flags_ref[level_idx]
            query_total += (gates_ref[row : row + 1, t_slice] * flag) * projected
            coef_out[row : row + 1, t_slice] += flag * jnp.sum(
                q_cols.astype(jnp.float32) * projected, axis=0, keepdims=True
            )
        query_out[t_slice, :] = query_total.astype(jnp.bfloat16).T
        key_out[s_all, :] += dot(grad_weights[s_all, :], query_ref[t_slice, :])
        value_out[s_all, :] += dot(weights[s_all, :], grad_ref[t_slice, :])

    @pl.when(head == last)
    def _():
        level = levels[...]
        for idx in range(tokens // block):
            product = sums[idx]
            for level_idx in range(base + 1):
                picked = jnp.sum(jnp.where(level == level_idx, product, 0.0), axis=0, keepdims=True)
                coef_out[level_idx : level_idx + 1, idx * block : (idx + 1) * block] = (
                    picked * level_weight(level_idx)
                )


def apply_kernel(key_ref, value_ref, key_local, value_local, state_ref, key_out, value_out):
    state = state_ref[0].astype(jnp.bfloat16)
    key_out[...] = (key_local[...] + dot(value_ref[...], state)).astype(jnp.bfloat16)
    value_out[...] = (value_local[...] + dot(key_ref[...], state.T)).astype(jnp.bfloat16)


def shards(queries, key_vectors, values, out_grad, level_coef, saved_states):
    tokens = queries.shape[0]
    cross_levels = saved_states.shape[1]
    head_count = saved_states.shape[2]
    key_width = saved_states.shape[3]
    value_width = saved_states.shape[4]
    level_count = level_coef.shape[0]
    local_levels = level_count - cross_levels
    shard_count = lax.axis_size("seq")
    bit_count = shard_count.bit_length() - 1
    shard_idx = lax.axis_index("seq")

    def head_block(width):
        return pl.BlockSpec((tokens, width), lambda h: (0, h))

    def whole(shape):
        return pl.BlockSpec(shape, lambda h: (0,) * len(shape))

    state_block = pl.BlockSpec((1, value_width, key_width), lambda h: (h, 0, 0))
    state_shape = jax.ShapeDtypeStruct((head_count, value_width, key_width), jnp.float32)
    contrib = pl.pallas_call(
        functools.partial(state_kernel, local_levels),
        grid=(head_count,),
        in_specs=[head_block(key_width), head_block(value_width), whole(level_coef.shape)],
        out_specs=[state_block] * bit_count,
        out_shape=[state_shape] * bit_count,
    )(queries, out_grad, level_coef)

    flags = jnp.bitwise_and(
        jnp.right_shift(shard_idx, jnp.arange(bit_count, dtype=jnp.int32)), 1
    ).astype(jnp.float32)
    block = LANES
    wide = 2 * block
    query_grad, key_local, value_local, coef_local = pl.pallas_call(
        functools.partial(local_kernel, local_levels, bit_count),
        grid=(head_count,),
        in_specs=[
            pl.BlockSpec(memory_space=pltpu.SMEM),
            head_block(key_width), head_block(key_width), head_block(value_width), head_block(value_width),
            whole(level_coef.shape),
            pl.BlockSpec((1, bit_count, 1, key_width, value_width), lambda h: (0, 0, h, 0, 0)),
        ],
        out_specs=[
            head_block(key_width), head_block(key_width), head_block(value_width),
            whole(level_coef.shape),
        ],
        out_shape=[
            jax.ShapeDtypeStruct(queries.shape, jnp.bfloat16),
            jax.ShapeDtypeStruct(queries.shape, jnp.float32),
            jax.ShapeDtypeStruct(values.shape, jnp.float32),
            jax.ShapeDtypeStruct(level_coef.shape, jnp.float32),
        ],
        scratch_shapes=[
            pltpu.VMEM((key_width, tokens), jnp.bfloat16),
            pltpu.VMEM((key_width, tokens), jnp.bfloat16),
            pltpu.VMEM((value_width, tokens), jnp.bfloat16),
            pltpu.VMEM((tokens // block, block, block), jnp.float32),
            pltpu.VMEM((block, block), jnp.int32),
            pltpu.VMEM((tokens // block, block, block), jnp.float32),
            pltpu.VMEM((tokens, wide), jnp.bfloat16),
            pltpu.VMEM((tokens, wide), jnp.bfloat16),
        ],
    )(flags, queries, key_vectors, values, out_grad, level_coef, saved_states)

    def send(value, mask, level_idx, both):
        pairs = [(p, p ^ mask) for p in range(shard_count) if (p >> level_idx) & 1]
        return lax.ppermute(value, "seq", pairs)

    grad_state = None
    for level_idx in reversed(range(bit_count)):
        partial_value = contrib[level_idx]
        for bit_pos in range(level_idx):
            partial_value = partial_value + send(partial_value, 2**bit_pos, level_idx, True)
        received = send(partial_value, 2**level_idx, level_idx, False)
        grad_state = received if grad_state is None else grad_state + received

    coef_grad = coef_local
    head_groups = lax.axis_size("head")
    for bit_pos in range(head_groups.bit_length() - 1):
        pairs = [(p, p ^ 2**bit_pos) for p in range(head_groups)]
        coef_grad = coef_grad + lax.ppermute(coef_grad, "head", pairs)

    key_grad, value_grad = pl.pallas_call(
        apply_kernel,
        grid=(head_count,),
        in_specs=[
            head_block(key_width), head_block(value_width), head_block(key_width), head_block(value_width),
            state_block,
        ],
        out_specs=[head_block(key_width), head_block(value_width)],
        out_shape=[
            jax.ShapeDtypeStruct(queries.shape, jnp.bfloat16),
            jax.ShapeDtypeStruct(values.shape, jnp.bfloat16),
        ],
    )(key_vectors, values, key_local, value_local, grad_state)
    return (query_grad, key_grad, value_grad, coef_grad)


def solution(mesh):
    in_specs = (
        P("seq", "head"),
        P("seq", "head"),
        P("seq", "head"),
        P("seq", "head"),
        P(None, "seq"),
        P("seq", None, "head", None, None),
    )
    out_specs = (P("seq", "head"), P("seq", "head"), P("seq", "head"), P(None, "seq"))
    return jax.shard_map(shards, mesh=mesh, in_specs=in_specs, out_specs=out_specs, check_vma=False)
```

time: 120 us -> 41.7 us (0.35)
  the two profiles are of different devices: /device:TPU:0 before, /device:TPU:12 now
where the time goes in v1:
time: 41.7 us; the launch traced here: 41.4 us
  Pallas kernels  13.8 us (33%)
  waiting for transfers between devices  12.5 us (30%)
  starting transfers between devices  11.5 us (28%)
  other arithmetic  2.84 us (7%)
  between operations  0.79 us (2%)
    ppermute x6, starting transfers between devices, send(): return lax.ppermute(value, 'seq', pairs)  9.9 us
    ppermute x6, waiting for transfers between devices, send(): return lax.ppermute(value, 'seq', pairs)  9.05 us
    pallas_call x1, Pallas kernels, shards(): pl.pallas_call(functools.partial(local_kernel, local_levels, bit_count),...  8.18 us
    ppermute x2, waiting for transfers between devices, shards(): coef_grad = coef_grad + lax.ppermute(coef_grad, 'head', pairs)  3.41 us
    pallas_call x1, Pallas kernels, shards(): pl.pallas_call(apply_kernel, grid=(head_count,), in_specs=[head_block(key...  2.93 us
    pallas_call x1, Pallas kernels, shards(): pl.pallas_call(functools.partial(state_kernel, local_levels), grid=(head_...  2.64 us
    ppermute x2, starting transfers between devices, shards(): coef_grad = coef_grad + lax.ppermute(coef_grad, 'head', pairs)  1.62 us
    add x3, other arithmetic, shards(): partial_value + send(partial_value, 2 ** bit_pos, level_idx, True)  0.96 us
  transfers between devices with their start and end apart: 8, of which 2 were waited for; matrix products, arithmetic and copies ran while one was open for 5% of the time, Pallas kernels for 20%

profile of v1, /device:TPU:12, one launch (start us, length us, event | category | flops | bytes accessed | tf_op | source)
XLA Modules:
  0.0 41.4 jit_solution(17624491289160257795)
XLA Ops:
  0.6 2.6 %shard_map.94 = (f32[2,128,128]{2,1,0:T(8,128)}, f32[2,128,128]{2,1,0:T(8,128)}, f32[2,128,128]{2,1,0:T(8,128)}) custom-call(bf16[1024,256]{1,0:T(8,128)(2,1)} %query_ref.3, bf16[1024,256]{1,0:T(8,128)(2,1)} %grad_ref.3, f32[17,1024]{1,0:T(8,128)} %gates_ref.3), custom_call_target="tpu_custom_call" | custom-call | tf_op jit(solution)/shard_map/pallas_call | solution.py:164
  3.3 0.7 %collective-permute-start = (f32[2,128,128]{2,1,0:T(8,128)}, f32[2,128,128]{2,1,0:T(8,128)S(1)}, u32[]{:S(2)}, u32[]{:S(2)}) collective-permute-start(f32[2,128,128]{2,1,0:T(8,128)} %get-tuple-element.16), channel_id=1, source_target_pairs={{16,20},{20,16},{24,28},{28,24},{17,21},{21,17},{25,29},{29,25},{1... | collective-permute-start | bytes 393224 | tf_op jit(solution)/shard_map/ppermute | solution.py:210
  3.9 2.4 %collective-permute-start.3 = (f32[2,128,128]{2,1,0:T(8,128)}, f32[2,128,128]{2,1,0:T(8,128)S(1)}, u32[]{:S(2)}, u32[]{:S(2)}) collective-permute-start(f32[2,128,128]{2,1,0:T(8,128)} %get-tuple-element.17), channel_id=1, source_target_pairs={{8,12},{12,8},{24,28},{28,24},{9,13},{13,9},{25,29},{29,25},{10,14... | collective-permute-start | bytes 393224 | tf_op jit(solution)/shard_map/ppermute | solution.py:210
  6.4 0.0 collective-permute-done
  6.4 0.9 %add.21 = f32[2,128,128]{2,1,0:T(8,128)S(1)} add(f32[2,128,128]{2,1,0:T(8,128)} %get-tuple-element.16, f32[2,128,128]{2,1,0:T(8,128)S(1)} %collective-permute-done) | non-fusion elementwise | flops 32768 | bytes 393216 | tf_op jit(solution)/shard_map/add | solution.py:216
  7.3 0.7 %collective-permute-start.1 = (f32[2,128,128]{2,1,0:T(8,128)S(1)}, f32[2,128,128]{2,1,0:T(8,128)S(1)}, u32[]{:S(2)}, u32[]{:S(2)}) collective-permute-start(f32[2,128,128]{2,1,0:T(8,128)S(1)} %add.21), channel_id=1, source_target_pairs={{16,24},{20,28},{24,16},{28,20},{17,25},{21,29},{25,17},{29,21},{1... | collective-permute-start | bytes 393224 | tf_op jit(solution)/shard_map/ppermute | solution.py:210
  8.0 0.5 %and_convert_fusion.flags_ref = f32[3]{0:T(128)} fusion(s32[]{:T(128)S(6)} %axis_index.15), kind=kLoop, calls=%fused_computation.1 | loop fusion | flops 9 | bytes 16 | tf_op jit(solution)/shard_map/convert_element_type | solution.py:174
  8.5 0.0 copy-start.2
  8.5 0.0 copy-start
  8.5 8.2 %shard_map.93 = (bf16[1024,256]{1,0:T(8,128)(2,1)}, f32[1024,256]{1,0:T(8,128)}, f32[1024,256]{1,0:T(8,128)}, f32[17,1024]{1,0:T(8,128)}) custom-call(f32[3]{0:T(128)} %and_convert_fusion.flags_ref, bf16[1024,256]{1,0:T(8,128)(2,1)} %query_ref.3, bf16[1024,256]{1,0:T(8,128)(2,1)} %key_ref.3, bf16[1024,256]{1,0:T(8,128)(2,1)} %value_ref.3, ...), custom_call_target="tpu_custom_call" | custom-call | tf_op jit(solution)/shard_map/pallas_call | solution.py:177
  16.7 0.1 collective-permute-start.6
  16.8 0.0 copy-done.2
  16.8 3.4 %collective-permute-start.5 = (f32[2,128,128]{2,1,0:T(8,128)S(1)}, f32[2,128,128]{2,1,0:T(8,128)S(1)}, u32[]{:S(2)}, u32[]{:S(2)}) collective-permute-start(f32[2,128,128]{2,1,0:T(8,128)S(1)} %copy-done.2), channel_id=1, source_target_pairs={{4,0},{12,8},{20,16},{28,24},{5,1},{13,9},{21,17},{29,25},{6,2},{1... | collective-permute-start | bytes 393224 | tf_op jit(solution)/shard_map/ppermute | solution.py:210
  20.2 0.0 collective-permute-done.3
  20.3 0.0 copy-done
  20.3 0.0 copy-start.1
  20.3 1.4 %collective-permute-start.4 = (f32[2,128,128]{2,1,0:T(8,128)S(1)}, f32[2,128,128]{2,1,0:T(8,128)S(1)}, u32[]{:S(2)}, u32[]{:S(2)}) collective-permute-start(f32[2,128,128]{2,1,0:T(8,128)S(1)} %add.23), channel_id=1, source_target_pairs={{8,0},{12,4},{24,16},{28,20},{9,1},{13,5},{25,17},{29,21},{10,2},{... | collective-permute-start | bytes 393224 | tf_op jit(solution)/shard_map/ppermute | solution.py:210
  21.7 0.0 collective-permute-done.1
  21.8 1.3 %collective-permute-start.2 = (f32[2,128,128]{2,1,0:T(8,128)S(1)}, f32[2,128,128]{2,1,0:T(8,128)S(1)}, u32[]{:S(2)}, u32[]{:S(2)}) collective-permute-start(f32[2,128,128]{2,1,0:T(8,128)S(1)} %add.22), channel_id=1, source_target_pairs={{16,0},{20,4},{24,8},{28,12},{17,1},{21,5},{25,9},{29,13},{18,2},{... | collective-permute-start | bytes 393224 | tf_op jit(solution)/shard_map/ppermute | solution.py:210
  23.1 0.0 collective-permute-done.6
  23.1 0.0 copy-done.1
  23.1 1.6 %collective-permute-start.7 = (f32[17,1024]{1,0:T(8,128)S(1)}, f32[17,1024]{1,0:T(8,128)S(1)}, u32[]{:S(2)}, u32[]{:S(2)}) collective-permute-start(f32[17,1024]{1,0:T(8,128)S(1)} %add.26), channel_id=1, source_target_pairs={{0,2},{1,3},{2,0},{3,1},{4,6},{5,7},{6,4},{7,5},{8,10},{9,11},{10,... | collective-permute-start | bytes 208904 | tf_op jit(solution)/shard_map/ppermute | solution.py:224
  24.7 3.4 %collective-permute-done.7 = f32[17,1024]{1,0:T(8,128)S(1)} collective-permute-done((f32[17,1024]{1,0:T(8,128)S(1)}, f32[17,1024]{1,0:T(8,128)S(1)}, u32[]{:S(2)}, u32[]{:S(2)}) %collective-permute-start.7) | collective-permute-done | bytes 69664 | tf_op jit(solution)/shard_map/ppermute | solution.py:224
  28.1 0.7 %add.27 = f32[17,1024]{1,0:T(8,128)} add(f32[17,1024]{1,0:T(8,128)S(1)} %add.26, f32[17,1024]{1,0:T(8,128)S(1)} %collective-permute-done.7) | non-fusion elementwise | flops 17408 | bytes 208896 | tf_op jit(solution)/shard_map/add | solution.py:224
  28.7 0.0 collective-permute-done.5
  28.7 0.0 collective-permute-done.4
  28.7 9.0 %collective-permute-done.2 = f32[2,128,128]{2,1,0:T(8,128)S(1)} collective-permute-done((f32[2,128,128]{2,1,0:T(8,128)S(1)}, f32[2,128,128]{2,1,0:T(8,128)S(1)}, u32[]{:S(2)}, u32[]{:S(2)}) %collective-permute-start.2) | collective-permute-done | bytes 131104 | tf_op jit(solution)/shard_map/ppermute | solution.py:210
  37.8 0.7 %add_add_fusion.state_ref = f32[2,128,128]{2,1,0:T(8,128)} fusion(f32[2,128,128]{2,1,0:T(8,128)S(1)} %collective-permute-done.5, f32[2,128,128]{2,1,0:T(8,128)S(1)} %collective-permute-done.2, f32[2,128,128]{2,1,0:T(8,128)S(1)} %collective-permute-done.4), kind=kLoop, calls=%fused_computation | loop fusion | flops 65536 | bytes 524288 | tf_op jit(solution)/shard_map/add | solution.py:218
  38.4 2.9 %shard_map.95 = (bf16[1024,256]{1,0:T(8,128)(2,1)}, bf16[1024,256]{1,0:T(8,128)(2,1)}) custom-call(bf16[1024,256]{1,0:T(8,128)(2,1)} %key_ref.3, bf16[1024,256]{1,0:T(8,128)(2,1)} %value_ref.3, f32[1024,256]{1,0:T(8,128)} %get-tuple-element.14.key_local, f32[1024,256]{1,0:T(8,128)} %get-tuple-element.15.value_local, f32[2,128,128]{2,1,0:T(8,128)} %add_add_fusion.state_ref), custom_call_target="tpu_custom_call" | custom-call | tf_op jit(solution)/shard_map/pallas_call | solution.py:226
  (3 shorter events, 0.0 us)
Async XLA Ops:
  3.3 3.1 %collective-permute-start = (f32[2,128,128]{2,1,0:T(8,128)}, f32[2,128,128]{2,1,0:T(8,128)S(1)}, u32[]{:S(2)}, u32[]{:S(2)}) collective-permute-start(f32[2,128,128]{2,1,0:T(8,128)} %get-tuple-element.16), channel_id=1, source_target_pairs={{16,20},{20,16},{24,28},{28,24},{17,21},{21,17},{25,29},{29,25},{1... | collective-permute-start | bytes 393224 | tf_op jit(solution)/shard_map/ppermute | solution.py:210
  3.9 16.3 %collective-permute-start.3 = (f32[2,128,128]{2,1,0:T(8,128)}, f32[2,128,128]{2,1,0:T(8,128)S(1)}, u32[]{:S(2)}, u32[]{:S(2)}) collective-permute-start(f32[2,128,128]{2,1,0:T(8,128)} %get-tuple-element.17), channel_id=1, source_target_pairs={{8,12},{12,8},{24,28},{28,24},{9,13},{13,9},{25,29},{29,25},{10,14... | collective-permute-start | bytes 393224 | tf_op jit(solution)/shard_map/ppermute | solution.py:210
  7.3 14.4 %collective-permute-start.1 = (f32[2,128,128]{2,1,0:T(8,128)S(1)}, f32[2,128,128]{2,1,0:T(8,128)S(1)}, u32[]{:S(2)}, u32[]{:S(2)}) collective-permute-start(f32[2,128,128]{2,1,0:T(8,128)S(1)} %add.21), channel_id=1, source_target_pairs={{16,24},{20,28},{24,16},{28,20},{17,25},{21,29},{25,17},{29,21},{1... | collective-permute-start | bytes 393224 | tf_op jit(solution)/shard_map/ppermute | solution.py:210
  8.5 8.3 %copy-start.2 = (f32[2,128,128]{2,1,0:T(8,128)S(1)}, f32[2,128,128]{2,1,0:T(8,128)}, u32[]{:S(2)}) copy-start(f32[2,128,128]{2,1,0:T(8,128)} %get-tuple-element.18) | copy-start | bytes 393220
  8.5 11.7 %copy-start = (f32[2,128,128]{2,1,0:T(8,128)S(1)}, f32[2,128,128]{2,1,0:T(8,128)}, u32[]{:S(2)}) copy-start(f32[2,128,128]{2,1,0:T(8,128)} %get-tuple-element.17) | copy-start | bytes 393220
  16.7 6.4 %collective-permute-start.6 = (f32[17,1024]{1,0:T(8,128)}, f32[17,1024]{1,0:T(8,128)S(1)}, u32[]{:S(2)}, u32[]{:S(2)}) collective-permute-start(f32[17,1024]{1,0:T(8,128)} %get-tuple-element.21), channel_id=1, source_target_pairs={{0,1},{1,0},{2,3},{3,2},{4,5},{5,4},{6,7},{7,6},{8,9},{9,8},{10,11... | collective-permute-start | bytes 208904 | tf_op jit(solution)/shard_map/ppermute | solution.py:224
  16.8 11.9 %collective-permute-start.5 = (f32[2,128,128]{2,1,0:T(8,128)S(1)}, f32[2,128,128]{2,1,0:T(8,128)S(1)}, u32[]{:S(2)}, u32[]{:S(2)}) collective-permute-start(f32[2,128,128]{2,1,0:T(8,128)S(1)} %copy-done.2), channel_id=1, source_target_pairs={{4,0},{12,8},{20,16},{28,24},{5,1},{13,9},{21,17},{29,25},{6,2},{1... | collective-permute-start | bytes 393224 | tf_op jit(solution)/shard_map/ppermute | solution.py:210
  20.3 2.8 %copy-start.1 = (f32[17,1024]{1,0:T(8,128)S(1)}, f32[17,1024]{1,0:T(8,128)}, u32[]{:S(2)}) copy-start(f32[17,1024]{1,0:T(8,128)} %get-tuple-element.21) | copy-start | bytes 208900
  20.3 8.4 %collective-permute-start.4 = (f32[2,128,128]{2,1,0:T(8,128)S(1)}, f32[2,128,128]{2,1,0:T(8,128)S(1)}, u32[]{:S(2)}, u32[]{:S(2)}) collective-permute-start(f32[2,128,128]{2,1,0:T(8,128)S(1)} %add.23), channel_id=1, source_target_pairs={{8,0},{12,4},{24,16},{28,20},{9,1},{13,5},{25,17},{29,21},{10,2},{... | collective-permute-start | bytes 393224 | tf_op jit(solution)/shard_map/ppermute | solution.py:210
  21.8 16.0 %collective-permute-start.2 = (f32[2,128,128]{2,1,0:T(8,128)S(1)}, f32[2,128,128]{2,1,0:T(8,128)S(1)}, u32[]{:S(2)}, u32[]{:S(2)}) collective-permute-start(f32[2,128,128]{2,1,0:T(8,128)S(1)} %add.22), channel_id=1, source_target_pairs={{16,0},{20,4},{24,8},{28,12},{17,1},{21,5},{25,9},{29,13},{18,2},{... | collective-permute-start | bytes 393224 | tf_op jit(solution)/shard_map/ppermute | solution.py:210
  23.1 5.0 %collective-permute-start.7 = (f32[17,1024]{1,0:T(8,128)S(1)}, f32[17,1024]{1,0:T(8,128)S(1)}, u32[]{:S(2)}, u32[]{:S(2)}) collective-permute-start(f32[17,1024]{1,0:T(8,128)S(1)} %add.26), channel_id=1, source_target_pairs={{0,2},{1,3},{2,0},{3,1},{4,6},{5,7},{6,4},{7,5},{8,10},{9,11},{10,... | collective-permute-start | bytes 208904 | tf_op jit(solution)/shard_map/ppermute | solution.py:224

commit v2 on v1

--- a/solution.py
+++ b/solution.py
@@ -20,20 +20,24 @@
     return jnp.dot(lhs, rhs, preferred_element_type=jnp.float32)
 
 
-def state_kernel(local_levels, query_ref, grad_ref, gates_ref, *out_refs):
-    grad_t = grad_ref[...].T.astype(jnp.float32)
-    query = query_ref[...]
-    for level_idx, out_ref in enumerate(out_refs):
-        row = local_levels + level_idx
-        scaled = (gates_ref[row : row + 1, :] * grad_t).astype(jnp.bfloat16)
-        out_ref[0] = dot(scaled, query) * level_weight(row)
+def state_gradient(row, flag, query_ref, grad_t, gates_ref):
+    scaled = (gates_ref[row : row + 1, :] * grad_t.astype(jnp.float32)).astype(jnp.bfloat16)
+    return dot(scaled, query_ref[...]) * (level_weight(row) * flag)
+
+
+def top_kernel(row, flags_ref, query_ref, grad_ref, gates_ref, out_ref):
+    flag = flags_ref[flags_ref.shape[0] - 1]
+    out_ref[0] = state_gradient(row, flag, query_ref, grad_ref[...].T, gates_ref)
 
 
 def local_kernel(
     local_levels, cross_levels, flags_ref, query_ref, key_ref, value_ref, grad_ref, gates_ref, states_ref,
-    query_out, key_out, value_out, coef_out,
+    query_out, key_out, value_out, coef_out, *rest,
+):
+    state_outs = rest[: cross_levels - 1]
+    (
     query_t, key_t, grad_t, mix, levels, sums, weights, grad_weights,
-):
+    ) = rest[cross_levels - 1 :]
     head = pl.program_id(0)
     last = pl.num_programs(0) - 1
     tokens = query_ref.shape[0]
@@ -64,7 +68,10 @@
         sums[...] = jnp.zeros_like(sums)
         coef_out[...] = jnp.zeros_like(coef_out)
 
-    key_acc = [None] * (tokens // block)
+    for level_idx, out_ref in enumerate(state_outs):
+        out_ref[0] = state_gradient(
+            local_levels + level_idx, flags_ref[level_idx], query_ref, grad_t[...], gates_ref
+        )
     key_out[...] = jnp.zeros_like(key_out)
     value_out[...] = jnp.zeros_like(value_out)
     for t_start in range(0, tokens, wide):
@@ -161,20 +168,28 @@
 
     state_block = pl.BlockSpec((1, value_width, key_width), lambda h: (h, 0, 0))
     state_shape = jax.ShapeDtypeStruct((head_count, value_width, key_width), jnp.float32)
-    contrib = pl.pallas_call(
-        functools.partial(state_kernel, local_levels),
-        grid=(head_count,),
-        in_specs=[head_block(key_width), head_block(value_width), whole(level_coef.shape)],
-        out_specs=[state_block] * bit_count,
-        out_shape=[state_shape] * bit_count,
-    )(queries, out_grad, level_coef)
-
     flags = jnp.bitwise_and(
         jnp.right_shift(shard_idx, jnp.arange(bit_count, dtype=jnp.int32)), 1
     ).astype(jnp.float32)
+    top = pl.pallas_call(
+        functools.partial(top_kernel, local_levels + bit_count - 1),
+        grid=(head_count,),
+        in_specs=[
+            pl.BlockSpec(memory_space=pltpu.SMEM),
+            head_block(key_width), head_block(value_width), whole(level_coef.shape),
+        ],
+        out_specs=state_block,
+        out_shape=state_shape,
+    )(flags, queries, out_grad, level_coef)
+
+    def exchange(value, bit_pos):
+        pairs = [(p, p ^ 2**bit_pos) for p in range(shard_count)]
+        return lax.ppermute(value, "seq", pairs)
+
+    grad_state = exchange(top, bit_count - 1)
     block = LANES
     wide = 2 * block
-    query_grad, key_local, value_local, coef_local = pl.pallas_call(
+    query_grad, key_local, value_local, coef_local, *contrib = pl.pallas_call(
         functools.partial(local_kernel, local_levels, bit_count),
         grid=(head_count,),
         in_specs=[
@@ -186,13 +201,15 @@
         out_specs=[
             head_block(key_width), head_block(key_width), head_block(value_width),
             whole(level_coef.shape),
-        ],
+        ]
+        + [state_block] * (bit_count - 1),
         out_shape=[
             jax.ShapeDtypeStruct(queries.shape, jnp.bfloat16),
             jax.ShapeDtypeStruct(queries.shape, jnp.float32),
             jax.ShapeDtypeStruct(values.shape, jnp.float32),
             jax.ShapeDtypeStruct(level_coef.shape, jnp.float32),
-        ],
+        ]
+        + [state_shape] * (bit_count - 1),
         scratch_shapes=[
             pltpu.VMEM((key_width, tokens), jnp.bfloat16),
             pltpu.VMEM((key_width, tokens), jnp.bfloat16),
@@ -205,17 +222,8 @@
         ],
     )(flags, queries, key_vectors, values, out_grad, level_coef, saved_states)
 
-    def send(value, mask, level_idx, both):
-        pairs = [(p, p ^ mask) for p in range(shard_count) if (p >> level_idx) & 1]
-        return lax.ppermute(value, "seq", pairs)
-
-    grad_state = None
-    for level_idx in reversed(range(bit_count)):
-        partial_value = contrib[level_idx]
-        for bit_pos in range(level_idx):
-            partial_value = partial_value + send(partial_value, 2**bit_pos, level_idx, True)
-        received = send(partial_value, 2**level_idx, level_idx, False)
-        grad_state = received if grad_state is None else grad_state + received
+    for level_idx in reversed(range(bit_count - 1)):
+        grad_state = grad_state + exchange(grad_state + contrib[level_idx], level_idx)
 
     coef_grad = coef_local
     head_groups = lax.axis_size("head")

time: 41.7 us -> 32.8 us (0.79)
  the two profiles are of different devices: /device:TPU:12 before, /device:TPU:0 now
where the time goes in v2:
time: 32.8 us; the launch traced here: 32.6 us
  Pallas kernels  13.6 us (41%)
  starting transfers between devices  8.85 us (27%)
  waiting for transfers between devices  6.52 us (20%)
  other arithmetic  2.92 us (9%)
  between operations  0.68 us (2%)
    pallas_call x1, Pallas kernels, shards(): pl.pallas_call(functools.partial(local_kernel, local_levels, bit_count),...  8.43 us
    ppermute x3, starting transfers between devices, exchange(): return lax.ppermute(value, 'seq', pairs)  7.29 us
    ppermute x3, waiting for transfers between devices, exchange(): return lax.ppermute(value, 'seq', pairs)  3.39 us
    ppermute x2, waiting for transfers between devices, shards(): coef_grad = coef_grad + lax.ppermute(coef_grad, 'head', pairs)  3.13 us
    pallas_call x1, Pallas kernels, shards(): pl.pallas_call(apply_kernel, grid=(head_count,), in_specs=[head_block(key...  2.93 us
    pallas_call x1, Pallas kernels, shards(): pl.pallas_call(functools.partial(top_kernel, local_levels + bit_count - 1...  2.27 us
    ppermute x2, starting transfers between devices, shards(): coef_grad = coef_grad + lax.ppermute(coef_grad, 'head', pairs)  1.56 us
    add x2, other arithmetic, shards(): grad_state + contrib[level_idx]  0.99 us
  transfers between devices with their start and end apart: 5, of which 2 were waited for; matrix products, arithmetic and copies ran while one was open for 2% of the time, Pallas kernels for 26%

profile of v2, /device:TPU:0, one launch (start us, length us, event | category | flops | bytes accessed | tf_op | source)
XLA Modules:
  0.0 32.6 jit_solution(3317078246471125899)
XLA Ops:
  0.6 0.6 %and_convert_fusion.flags_ref = f32[3]{0:T(128)} fusion(s32[]{:T(128)S(6)} %axis_index.15), kind=kLoop, calls=%fused_computation | loop fusion | flops 9 | bytes 16 | tf_op jit(solution)/shard_map/convert_element_type | solution.py:173
  1.2 2.3 %shard_map.94 = f32[2,128,128]{2,1,0:T(8,128)} custom-call(f32[3]{0:T(128)} %and_convert_fusion.flags_ref, bf16[1024,256]{1,0:T(8,128)(2,1)} %query_ref.3, bf16[1024,256]{1,0:T(8,128)(2,1)} %grad_ref.3, f32[17,1024]{1,0:T(8,128)} %gates_ref.3), custom_call_target="tpu_custom_call" | custom-call | tf_op jit(solution)/shard_map/pallas_call | solution.py:174
  3.5 4.1 %collective-permute-start = (f32[2,128,128]{2,1,0:T(8,128)}, f32[2,128,128]{2,1,0:T(8,128)S(1)}, u32[]{:S(2)}, u32[]{:S(2)}) collective-permute-start(f32[2,128,128]{2,1,0:T(8,128)} %shard_map.94), channel_id=1, source_target_pairs={{0,16},{4,20},{8,24},{12,28},{16,0},{20,4},{24,8},{28,12},{1,17},{... | collective-permute-start | bytes 393224 | tf_op jit(solution)/shard_map/ppermute | solution.py:187
  7.6 8.4 %shard_map.93 = (bf16[1024,256]{1,0:T(8,128)(2,1)}, f32[1024,256]{1,0:T(8,128)}, f32[1024,256]{1,0:T(8,128)}, f32[17,1024]{1,0:T(8,128)}, f32[2,128,128]{2,1,0:T(8,128)}, /*index=5*/f32[2,128,128]{2,1,0:T(8,128)}) custom-call(f32[3]{0:T(128)} %and_convert_fusion.flags_ref, bf16[1024,256]{1,0:T(8,128)(2,1)} %query_ref.3, bf16[1024,256]{1,0:T(8,128)(2,1)} %key_ref.3, ...), custom_call_target="tpu_custom_call" | custom-call | tf_op jit(solution)/shard_map/pallas_call | solution.py:192
  16.0 0.0 collective-permute-done
  16.0 0.0 copy-start.1
  16.0 0.0 copy-start
  16.0 1.0 %add.18 = f32[2,128,128]{2,1,0:T(8,128)S(1)} add(f32[2,128,128]{2,1,0:T(8,128)S(1)} %collective-permute-done, f32[2,128,128]{2,1,0:T(8,128)} %get-tuple-element.15) | non-fusion elementwise | flops 32768 | bytes 393216 | tf_op jit(solution)/shard_map/add | solution.py:226
  17.0 1.6 %collective-permute-start.1 = (f32[2,128,128]{2,1,0:T(8,128)S(1)}, f32[2,128,128]{2,1,0:T(8,128)S(1)}, u32[]{:S(2)}, u32[]{:S(2)}) collective-permute-start(f32[2,128,128]{2,1,0:T(8,128)S(1)} %add.18), channel_id=1, source_target_pairs={{0,8},{4,12},{8,0},{12,4},{16,24},{20,28},{24,16},{28,20},{1,9},{5... | collective-permute-start | bytes 393224 | tf_op jit(solution)/shard_map/ppermute | solution.py:187
  18.6 0.0 copy-done.1
  18.6 0.0 collective-permute-start.3
  18.6 3.4 %collective-permute-done.1 = f32[2,128,128]{2,1,0:T(8,128)S(1)} collective-permute-done((f32[2,128,128]{2,1,0:T(8,128)S(1)}, f32[2,128,128]{2,1,0:T(8,128)S(1)}, u32[]{:S(2)}, u32[]{:S(2)}) %collective-permute-start.1) | collective-permute-done | bytes 131104 | tf_op jit(solution)/shard_map/ppermute | solution.py:187
  22.0 0.0 copy-done
  22.1 1.6 %collective-permute-start.2 = (f32[2,128,128]{2,1,0:T(8,128)S(1)}, f32[2,128,128]{2,1,0:T(8,128)S(1)}, u32[]{:S(2)}, u32[]{:S(2)}) collective-permute-start(f32[2,128,128]{2,1,0:T(8,128)S(1)} %get-tuple-element.20), channel_id=1, source_target_pairs={{0,4},{4,0},{8,12},{12,8},{16,20},{20,16},{24,28},{28,24},{1,5},{5... | collective-permute-start | bytes 393224 | tf_op jit(solution)/shard_map/ppermute | solution.py:187
  23.7 0.0 collective-permute-done.3
  23.7 1.6 %collective-permute-start.4 = (f32[17,1024]{1,0:T(8,128)S(1)}, f32[17,1024]{1,0:T(8,128)S(1)}, u32[]{:S(2)}, u32[]{:S(2)}) collective-permute-start(f32[17,1024]{1,0:T(8,128)S(1)} %add.22), channel_id=1, source_target_pairs={{0,2},{1,3},{2,0},{3,1},{4,6},{5,7},{6,4},{7,5},{8,10},{9,11},{10,... | collective-permute-start | bytes 208904 | tf_op jit(solution)/shard_map/ppermute | solution.py:232
  25.2 3.1 %collective-permute-done.4 = f32[17,1024]{1,0:T(8,128)S(1)} collective-permute-done((f32[17,1024]{1,0:T(8,128)S(1)}, f32[17,1024]{1,0:T(8,128)S(1)}, u32[]{:S(2)}, u32[]{:S(2)}) %collective-permute-start.4) | collective-permute-done | bytes 69664 | tf_op jit(solution)/shard_map/ppermute | solution.py:232
  28.4 0.7 %add.23 = f32[17,1024]{1,0:T(8,128)} add(f32[17,1024]{1,0:T(8,128)S(1)} %add.22, f32[17,1024]{1,0:T(8,128)S(1)} %collective-permute-done.4) | non-fusion elementwise | flops 17408 | bytes 208896 | tf_op jit(solution)/shard_map/add | solution.py:232
  29.0 0.0 collective-permute-done.2
  29.0 0.7 %add.21.state_ref = f32[2,128,128]{2,1,0:T(8,128)} add(f32[2,128,128]{2,1,0:T(8,128)S(1)} %get-tuple-element.21, f32[2,128,128]{2,1,0:T(8,128)S(1)} %collective-permute-done.2) | non-fusion elementwise | flops 32768 | bytes 393216 | tf_op jit(solution)/shard_map/add | solution.py:226
  29.7 2.9 %shard_map.95 = (bf16[1024,256]{1,0:T(8,128)(2,1)}, bf16[1024,256]{1,0:T(8,128)(2,1)}) custom-call(bf16[1024,256]{1,0:T(8,128)(2,1)} %key_ref.3, bf16[1024,256]{1,0:T(8,128)(2,1)} %value_ref.3, f32[1024,256]{1,0:T(8,128)} %get-tuple-element.13.key_local, f32[1024,256]{1,0:T(8,128)} %get-tuple-element.14.value_local, f32[2,128,128]{2,1,0:T(8,128)} %add.21.state_ref), custom_call_target="tpu_custom_call" | custom-call | tf_op jit(solution)/shard_map/pallas_call | solution.py:234
  (2 shorter events, 0.0 us)
Async XLA Ops:
  3.5 12.5 %collective-permute-start = (f32[2,128,128]{2,1,0:T(8,128)}, f32[2,128,128]{2,1,0:T(8,128)S(1)}, u32[]{:S(2)}, u32[]{:S(2)}) collective-permute-start(f32[2,128,128]{2,1,0:T(8,128)} %shard_map.94), channel_id=1, source_target_pairs={{0,16},{4,20},{8,24},{12,28},{16,0},{20,4},{24,8},{28,12},{1,17},{... | collective-permute-start | bytes 393224 | tf_op jit(solution)/shard_map/ppermute | solution.py:187
  16.0 2.6 %copy-start.1 = (f32[17,1024]{1,0:T(8,128)S(1)}, f32[17,1024]{1,0:T(8,128)}, u32[]{:S(2)}) copy-start(f32[17,1024]{1,0:T(8,128)} %get-tuple-element.19) | copy-start | bytes 208900
  16.0 6.0 %copy-start = (f32[2,128,128]{2,1,0:T(8,128)S(1)}, f32[2,128,128]{2,1,0:T(8,128)}, u32[]{:S(2)}) copy-start(f32[2,128,128]{2,1,0:T(8,128)} %get-tuple-element.16) | copy-start | bytes 393220
  17.0 5.0 %collective-permute-start.1 = (f32[2,128,128]{2,1,0:T(8,128)S(1)}, f32[2,128,128]{2,1,0:T(8,128)S(1)}, u32[]{:S(2)}, u32[]{:S(2)}) collective-permute-start(f32[2,128,128]{2,1,0:T(8,128)S(1)} %add.18), channel_id=1, source_target_pairs={{0,8},{4,12},{8,0},{12,4},{16,24},{20,28},{24,16},{28,20},{1,9},{5... | collective-permute-start | bytes 393224 | tf_op jit(solution)/shard_map/ppermute | solution.py:187
  18.6 5.0 %collective-permute-start.3 = (f32[17,1024]{1,0:T(8,128)S(1)}, f32[17,1024]{1,0:T(8,128)S(1)}, u32[]{:S(2)}, u32[]{:S(2)}) collective-permute-start(f32[17,1024]{1,0:T(8,128)S(1)} %copy-done.1), channel_id=1, source_target_pairs={{0,1},{1,0},{2,3},{3,2},{4,5},{5,4},{6,7},{7,6},{8,9},{9,8},{10,11... | collective-permute-start | bytes 208904 | tf_op jit(solution)/shard_map/ppermute | solution.py:232
  22.1 6.9 %collective-permute-start.2 = (f32[2,128,128]{2,1,0:T(8,128)S(1)}, f32[2,128,128]{2,1,0:T(8,128)S(1)}, u32[]{:S(2)}, u32[]{:S(2)}) collective-permute-start(f32[2,128,128]{2,1,0:T(8,128)S(1)} %get-tuple-element.20), channel_id=1, source_target_pairs={{0,4},{4,0},{8,12},{12,8},{16,20},{20,16},{24,28},{28,24},{1,5},{5... | collective-permute-start | bytes 393224 | tf_op jit(solution)/shard_map/ppermute | solution.py:187
  23.7 4.7 %collective-permute-start.4 = (f32[17,1024]{1,0:T(8,128)S(1)}, f32[17,1024]{1,0:T(8,128)S(1)}, u32[]{:S(2)}, u32[]{:S(2)}) collective-permute-start(f32[17,1024]{1,0:T(8,128)S(1)} %add.22), channel_id=1, source_target_pairs={{0,2},{1,3},{2,0},{3,1},{4,6},{5,7},{6,4},{7,5},{8,10},{9,11},{10,... | collective-permute-start | bytes 208904 | tf_op jit(solution)/shard_map/ppermute | solution.py:232

commit v3 on v0

v3 whole, which is shorter than its diff:
```python
import functools

import jax
import jax.numpy as jnp
from jax import lax
from jax.experimental import pallas as pl
from jax.experimental.pallas import tpu as pltpu
from jax.sharding import PartitionSpec as P

LANES = 128
SUBLANES = 8
MIB = 2**20


def level_weight(level_idx):
    if level_idx == 0:
        return 1.0
    return 2.0 ** (-(level_idx - 1) / 2.0)


def dot(lhs, rhs):
    return jnp.dot(lhs, rhs, preferred_element_type=jnp.float32)


def shard_bit(level_idx):
    return jnp.bitwise_and(jnp.right_shift(lax.axis_index("seq"), level_idx), 1).astype(jnp.float32)


def state_gradients(rows, query, grad_t, gates_ref):
    grad_t = grad_t.astype(jnp.float32)
    scaled = [(gates_ref[row : row + 1, :] * grad_t).astype(jnp.bfloat16) for row in rows]
    return dot(jnp.concatenate(scaled, axis=0), query)


def top_kernel(head_count, level_idx, row, *refs):
    query_hbm, key_hbm, value_hbm, grad_hbm, gates_hbm, states_hbm = refs[:6]
    query, key, value, grad, gates, states, out_ref, sems = refs[6:]
    key_width = query.shape[1] // head_count
    value_width = grad.shape[1] // head_count
    first = [pltpu.make_async_copy(gates_hbm, gates, sems.at[0])]
    for head in range(head_count):
        for source, target, width in ((grad_hbm, grad, value_width), (query_hbm, query, key_width)):
            cols = slice(head * width, (head + 1) * width)
            first.append(pltpu.make_async_copy(source.at[:, cols], target.at[:, cols], sems.at[len(first)]))
    later = []
    for source, target in ((key_hbm, key), (value_hbm, value), (states_hbm, states)):
        later.append(pltpu.make_async_copy(source, target, sems.at[len(first) + len(later)]))
    for copy in first + later:
        copy.start()
    first[0].wait()
    scale = shard_bit(level_idx) * level_weight(row)
    for head in range(head_count):
        first[2 * head + 1].wait()
        grad_t = grad[:, head * value_width : (head + 1) * value_width].T
        first[2 * head + 2].wait()
        keys = slice(head * key_width, (head + 1) * key_width)
        out_ref[head] = state_gradients([row], query[:, keys], grad_t, gates) * scale
    for copy in later:
        copy.wait()


def within_block(block):
    col = lax.broadcasted_iota(jnp.int32, (SUBLANES, block), 0)
    row = jnp.bitwise_and(lax.broadcasted_iota(jnp.int32, (SUBLANES, block), 1), SUBLANES - 1)
    mixed = jnp.bitwise_xor(row, col)
    level = jnp.zeros((SUBLANES, block), jnp.int32)
    for bit_pos in range(SUBLANES.bit_length() - 1):
        level = level + (jnp.right_shift(mixed, bit_pos) > 0).astype(jnp.int32)
    return jnp.where(col <= row, level, -1)


def local_kernel(
    local_levels, cross_levels, head_count,
    query_ref, key_ref, value_ref, grad_ref, gates_ref, states_ref,
    query_out, key_out, value_out, coef_out, *rest,
):
    state_outs = rest[: cross_levels - 1]
    key_t, grad_t, mix, sums, weights, grad_weights = rest[cross_levels - 1 :]
    tokens = query_ref.shape[0]
    key_width = query_ref.shape[1] // head_count
    value_width = value_ref.shape[1] // head_count
    block = LANES
    wide = 2 * block
    base = block.bit_length() - 1
    inner = SUBLANES.bit_length() - 1
    groups = block // SUBLANES

    level_in = within_block(block)
    lane_group = jnp.right_shift(lax.broadcasted_iota(jnp.int32, (SUBLANES, block), 1), inner)
    row_group = jnp.right_shift(lax.broadcasted_iota(jnp.int32, (groups, block), 1), inner)
    col_group = lax.broadcasted_iota(jnp.int32, (groups, block), 0)
    mixed = jnp.bitwise_xor(row_group, col_group)
    level_out = jnp.zeros((groups, block), jnp.int32)
    for bit_pos in range(base - inner):
        level_out = level_out + (jnp.right_shift(mixed, bit_pos) > 0).astype(jnp.int32)
    level_out = jnp.where(col_group < row_group, level_out + inner, -1)

    for idx in range(tokens // block):
        gates = [
            gates_ref[level : level + 1, idx * block : (idx + 1) * block] * level_weight(level)
            for level in range(base + 1)
        ]
        inside = jnp.zeros((SUBLANES, block), jnp.float32)
        for level in range(inner + 1):
            inside = jnp.where(level_in == level, gates[level], inside)
        outside = jnp.zeros((groups, block), jnp.float32)
        for level in range(inner + 1, base + 1):
            outside = jnp.where(level_out == level, gates[level], outside)
        for group in range(groups):
            mix[idx, group * SUBLANES : (group + 1) * SUBLANES, :] = jnp.where(
                lane_group == group, inside, outside[group : group + 1, :]
            )

    def diagonal_sums(product):
        parts = [product[group * SUBLANES : (group + 1) * SUBLANES, :] for group in range(groups)]
        inside = parts[0]
        for group in range(1, groups):
            inside = jnp.where(lane_group == group, parts[group], inside)
        totals = [jnp.where(level_in == level, inside, 0.0) for level in range(inner + 1)]
        for level in range(inner + 1, base + 1):
            picked = parts[0]
            for pair in range(1, len(parts) // 2):
                picked = jnp.where(jnp.right_shift(lane_group, level - inner) == pair, parts[2 * pair], picked)
            right = jnp.bitwise_and(jnp.right_shift(lane_group, level - inner - 1), 1) == 1
            totals.append(jnp.where(right, picked, 0.0))
            parts = [parts[2 * pair] + parts[2 * pair + 1] for pair in range(len(parts) // 2)]
        return [jnp.sum(total, axis=0, keepdims=True) for total in totals]

    for t_start in range(0, tokens, wide):
        t_end = t_start + wide
        t_slice = slice(t_start, t_end)
        idx = t_start // block
        low = slice(t_start, t_start + block)
        high = slice(t_start + block, t_end)
        near = base + 1
        chunks = []
        s_start = 0
        while s_start < t_start:
            level = (s_start ^ t_start).bit_length()
            size = min(1 << (level - 1), t_start - s_start)
            chunks.append((s_start, s_start + size, level))
            s_start += size
        level_sums = {}
        cross_sums = [None] * cross_levels
        for head in range(head_count):
            keys = slice(head * key_width, (head + 1) * key_width)
            vals = slice(head * value_width, (head + 1) * value_width)
            q_cols = query_ref[t_slice, keys].T
            g_cols = grad_ref[t_slice, vals].T
            key_t[head, :, t_slice] = key_ref[t_slice, keys].T
            grad_t[head, :, t_slice] = g_cols
            for s_start, s_end, level in chunks:
                s_slice = slice(s_start, s_end)
                gate = gates_ref[level : level + 1, t_slice] * level_weight(level)
                score = dot(key_ref[s_slice, keys], q_cols)
                grad_score = dot(value_ref[s_slice, vals], g_cols)
                product = jnp.sum((score * grad_score).reshape(-1, SUBLANES, wide), axis=0)
                level_sums[level] = level_sums[level] + product if level in level_sums else product
                weights[s_slice, :] = (gate * score).astype(jnp.bfloat16)
                grad_weights[s_slice, :] = (gate * grad_score).astype(jnp.bfloat16)
            score = dot(key_ref[t_slice, keys], q_cols)
            grad_score = dot(value_ref[t_slice, vals], g_cols)
            product = score * grad_score
            gate = jnp.broadcast_to(gates_ref[near : near + 1, high] * level_weight(near), (block, block))
            tile = jnp.concatenate([mix[idx], gate], axis=1)
            weights[low, :] = (tile * score[:block]).astype(jnp.bfloat16)
            grad_weights[low, :] = (tile * grad_score[:block]).astype(jnp.bfloat16)
            zeros = jnp.zeros((block, block), jnp.bfloat16)
            tile = mix[idx + 1]
            weights[high, :block] = zeros
            grad_weights[high, :block] = zeros
            weights[high, block:] = (tile * score[block:, block:]).astype(jnp.bfloat16)
            grad_weights[high, block:] = (tile * grad_score[block:, block:]).astype(jnp.bfloat16)
            three = [product[:block, :block], product[:block, block:], product[block:, block:]]
            if head > 0:
                three = [part + sums[k] for k, part in enumerate(three)]
            if head < head_count - 1:
                for k, part in enumerate(three):
                    sums[k] = part

            s_all = slice(0, t_end)
            query_total = dot(key_t[head, :, s_all], grad_weights[s_all, :])
            stacked = states_ref[0, :cross_levels, head].reshape(cross_levels * key_width, value_width)
            projected = dot(stacked, g_cols)
            q_wide = q_cols.astype(jnp.float32)
            for level_idx in range(cross_levels):
                row = local_levels + level_idx
                part = projected[level_idx * key_width : (level_idx + 1) * key_width]
                query_total += (gates_ref[row : row + 1, t_slice] * shard_bit(level_idx)) * part
                total = jnp.sum((q_wide * part).reshape(-1, SUBLANES, wide), axis=0)
                cross_sums[level_idx] = total if head == 0 else cross_sums[level_idx] + total
            query_out[t_slice, keys] = query_total.astype(jnp.bfloat16).T
            key_part = dot(grad_weights[s_all, :], query_ref[t_slice, keys])
            value_part = dot(weights[s_all, :], grad_ref[t_slice, vals])
            key_out[t_slice, keys] = key_part[t_start:]
            value_out[t_slice, vals] = value_part[t_start:]
            if t_start:
                key_out[:t_start, keys] += key_part[:t_start]
                value_out[:t_start, vals] += value_part[:t_start]

        for level in range(near + 1, local_levels):
            if level in level_sums:
                total = jnp.sum(level_sums[level], axis=0, keepdims=True) * level_weight(level)
            else:
                total = jnp.zeros((1, wide), jnp.float32)
            coef_out[level : level + 1, t_slice] = total
        coef_out[near : near + 1, low] = jnp.zeros((1, block), jnp.float32)
        coef_out[near : near + 1, high] = jnp.sum(three[1], axis=0, keepdims=True) * level_weight(near)
        for part, where in ((three[0], low), (three[2], high)):
            for level, total in enumerate(diagonal_sums(part)):
                coef_out[level : level + 1, where] = total * level_weight(level)
        for level_idx, total in enumerate(cross_sums):
            row = local_levels + level_idx
            coef_out[row : row + 1, t_slice] = jnp.sum(total, axis=0, keepdims=True) * shard_bit(level_idx)

    level_count = coef_out.shape[0]
    if local_levels + cross_levels < level_count:
        coef_out[local_levels + cross_levels :, :] = jnp.zeros(
            (level_count - local_levels - cross_levels, tokens), jnp.float32
        )
    rows = [local_levels + level_idx for level_idx in range(cross_levels - 1)]
    for head in range(head_count):
        if not rows:
            break
        keys = slice(head * key_width, (head + 1) * key_width)
        stacked = state_gradients(rows, query_ref[:, keys], grad_t[head], gates_ref)
        for level_idx, row in enumerate(rows):
            part = stacked[level_idx * value_width : (level_idx + 1) * value_width]
            state_outs[level_idx][head] = part * (shard_bit(level_idx) * level_weight(row))


def apply_kernel(
    head_count, key_ref, value_ref, key_local, value_local, state_ref, received_ref, coef_ref, coef_received,
    key_out, value_out, coef_out, key_total, value_total, coef_total, sems,
):
    tokens = key_ref.shape[0]
    key_width = key_ref.shape[1] // head_count
    value_width = value_ref.shape[1] // head_count
    wide = 2 * LANES
    coef_total[...] = coef_ref[...] + coef_received[...]
    copies = [pltpu.make_async_copy(coef_total, coef_out, sems.at[0])]
    copies[0].start()
    states = [(state_ref[head] + received_ref[head]).astype(jnp.bfloat16) for head in range(head_count)]
    flipped = [state.T for state in states]
    for start in range(0, tokens, wide):
        part = slice(start, start + wide)
        for head in range(head_count):
            keys = slice(head * key_width, (head + 1) * key_width)
            vals = slice(head * value_width, (head + 1) * value_width)
            key_total[part, keys] = (key_local[part, keys] + dot(value_ref[part, vals], states[head])).astype(
                jnp.bfloat16
            )
            value_total[part, vals] = (value_local[part, vals] + dot(key_ref[part, keys], flipped[head])).astype(
                jnp.bfloat16
            )
        for source, target in ((key_total, key_out), (value_total, value_out)):
            copy = pltpu.make_async_copy(
                source.at[start : start + wide, :], target.at[start : start + wide, :], sems.at[len(copies)]
            )
            copy.start()
            copies.append(copy)
    for copy in copies:
        copy.wait()


def shards(queries, key_vectors, values, out_grad, level_coef, saved_states):
    tokens, key_cols = queries.shape
    value_cols = values.shape[1]
    cross_levels = saved_states.shape[1]
    head_count = saved_states.shape[2]
    key_width = saved_states.shape[3]
    value_width = saved_states.shape[4]
    local_levels = level_coef.shape[0] - cross_levels
    shard_count = lax.axis_size("seq")
    bit_count = shard_count.bit_length() - 1
    block = LANES
    wide = 2 * block
    vmem = pl.BlockSpec(memory_space=pltpu.VMEM)
    hbm = pl.BlockSpec(memory_space=pltpu.HBM)
    state_shape = jax.ShapeDtypeStruct((head_count, value_width, key_width), jnp.float32)

    inputs = (queries, key_vectors, values, out_grad, level_coef, saved_states)
    *inputs, top = pl.pallas_call(
        functools.partial(top_kernel, head_count, bit_count - 1, local_levels + bit_count - 1),
        in_specs=[hbm] * 6,
        out_specs=[vmem] * 7,
        out_shape=[jax.ShapeDtypeStruct(x.shape, x.dtype) for x in inputs] + [state_shape],
        scratch_shapes=[pltpu.SemaphoreType.DMA((2 * head_count + 4,))],
        compiler_params=pltpu.CompilerParams(vmem_limit_bytes=8 * MIB),
    )(*[pltpu.with_memory_space_constraint(x, pltpu.HBM) for x in inputs])

    def exchange(value, axis, bit_pos):
        pairs = [(p, p ^ 2**bit_pos) for p in range(lax.axis_size(axis))]
        return lax.ppermute(value, axis, pairs)

    received = exchange(top, "seq", bit_count - 1)

    flops = 8 * head_count * tokens * tokens * key_width
    query_grad, key_local, value_local, coef_grad, *contrib = pl.pallas_call(
        functools.partial(local_kernel, local_levels, bit_count, head_count),
        in_specs=[vmem] * 6,
        out_specs=[vmem] * (4 + bit_count - 1),
        out_shape=[
            jax.ShapeDtypeStruct(queries.shape, jnp.bfloat16),
            jax.ShapeDtypeStruct(queries.shape, jnp.float32),
            jax.ShapeDtypeStruct(values.shape, jnp.float32),
            jax.ShapeDtypeStruct(level_coef.shape, jnp.float32),
        ]
        + [state_shape] * (bit_count - 1),
        scratch_shapes=[
            pltpu.VMEM((head_count, key_width, tokens), jnp.bfloat16),
            pltpu.VMEM((head_count, value_width, tokens), jnp.bfloat16),
            pltpu.VMEM((tokens // block, block, block), jnp.float32),
            pltpu.VMEM((3, block, block), jnp.float32),
            pltpu.VMEM((tokens, wide), jnp.bfloat16),
            pltpu.VMEM((tokens, wide), jnp.bfloat16),
        ],
        compiler_params=pltpu.CompilerParams(vmem_limit_bytes=24 * MIB),
        cost_estimate=pl.CostEstimate(flops=flops, bytes_accessed=8 * MIB, transcendentals=0),
    )(*inputs)

    grad_state = jnp.zeros(state_shape.shape, jnp.float32)
    for level_idx in reversed(range(bit_count - 1)):
        grad_state = grad_state + received
        received = exchange(grad_state + contrib[level_idx], "seq", level_idx)

    head_bits = lax.axis_size("head").bit_length() - 1
    coef_received = jnp.zeros_like(coef_grad)
    for bit_pos in range(head_bits):
        if bit_pos:
            coef_grad = coef_grad + coef_received
        coef_received = exchange(coef_grad, "head", bit_pos)

    pieces = 2 * (tokens // wide) + 1
    key_grad, value_grad, coef_grad = pl.pallas_call(
        functools.partial(apply_kernel, head_count),
        in_specs=[vmem] * 8,
        out_specs=[hbm] * 3,
        out_shape=[
            jax.ShapeDtypeStruct(queries.shape, jnp.bfloat16),
            jax.ShapeDtypeStruct(values.shape, jnp.bfloat16),
            jax.ShapeDtypeStruct(level_coef.shape, jnp.float32),
        ],
        scratch_shapes=[
            pltpu.VMEM(queries.shape, jnp.bfloat16),
            pltpu.VMEM(values.shape, jnp.bfloat16),
            pltpu.VMEM(level_coef.shape, jnp.float32),
            pltpu.SemaphoreType.DMA((pieces,)),
        ],
        compiler_params=pltpu.CompilerParams(vmem_limit_bytes=12 * MIB),
    )(inputs[1], inputs[2], key_local, value_local, grad_state, received, coef_grad, coef_received)
    return (query_grad, key_grad, value_grad, coef_grad)


def solution(mesh):
    in_specs = (
        P("seq", "head"),
        P("seq", "head"),
        P("seq", "head"),
        P("seq", "head"),
        P(None, "seq"),
        P("seq", None, "head", None, None),
    )
    out_specs = (P("seq", "head"), P("seq", "head"), P("seq", "head"), P(None, "seq"))
    return jax.shard_map(shards, mesh=mesh, in_specs=in_specs, out_specs=out_specs, check_vma=False)
```

time: 120 us -> 25.7 us (0.21)
  other arithmetic: 42.9 us -> 0.05 us
  local copies, waits for them, and re-layouts: 28.4 us -> 0 us
  matrix products: 19 us -> 0 us
  between operations: 15.6 us -> 0.66 us
  Pallas kernels: 0 us -> 8.28 us
  waiting for transfers between devices: 3.65 us -> 8.42 us
  starting transfers between devices: 9.67 us -> 8.11 us
    reduce_sum x36 -> x0, other arithmetic: 19.1 us -> none  [the longest x18 11.2 us: level_sums(): blocked = blocked.reshape(row_total, blocked.shape[1] // 2, 2).sum(axis=2)]
    dot_general x14 -> x0, matrix products: 19 us -> none  [the longest x2 5.18 us: shards(): jnp.einsum('thd,shd->hts', query_rows, key_cols, preferred_element_type=j...]
    xor x19 -> x0, other arithmetic: 11.1 us -> none  [level_sums(): sibling = jnp.bitwise_xor(jnp.right_shift(row_pos, level_idx - 1), 1)]
    reduce_sum x6 -> x0, local copies, waits for them, and re-layouts: 9.42 us -> none  [the longest x4 6.52 us: shards(): products = jnp.where(causal, jnp.sum(scores * grad_scores, axis=0), 0.0)]
    pallas_call x0 -> x3, Pallas kernels: none -> 8.28 us  [the longest x1 5.26 us: shards(): pl.pallas_call(functools.partial(local_kernel, local_levels, bit_count, h...]
    unnamed x164 -> x0, local copies, waits for them, and re-layouts: 6.69 us -> none
    ppermute x6 -> x5, waiting for transfers between devices: 2.02 us -> 8.42 us  [exchange(): return lax.ppermute(value, axis, pairs)]
    reshape x18 -> x0, local copies, waits for them, and re-layouts: 6.29 us -> none  [the longest x15 2.86 us: level_sums(): blocked = blocked.reshape(row_total, blocked.shape[1] // 2, 2).sum(axis=2)]
  transfers between devices with their start and end apart: 7 -> 5, of which waited for: 3 -> 3; matrix products, arithmetic and copies ran while one was open for 67% -> 0% of each run, Pallas kernels for 0% -> 21%
where the time goes in v3:
time: 25.7 us; the launch traced here: 25.5 us
  waiting for transfers between devices  8.42 us (33%)
  Pallas kernels  8.28 us (32%)
  starting transfers between devices  8.11 us (32%)
  between operations  0.66 us (3%)
    ppermute x5, waiting for transfers between devices, exchange(): return lax.ppermute(value, axis, pairs)  8.42 us
    ppermute x5, starting transfers between devices, exchange(): return lax.ppermute(value, axis, pairs)  8.11 us
    pallas_call x1, Pallas kernels, shards(): pl.pallas_call(functools.partial(local_kernel, local_levels, bit_count, h...  5.26 us
    pallas_call x1, Pallas kernels, shards(): pl.pallas_call(functools.partial(top_kernel, head_count, bit_count - 1, l...  1.78 us
    pallas_call x1, Pallas kernels, shards(): pl.pallas_call(functools.partial(apply_kernel, head_count), in_specs=[vme...  1.25 us
  transfers between devices with their start and end apart: 5, of which 3 were waited for; matrix products, arithmetic and copies ran while one was open for 0% of the time, Pallas kernels for 21%

profile of v3, /device:TPU:0, one launch (start us, length us, event | category | flops | bytes accessed | tf_op | source)
XLA Modules:
  0.0 25.5 jit_solution(3532778158428260992)
XLA Ops:
  0.6 1.8 %shard_map.93 = (bf16[1024,256]{1,0:T(8,128)(2,1)S(1)}, bf16[1024,256]{1,0:T(8,128)(2,1)S(1)}, bf16[1024,256]{1,0:T(8,128)(2,1)S(1)}, bf16[1024,256]{1,0:T(8,128...) custom-call(bf16[1024,256]{1,0:T(8,128)(2,1)} %refs_0_.1, ...), custom_call_target="tpu_custom_call" | custom-call | tf_op jit(solution)/shard_map/pallas_call | solution.py:283
  2.4 4.1 %collective-permute-start = (f32[2,128,128]{2,1,0:T(8,128)S(1)}, f32[2,128,128]{2,1,0:T(8,128)S(1)}, u32[]{:S(2)}, u32[]{:S(2)}) collective-permute-start(f32[2,128,128]{2,1,0:T(8,128)S(1)} %get-tuple-element.29), channel_id=1, source_target_pairs={{0,16},{4,20},{8,24},{12,28},{16,0},{20,4},{24,8},{28,12},{1,17},{... | collective-permute-start | bytes 393224 | tf_op jit(solution)/shard_map/ppermute | solution.py:294
  6.5 5.3 %shard_map.94 = (bf16[1024,256]{1,0:T(8,128)(2,1)}, f32[1024,256]{1,0:T(8,128)S(1)}, f32[1024,256]{1,0:T(8,128)S(1)}, f32[17,1024]{1,0:T(8,128)S(1)}, f32[2,128,...) custom-call(bf16[1024,256]{1,0:T(8,128)(2,1)S(1)} %get-tuple-element.20.query_ref, ...), custom_call_target="tpu_custom_call" | custom-call | flops 2147483648 | bytes 8388608 | tf_op jit(solution)/shard_map/pallas_call | solution.py:299
  11.8 1.0 %collective-permute-done = f32[2,128,128]{2,1,0:T(8,128)S(1)} collective-permute-done((f32[2,128,128]{2,1,0:T(8,128)S(1)}, f32[2,128,128]{2,1,0:T(8,128)S(1)}, u32[]{:S(2)}, u32[]{:S(2)}) %collective-permute-start) | collective-permute-done | bytes 131104 | tf_op jit(solution)/shard_map/ppermute | solution.py:294
  12.9 0.8 %collective-permute-start.1 = (f32[2,128,128]{2,1,0:T(8,128)S(1)}, f32[2,128,128]{2,1,0:T(8,128)S(1)}, u32[]{:S(2)}, u32[]{:S(2)}) collective-permute-start(f32[2,128,128]{2,1,0:T(8,128)S(1)} %add.12), channel_id=1, source_target_pairs={{0,8},{4,12},{8,0},{12,4},{16,24},{20,28},{24,16},{28,20},{1,9},{5... | collective-permute-start | bytes 393224 | tf_op jit(solution)/shard_map/ppermute | solution.py:294
  13.7 0.0 collective-permute-start.3
  13.7 4.2 %collective-permute-done.1 = f32[2,128,128]{2,1,0:T(8,128)S(1)} collective-permute-done((f32[2,128,128]{2,1,0:T(8,128)S(1)}, f32[2,128,128]{2,1,0:T(8,128)S(1)}, u32[]{:S(2)}, u32[]{:S(2)}) %collective-permute-start.1) | collective-permute-done | bytes 131104 | tf_op jit(solution)/shard_map/ppermute | solution.py:294
  17.9 1.6 %collective-permute-start.2 = (f32[2,128,128]{2,1,0:T(8,128)S(1)}, f32[2,128,128]{2,1,0:T(8,128)S(1)}, u32[]{:S(2)}, u32[]{:S(2)}) collective-permute-start(f32[2,128,128]{2,1,0:T(8,128)S(1)} %get-tuple-element.36), channel_id=1, source_target_pairs={{0,4},{4,0},{8,12},{12,8},{16,20},{20,16},{24,28},{28,24},{1,5},{5... | collective-permute-start | bytes 393224 | tf_op jit(solution)/shard_map/ppermute | solution.py:294
  19.6 0.0 collective-permute-done.3
  19.6 1.6 %collective-permute-start.4 = (f32[17,1024]{1,0:T(8,128)S(1)}, f32[17,1024]{1,0:T(8,128)S(1)}, u32[]{:S(2)}, u32[]{:S(2)}) collective-permute-start(f32[17,1024]{1,0:T(8,128)S(1)} %add.15.coef_ref), channel_id=1, source_target_pairs={{0,2},{1,3},{2,0},{3,1},{4,6},{5,7},{6,4},{7,5},{8,10},{9,11},{10,... | collective-permute-start | bytes 208904 | tf_op jit(solution)/shard_map/ppermute | solution.py:294
  21.1 3.1 %collective-permute-done.4.coef_received = f32[17,1024]{1,0:T(8,128)S(1)} collective-permute-done((f32[17,1024]{1,0:T(8,128)S(1)}, f32[17,1024]{1,0:T(8,128)S(1)}, u32[]{:S(2)}, u32[]{:S(2)}) %collective-permute-start.4) | collective-permute-done | bytes 69664 | tf_op jit(solution)/shard_map/ppermute | solution.py:294
  24.3 0.0 collective-permute-done.2.received_ref
  24.3 1.2 %shard_map.95 = (bf16[1024,256]{1,0:T(8,128)(2,1)}, bf16[1024,256]{1,0:T(8,128)(2,1)}, f32[17,1024]{1,0:T(8,128)}) custom-call(bf16[1024,256]{1,0:T(8,128)(2,1)S(1)} %get-tuple-element.21.key_ref, bf16[1024,256]{1,0:T(8,128)(2,1)S(1)} %get-tuple-element.22.value_ref, f32[1024,256]{1,0:T(8,128)S(1)} %get-tuple-element.27.key_local, ...), custom_call_target="tpu_custom_call" | custom-call | tf_op jit(solution)/shard_map/pallas_call | solution.py:335
  (3 shorter events, 0.1 us)
Async XLA Ops:
  2.4 10.4 %collective-permute-start = (f32[2,128,128]{2,1,0:T(8,128)S(1)}, f32[2,128,128]{2,1,0:T(8,128)S(1)}, u32[]{:S(2)}, u32[]{:S(2)}) collective-permute-start(f32[2,128,128]{2,1,0:T(8,128)S(1)} %get-tuple-element.29), channel_id=1, source_target_pairs={{0,16},{4,20},{8,24},{12,28},{16,0},{20,4},{24,8},{28,12},{1,17},{... | collective-permute-start | bytes 393224 | tf_op jit(solution)/shard_map/ppermute | solution.py:294
  12.9 5.0 %collective-permute-start.1 = (f32[2,128,128]{2,1,0:T(8,128)S(1)}, f32[2,128,128]{2,1,0:T(8,128)S(1)}, u32[]{:S(2)}, u32[]{:S(2)}) collective-permute-start(f32[2,128,128]{2,1,0:T(8,128)S(1)} %add.12), channel_id=1, source_target_pairs={{0,8},{4,12},{8,0},{12,4},{16,24},{20,28},{24,16},{28,20},{1,9},{5... | collective-permute-start | bytes 393224 | tf_op jit(solution)/shard_map/ppermute | solution.py:294
  13.7 5.9 %collective-permute-start.3 = (f32[17,1024]{1,0:T(8,128)S(1)}, f32[17,1024]{1,0:T(8,128)S(1)}, u32[]{:S(2)}, u32[]{:S(2)}) collective-permute-start(f32[17,1024]{1,0:T(8,128)S(1)} %get-tuple-element.32), channel_id=1, source_target_pairs={{0,1},{1,0},{2,3},{3,2},{4,5},{5,4},{6,7},{7,6},{8,9},{9,8},{10,11... | collective-permute-start | bytes 208904 | tf_op jit(solution)/shard_map/ppermute | solution.py:294
  17.9 6.3 %collective-permute-start.2 = (f32[2,128,128]{2,1,0:T(8,128)S(1)}, f32[2,128,128]{2,1,0:T(8,128)S(1)}, u32[]{:S(2)}, u32[]{:S(2)}) collective-permute-start(f32[2,128,128]{2,1,0:T(8,128)S(1)} %get-tuple-element.36), channel_id=1, source_target_pairs={{0,4},{4,0},{8,12},{12,8},{16,20},{20,16},{24,28},{28,24},{1,5},{5... | collective-permute-start | bytes 393224 | tf_op jit(solution)/shard_map/ppermute | solution.py:294
  19.6 4.7 %collective-permute-start.4 = (f32[17,1024]{1,0:T(8,128)S(1)}, f32[17,1024]{1,0:T(8,128)S(1)}, u32[]{:S(2)}, u32[]{:S(2)}) collective-permute-start(f32[17,1024]{1,0:T(8,128)S(1)} %add.15.coef_ref), channel_id=1, source_target_pairs={{0,2},{1,3},{2,0},{3,1},{4,6},{5,7},{6,4},{7,5},{8,10},{9,11},{10,... | collective-permute-start | bytes 208904 | tf_op jit(solution)/shard_map/ppermute | solution.py:294

commit v4 on v3

--- a/solution.py
+++ b/solution.py
@@ -7,6 +7,7 @@
 from jax.experimental.pallas import tpu as pltpu
 from jax.sharding import PartitionSpec as P
 
+
 LANES = 128
 SUBLANES = 8
 MIB = 2**20
@@ -34,7 +35,7 @@
 
 def top_kernel(head_count, level_idx, row, *refs):
     query_hbm, key_hbm, value_hbm, grad_hbm, gates_hbm, states_hbm = refs[:6]
-    query, key, value, grad, gates, states, out_ref, sems = refs[6:]
+    query, key, value, grad, gates, states, *out_refs, sems = refs[6:]
     key_width = query.shape[1] // head_count
     value_width = grad.shape[1] // head_count
     first = [pltpu.make_async_copy(gates_hbm, gates, sems.at[0])]
@@ -54,7 +55,7 @@
         grad_t = grad[:, head * value_width : (head + 1) * value_width].T
         first[2 * head + 2].wait()
         keys = slice(head * key_width, (head + 1) * key_width)
-        out_ref[head] = state_gradients([row], query[:, keys], grad_t, gates) * scale
+        out_refs[head][...] = state_gradients([row], query[:, keys], grad_t, gates) * scale
     for copy in later:
         copy.wait()
 
@@ -74,8 +75,7 @@
     query_ref, key_ref, value_ref, grad_ref, gates_ref, states_ref,
     query_out, key_out, value_out, coef_out, *rest,
 ):
-    state_outs = rest[: cross_levels - 1]
-    key_t, grad_t, mix, sums, weights, grad_weights = rest[cross_levels - 1 :]
+    *state_outs, key_t, grad_t, mix, sums, weights, grad_weights = rest
     tokens = query_ref.shape[0]
     key_width = query_ref.shape[1] // head_count
     value_width = value_ref.shape[1] // head_count
@@ -226,13 +226,14 @@
         stacked = state_gradients(rows, query_ref[:, keys], grad_t[head], gates_ref)
         for level_idx, row in enumerate(rows):
             part = stacked[level_idx * value_width : (level_idx + 1) * value_width]
-            state_outs[level_idx][head] = part * (shard_bit(level_idx) * level_weight(row))
+            state_outs[level_idx * head_count + head][...] = part * (shard_bit(level_idx) * level_weight(row))
 
 
 def apply_kernel(
-    head_count, key_ref, value_ref, key_local, value_local, state_ref, received_ref, coef_ref, coef_received,
-    key_out, value_out, coef_out, key_total, value_total, coef_total, sems,
+    head_count, key_ref, value_ref, key_local, value_local, coef_ref, coef_received, *refs,
 ):
+    state_refs = refs[: 2 * head_count]
+    key_out, value_out, coef_out, key_total, value_total, coef_total, sems = refs[2 * head_count :]
     tokens = key_ref.shape[0]
     key_width = key_ref.shape[1] // head_count
     value_width = value_ref.shape[1] // head_count
@@ -240,7 +241,9 @@
     coef_total[...] = coef_ref[...] + coef_received[...]
     copies = [pltpu.make_async_copy(coef_total, coef_out, sems.at[0])]
     copies[0].start()
-    states = [(state_ref[head] + received_ref[head]).astype(jnp.bfloat16) for head in range(head_count)]
+    states = [
+        (state_refs[head][...] + state_refs[head_count + head][...]).astype(jnp.bfloat16) for head in range(head_count)
+    ]
     flipped = [state.T for state in states]
     for start in range(0, tokens, wide):
         part = slice(start, start + wide)
@@ -264,8 +267,7 @@
 
 
 def shards(queries, key_vectors, values, out_grad, level_coef, saved_states):
-    tokens, key_cols = queries.shape
-    value_cols = values.shape[1]
+    tokens, _ = queries.shape
     cross_levels = saved_states.shape[1]
     head_count = saved_states.shape[2]
     key_width = saved_states.shape[3]
@@ -277,36 +279,39 @@
     wide = 2 * block
     vmem = pl.BlockSpec(memory_space=pltpu.VMEM)
     hbm = pl.BlockSpec(memory_space=pltpu.HBM)
-    state_shape = jax.ShapeDtypeStruct((head_count, value_width, key_width), jnp.float32)
+    state_shape = jax.ShapeDtypeStruct((value_width, key_width), jnp.float32)
+    heads = range(head_count)
 
     inputs = (queries, key_vectors, values, out_grad, level_coef, saved_states)
-    *inputs, top = pl.pallas_call(
+    count = len(inputs)
+    results = pl.pallas_call(
         functools.partial(top_kernel, head_count, bit_count - 1, local_levels + bit_count - 1),
         in_specs=[hbm] * 6,
-        out_specs=[vmem] * 7,
-        out_shape=[jax.ShapeDtypeStruct(x.shape, x.dtype) for x in inputs] + [state_shape],
+        out_specs=[vmem] * (count + head_count),
+        out_shape=[jax.ShapeDtypeStruct(x.shape, x.dtype) for x in inputs] + [state_shape] * head_count,
         scratch_shapes=[pltpu.SemaphoreType.DMA((2 * head_count + 4,))],
         compiler_params=pltpu.CompilerParams(vmem_limit_bytes=8 * MIB),
     )(*[pltpu.with_memory_space_constraint(x, pltpu.HBM) for x in inputs])
+    inputs, tops = results[:count], results[count:]
 
     def exchange(value, axis, bit_pos):
         pairs = [(p, p ^ 2**bit_pos) for p in range(lax.axis_size(axis))]
         return lax.ppermute(value, axis, pairs)
 
-    received = exchange(top, "seq", bit_count - 1)
+    received = [exchange(tops[head], "seq", bit_count - 1) for head in heads]
 
     flops = 8 * head_count * tokens * tokens * key_width
-    query_grad, key_local, value_local, coef_grad, *contrib = pl.pallas_call(
+    local_call = pl.pallas_call(
         functools.partial(local_kernel, local_levels, bit_count, head_count),
         in_specs=[vmem] * 6,
-        out_specs=[vmem] * (4 + bit_count - 1),
+        out_specs=[vmem] * (4 + (bit_count - 1) * head_count),
         out_shape=[
             jax.ShapeDtypeStruct(queries.shape, jnp.bfloat16),
             jax.ShapeDtypeStruct(queries.shape, jnp.float32),
             jax.ShapeDtypeStruct(values.shape, jnp.float32),
             jax.ShapeDtypeStruct(level_coef.shape, jnp.float32),
         ]
-        + [state_shape] * (bit_count - 1),
+        + [state_shape] * ((bit_count - 1) * head_count),
         scratch_shapes=[
             pltpu.VMEM((head_count, key_width, tokens), jnp.bfloat16),
             pltpu.VMEM((head_count, value_width, tokens), jnp.bfloat16),
@@ -317,24 +322,27 @@
         ],
         compiler_params=pltpu.CompilerParams(vmem_limit_bytes=24 * MIB),
         cost_estimate=pl.CostEstimate(flops=flops, bytes_accessed=8 * MIB, transcendentals=0),
-    )(*inputs)
-
-    grad_state = jnp.zeros(state_shape.shape, jnp.float32)
+    )
+    query_grad, key_local, value_local, coef_grad, *contrib = local_call(*inputs)
+
+    grad_state = [jnp.zeros(state_shape.shape, jnp.float32) for _ in heads]
     for level_idx in reversed(range(bit_count - 1)):
-        grad_state = grad_state + received
-        received = exchange(grad_state + contrib[level_idx], "seq", level_idx)
+        for head in heads:
+            grad_state[head] = grad_state[head] + received[head]
+            own = contrib[level_idx * head_count + head]
+            received[head] = exchange(grad_state[head] + own, "seq", level_idx)
 
     head_bits = lax.axis_size("head").bit_length() - 1
     coef_received = jnp.zeros_like(coef_grad)
-    for bit_pos in range(head_bits):
-        if bit_pos:
+    for bit_pos in reversed(range(head_bits)):
+        if bit_pos < head_bits - 1:
             coef_grad = coef_grad + coef_received
         coef_received = exchange(coef_grad, "head", bit_pos)
 
     pieces = 2 * (tokens // wide) + 1
     key_grad, value_grad, coef_grad = pl.pallas_call(
         functools.partial(apply_kernel, head_count),
-        in_specs=[vmem] * 8,
+        in_specs=[vmem] * (6 + 2 * head_count),
         out_specs=[hbm] * 3,
         out_shape=[
             jax.ShapeDtypeStruct(queries.shape, jnp.bfloat16),
@@ -348,7 +356,7 @@
             pltpu.SemaphoreType.DMA((pieces,)),
         ],
         compiler_params=pltpu.CompilerParams(vmem_limit_bytes=12 * MIB),
-    )(inputs[1], inputs[2], key_local, value_local, grad_state, received, coef_grad, coef_received)
+    )(inputs[1], inputs[2], key_local, value_local, coef_grad, coef_received, *grad_state, *received)
     return (query_grad, key_grad, value_grad, coef_grad)
 
 
@@ -362,4 +370,5 @@
         P("seq", None, "head", None, None),
     )
     out_specs = (P("seq", "head"), P("seq", "head"), P("seq", "head"), P(None, "seq"))
+
     return jax.shard_map(shards, mesh=mesh, in_specs=in_specs, out_specs=out_specs, check_vma=False)

time: 25.7 us -> 28.7 us (1.12)
  starting transfers between devices: 8.11 us -> 12.4 us
  waiting for transfers between devices: 8.42 us -> 7.1 us
    ppermute x5 -> x8, starting transfers between devices: 8.11 us -> 12.4 us  [exchange(): return lax.ppermute(value, axis, pairs)]
    ppermute x5 -> x8, waiting for transfers between devices: 8.42 us -> 7.1 us  [exchange(): return lax.ppermute(value, axis, pairs)]
  transfers between devices with their start and end apart: 5 -> 8, of which waited for: 3 -> 4; matrix products, arithmetic and copies ran while one was open for 0% -> 0% of each run, Pallas kernels for 21% -> 18%
where the time goes in v4:
time: 28.7 us; the launch traced here: 28.5 us
  starting transfers between devices  12.4 us (43%)
  Pallas kernels  8.28 us (29%)
  waiting for transfers between devices  7.1 us (25%)
  between operations  0.69 us (2%)
    ppermute x8, starting transfers between devices, exchange(): return lax.ppermute(value, axis, pairs)  12.4 us
    ppermute x8, waiting for transfers between devices, exchange(): return lax.ppermute(value, axis, pairs)  7.1 us
    pallas_call x1, Pallas kernels, shards(): local_call(*inputs)  5.26 us
    pallas_call x1, Pallas kernels, shards(): pl.pallas_call(functools.partial(top_kernel, head_count, bit_count - 1, l...  1.78 us
    pallas_call x1, Pallas kernels, shards(): pl.pallas_call(functools.partial(apply_kernel, head_count), in_specs=[vme...  1.24 us
  transfers between devices with their start and end apart: 8, of which 4 were waited for; matrix products, arithmetic and copies ran while one was open for 0% of the time, Pallas kernels for 18%

profile of v4, /device:TPU:0, one launch (start us, length us, event | category | flops | bytes accessed | tf_op | source)
XLA Modules:
  0.0 28.5 jit_solution(18312122442243461097)
XLA Ops:
  0.6 1.8 %shard_map.93 = (bf16[1024,256]{1,0:T(8,128)(2,1)S(1)}, bf16[1024,256]{1,0:T(8,128)(2,1)S(1)}, bf16[1024,256]{1,0:T(8,128)(2,1)S(1)}, bf16[1024,256]{1,0:T(8,128...) custom-call(bf16[1024,256]{1,0:T(8,128)(2,1)} %refs_0_.1, ...), custom_call_target="tpu_custom_call" | custom-call | tf_op jit(solution)/shard_map/pallas_call | solution.py:287
  2.4 4.1 %collective-permute-start.4 = (f32[128,128]{1,0:T(8,128)S(1)}, f32[128,128]{1,0:T(8,128)S(1)}, u32[]{:S(2)}, u32[]{:S(2)}) collective-permute-start(f32[128,128]{1,0:T(8,128)S(1)} %get-tuple-element.35), channel_id=1, source_target_pairs={{0,16},{4,20},{8,24},{12,28},{16,0},{20,4},{24,8},{28,12},{1,17},{... | collective-permute-start | bytes 196616 | tf_op jit(solution)/shard_map/ppermute | solution.py:299
  6.5 5.3 %shard_map.94 = (bf16[1024,256]{1,0:T(8,128)(2,1)}, f32[1024,256]{1,0:T(8,128)S(1)}, f32[1024,256]{1,0:T(8,128)S(1)}, f32[17,1024]{1,0:T(8,128)S(1)}, f32[128,12...) custom-call(bf16[1024,256]{1,0:T(8,128)(2,1)S(1)} %get-tuple-element.23.query_ref, ...), custom_call_target="tpu_custom_call" | custom-call | flops 2147483648 | bytes 8388608 | tf_op jit(solution)/shard_map/pallas_call | solution.py:326
  11.8 1.5 %collective-permute-start = (f32[17,1024]{1,0:T(8,128)S(1)}, f32[17,1024]{1,0:T(8,128)S(1)}, u32[]{:S(2)}, u32[]{:S(2)}) collective-permute-start(f32[17,1024]{1,0:T(8,128)S(1)} %get-tuple-element.32), channel_id=1, source_target_pairs={{0,2},{1,3},{2,0},{3,1},{4,6},{5,7},{6,4},{7,5},{8,10},{9,11},{10,... | collective-permute-start | bytes 208904 | tf_op jit(solution)/shard_map/ppermute | solution.py:299
  13.3 0.3 %collective-permute-start.2 = (f32[128,128]{1,0:T(8,128)S(1)}, f32[128,128]{1,0:T(8,128)S(1)}, u32[]{:S(2)}, u32[]{:S(2)}) collective-permute-start(f32[128,128]{1,0:T(8,128)S(1)} %get-tuple-element.33), channel_id=1, source_target_pairs={{0,16},{4,20},{8,24},{12,28},{16,0},{20,4},{24,8},{28,12},{1,17},{... | collective-permute-start | bytes 196616 | tf_op jit(solution)/shard_map/ppermute | solution.py:299
  13.6 0.0 collective-permute-done.4
  13.7 1.6 %collective-permute-start.5 = (f32[128,128]{1,0:T(8,128)S(1)}, f32[128,128]{1,0:T(8,128)S(1)}, u32[]{:S(2)}, u32[]{:S(2)}) collective-permute-start(f32[128,128]{1,0:T(8,128)S(1)} %add.24), channel_id=1, source_target_pairs={{0,8},{4,12},{8,0},{12,4},{16,24},{20,28},{24,16},{28,20},{1,9},{5... | collective-permute-start | bytes 196616 | tf_op jit(solution)/shard_map/ppermute | solution.py:299
  15.3 3.3 %collective-permute-done.2 = f32[128,128]{1,0:T(8,128)S(1)} collective-permute-done((f32[128,128]{1,0:T(8,128)S(1)}, f32[128,128]{1,0:T(8,128)S(1)}, u32[]{:S(2)}, u32[]{:S(2)}) %collective-permute-start.2) | collective-permute-done | bytes 65568 | tf_op jit(solution)/shard_map/ppermute | solution.py:299
  18.6 1.5 %collective-permute-start.3 = (f32[128,128]{1,0:T(8,128)S(1)}, f32[128,128]{1,0:T(8,128)S(1)}, u32[]{:S(2)}, u32[]{:S(2)}) collective-permute-start(f32[128,128]{1,0:T(8,128)S(1)} %add.22), channel_id=1, source_target_pairs={{0,8},{4,12},{8,0},{12,4},{16,24},{20,28},{24,16},{28,20},{1,9},{5... | collective-permute-start | bytes 196616 | tf_op jit(solution)/shard_map/ppermute | solution.py:299
  20.1 0.0 collective-permute-done
  20.2 0.1 collective-permute-start.1
  20.2 0.0 collective-permute-done.5
  20.3 1.6 %collective-permute-start.7 = (f32[128,128]{1,0:T(8,128)S(1)}, f32[128,128]{1,0:T(8,128)S(1)}, u32[]{:S(2)}, u32[]{:S(2)}) collective-permute-start(f32[128,128]{1,0:T(8,128)S(1)} %get-tuple-element.42), channel_id=1, source_target_pairs={{0,4},{4,0},{8,12},{12,8},{16,20},{20,16},{24,28},{28,24},{1,5},{5... | collective-permute-start | bytes 196616 | tf_op jit(solution)/shard_map/ppermute | solution.py:299
  21.9 1.1 %collective-permute-done.3 = f32[128,128]{1,0:T(8,128)S(1)} collective-permute-done((f32[128,128]{1,0:T(8,128)S(1)}, f32[128,128]{1,0:T(8,128)S(1)}, u32[]{:S(2)}, u32[]{:S(2)}) %collective-permute-start.3) | collective-permute-done | bytes 65568 | tf_op jit(solution)/shard_map/ppermute | solution.py:299
  22.9 1.6 %collective-permute-start.6 = (f32[128,128]{1,0:T(8,128)S(1)}, f32[128,128]{1,0:T(8,128)S(1)}, u32[]{:S(2)}, u32[]{:S(2)}) collective-permute-start(f32[128,128]{1,0:T(8,128)S(1)} %get-tuple-element.44), channel_id=1, source_target_pairs={{0,4},{4,0},{8,12},{12,8},{16,20},{20,16},{24,28},{28,24},{1,5},{5... | collective-permute-start | bytes 196616 | tf_op jit(solution)/shard_map/ppermute | solution.py:299
  24.5 0.0 collective-permute-done.1.coef_received
  24.5 0.3 %collective-permute-done.7.refs_3_ = f32[128,128]{1,0:T(8,128)S(1)} collective-permute-done((f32[128,128]{1,0:T(8,128)S(1)}, f32[128,128]{1,0:T(8,128)S(1)}, u32[]{:S(2)}, u32[]{:S(2)}) %collective-permute-start.7) | collective-permute-done | bytes 65568 | tf_op jit(solution)/shard_map/ppermute | solution.py:299
  24.9 2.4 %collective-permute-done.6.refs_2_ = f32[128,128]{1,0:T(8,128)S(1)} collective-permute-done((f32[128,128]{1,0:T(8,128)S(1)}, f32[128,128]{1,0:T(8,128)S(1)}, u32[]{:S(2)}, u32[]{:S(2)}) %collective-permute-start.6) | collective-permute-done | bytes 65568 | tf_op jit(solution)/shard_map/ppermute | solution.py:299
  27.3 1.2 %shard_map.95 = (bf16[1024,256]{1,0:T(8,128)(2,1)}, bf16[1024,256]{1,0:T(8,128)(2,1)}, f32[17,1024]{1,0:T(8,128)}) custom-call(bf16[1024,256]{1,0:T(8,128)(2,1)S(1)} %get-tuple-element.24.key_ref, bf16[1024,256]{1,0:T(8,128)(2,1)S(1)} %get-tuple-element.25.value_ref, f32[1024,256]{1,0:T(8,128)S(1)} %get-tuple-element.30.key_local, ...), custom_call_target="tpu_custom_call" | custom-call | tf_op jit(solution)/shard_map/pallas_call | solution.py:343
  (5 shorter events, 0.1 us)
Async XLA Ops:
  2.4 11.2 %collective-permute-start.4 = (f32[128,128]{1,0:T(8,128)S(1)}, f32[128,128]{1,0:T(8,128)S(1)}, u32[]{:S(2)}, u32[]{:S(2)}) collective-permute-start(f32[128,128]{1,0:T(8,128)S(1)} %get-tuple-element.35), channel_id=1, source_target_pairs={{0,16},{4,20},{8,24},{12,28},{16,0},{20,4},{24,8},{28,12},{1,17},{... | collective-permute-start | bytes 196616 | tf_op jit(solution)/shard_map/ppermute | solution.py:299
  11.8 8.3 %collective-permute-start = (f32[17,1024]{1,0:T(8,128)S(1)}, f32[17,1024]{1,0:T(8,128)S(1)}, u32[]{:S(2)}, u32[]{:S(2)}) collective-permute-start(f32[17,1024]{1,0:T(8,128)S(1)} %get-tuple-element.32), channel_id=1, source_target_pairs={{0,2},{1,3},{2,0},{3,1},{4,6},{5,7},{6,4},{7,5},{8,10},{9,11},{10,... | collective-permute-start | bytes 208904 | tf_op jit(solution)/shard_map/ppermute | solution.py:299
  13.3 5.3 %collective-permute-start.2 = (f32[128,128]{1,0:T(8,128)S(1)}, f32[128,128]{1,0:T(8,128)S(1)}, u32[]{:S(2)}, u32[]{:S(2)}) collective-permute-start(f32[128,128]{1,0:T(8,128)S(1)} %get-tuple-element.33), channel_id=1, source_target_pairs={{0,16},{4,20},{8,24},{12,28},{16,0},{20,4},{24,8},{28,12},{1,17},{... | collective-permute-start | bytes 196616 | tf_op jit(solution)/shard_map/ppermute | solution.py:299
  13.7 6.6 %collective-permute-start.5 = (f32[128,128]{1,0:T(8,128)S(1)}, f32[128,128]{1,0:T(8,128)S(1)}, u32[]{:S(2)}, u32[]{:S(2)}) collective-permute-start(f32[128,128]{1,0:T(8,128)S(1)} %add.24), channel_id=1, source_target_pairs={{0,8},{4,12},{8,0},{12,4},{16,24},{20,28},{24,16},{28,20},{1,9},{5... | collective-permute-start | bytes 196616 | tf_op jit(solution)/shard_map/ppermute | solution.py:299
  18.6 4.3 %collective-permute-start.3 = (f32[128,128]{1,0:T(8,128)S(1)}, f32[128,128]{1,0:T(8,128)S(1)}, u32[]{:S(2)}, u32[]{:S(2)}) collective-permute-start(f32[128,128]{1,0:T(8,128)S(1)} %add.22), channel_id=1, source_target_pairs={{0,8},{4,12},{8,0},{12,4},{16,24},{20,28},{24,16},{28,20},{1,9},{5... | collective-permute-start | bytes 196616 | tf_op jit(solution)/shard_map/ppermute | solution.py:299
  20.2 4.4 %collective-permute-start.1 = (f32[17,1024]{1,0:T(8,128)S(1)}, f32[17,1024]{1,0:T(8,128)S(1)}, u32[]{:S(2)}, u32[]{:S(2)}) collective-permute-start(f32[17,1024]{1,0:T(8,128)S(1)} %add.21.coef_ref), channel_id=1, source_target_pairs={{0,1},{1,0},{2,3},{3,2},{4,5},{5,4},{6,7},{7,6},{8,9},{9,8},{10,11... | collective-permute-start | bytes 208904 | tf_op jit(solution)/shard_map/ppermute | solution.py:299
  20.3 4.6 %collective-permute-start.7 = (f32[128,128]{1,0:T(8,128)S(1)}, f32[128,128]{1,0:T(8,128)S(1)}, u32[]{:S(2)}, u32[]{:S(2)}) collective-permute-start(f32[128,128]{1,0:T(8,128)S(1)} %get-tuple-element.42), channel_id=1, source_target_pairs={{0,4},{4,0},{8,12},{12,8},{16,20},{20,16},{24,28},{28,24},{1,5},{5... | collective-permute-start | bytes 196616 | tf_op jit(solution)/shard_map/ppermute | solution.py:299
  22.9 4.3 %collective-permute-start.6 = (f32[128,128]{1,0:T(8,128)S(1)}, f32[128,128]{1,0:T(8,128)S(1)}, u32[]{:S(2)}, u32[]{:S(2)}) collective-permute-start(f32[128,128]{1,0:T(8,128)S(1)} %get-tuple-element.44), channel_id=1, source_target_pairs={{0,4},{4,0},{8,12},{12,8},{16,20},{20,16},{24,28},{28,24},{1,5},{5... | collective-permute-start | bytes 196616 | tf_op jit(solution)/shard_map/ppermute | solution.py:299

commit v5 on v4

--- a/solution.py
+++ b/solution.py
@@ -23,6 +23,33 @@
     return jnp.dot(lhs, rhs, preferred_element_type=jnp.float32)
 
 
+def dot_t(lhs, rhs):
+    return lax.dot_general(lhs, rhs, (((1,), (1,)), ((), ())), preferred_element_type=jnp.float32)
+
+
+def chunk_rows(head_count, value_width):
+    rows = head_count * value_width
+    cut = rows // 2 // 16 * 16
+    return ((0, cut), (cut, rows))
+
+
+def store_rows(refs, chunks, head, state):
+    width = state.shape[0]
+    for ref, (start, stop) in zip(refs, chunks):
+        low, high = max(start, head * width), min(stop, (head + 1) * width)
+        if low < high:
+            ref[low - start : high - start, :] = state[low - head * width : high - head * width]
+
+
+def load_rows(refs, chunks, head, width):
+    parts = []
+    for ref, (start, stop) in zip(refs, chunks):
+        low, high = max(start, head * width), min(stop, (head + 1) * width)
+        if low < high:
+            parts.append(ref[low - start : high - start, :])
+    return parts[0] if len(parts) == 1 else jnp.concatenate(parts, axis=0)
+
+
 def shard_bit(level_idx):
     return jnp.bitwise_and(jnp.right_shift(lax.axis_index("seq"), level_idx), 1).astype(jnp.float32)
 
@@ -35,9 +62,10 @@
 
 def top_kernel(head_count, level_idx, row, *refs):
     query_hbm, key_hbm, value_hbm, grad_hbm, gates_hbm, states_hbm = refs[:6]
-    query, key, value, grad, gates, states, *out_refs, sems = refs[6:]
+    query, key, value, grad, gates, states, grad_t, *out_refs, sems = refs[6:]
     key_width = query.shape[1] // head_count
     value_width = grad.shape[1] // head_count
+    chunks = chunk_rows(head_count, value_width)
     first = [pltpu.make_async_copy(gates_hbm, gates, sems.at[0])]
     for head in range(head_count):
         for source, target, width in ((grad_hbm, grad, value_width), (query_hbm, query, key_width)):
@@ -52,10 +80,10 @@
     scale = shard_bit(level_idx) * level_weight(row)
     for head in range(head_count):
         first[2 * head + 1].wait()
-        grad_t = grad[:, head * value_width : (head + 1) * value_width].T
+        grad_t[head] = grad[:, head * value_width : (head + 1) * value_width].T
         first[2 * head + 2].wait()
         keys = slice(head * key_width, (head + 1) * key_width)
-        out_refs[head][...] = state_gradients([row], query[:, keys], grad_t, gates) * scale
+        store_rows(out_refs, chunks, head, state_gradients([row], query[:, keys], grad_t[head], gates) * scale)
     for copy in later:
         copy.wait()
 
@@ -72,10 +100,10 @@
 
 def local_kernel(
     local_levels, cross_levels, head_count,
-    query_ref, key_ref, value_ref, grad_ref, gates_ref, states_ref,
-    query_out, key_out, value_out, coef_out, *rest,
+    query_ref, key_ref, value_ref, grad_ref, gates_ref, grad_t,
+    key_out, value_out, coef_out, grad_weights_out, *rest,
 ):
-    *state_outs, key_t, grad_t, mix, sums, weights, grad_weights = rest
+    *state_outs, mix, sums, weights = rest
     tokens = query_ref.shape[0]
     key_width = query_ref.shape[1] // head_count
     value_width = value_ref.shape[1] // head_count
@@ -141,25 +169,23 @@
             chunks.append((s_start, s_start + size, level))
             s_start += size
         level_sums = {}
-        cross_sums = [None] * cross_levels
         for head in range(head_count):
             keys = slice(head * key_width, (head + 1) * key_width)
             vals = slice(head * value_width, (head + 1) * value_width)
-            q_cols = query_ref[t_slice, keys].T
-            g_cols = grad_ref[t_slice, vals].T
-            key_t[head, :, t_slice] = key_ref[t_slice, keys].T
-            grad_t[head, :, t_slice] = g_cols
+            q_rows = query_ref[t_slice, keys]
+            g_rows = grad_ref[t_slice, vals]
+            grad_weights = grad_weights_out.at[head, t_start // wide]
             for s_start, s_end, level in chunks:
                 s_slice = slice(s_start, s_end)
                 gate = gates_ref[level : level + 1, t_slice] * level_weight(level)
-                score = dot(key_ref[s_slice, keys], q_cols)
-                grad_score = dot(value_ref[s_slice, vals], g_cols)
+                score = dot_t(key_ref[s_slice, keys], q_rows)
+                grad_score = dot_t(value_ref[s_slice, vals], g_rows)
                 product = jnp.sum((score * grad_score).reshape(-1, SUBLANES, wide), axis=0)
                 level_sums[level] = level_sums[level] + product if level in level_sums else product
                 weights[s_slice, :] = (gate * score).astype(jnp.bfloat16)
                 grad_weights[s_slice, :] = (gate * grad_score).astype(jnp.bfloat16)
-            score = dot(key_ref[t_slice, keys], q_cols)
-            grad_score = dot(value_ref[t_slice, vals], g_cols)
+            score = dot_t(key_ref[t_slice, keys], q_rows)
+            grad_score = dot_t(value_ref[t_slice, vals], g_rows)
             product = score * grad_score
             gate = jnp.broadcast_to(gates_ref[near : near + 1, high] * level_weight(near), (block, block))
             tile = jnp.concatenate([mix[idx], gate], axis=1)
@@ -179,19 +205,8 @@
                     sums[k] = part
 
             s_all = slice(0, t_end)
-            query_total = dot(key_t[head, :, s_all], grad_weights[s_all, :])
-            stacked = states_ref[0, :cross_levels, head].reshape(cross_levels * key_width, value_width)
-            projected = dot(stacked, g_cols)
-            q_wide = q_cols.astype(jnp.float32)
-            for level_idx in range(cross_levels):
-                row = local_levels + level_idx
-                part = projected[level_idx * key_width : (level_idx + 1) * key_width]
-                query_total += (gates_ref[row : row + 1, t_slice] * shard_bit(level_idx)) * part
-                total = jnp.sum((q_wide * part).reshape(-1, SUBLANES, wide), axis=0)
-                cross_sums[level_idx] = total if head == 0 else cross_sums[level_idx] + total
-            query_out[t_slice, keys] = query_total.astype(jnp.bfloat16).T
-            key_part = dot(grad_weights[s_all, :], query_ref[t_slice, keys])
-            value_part = dot(weights[s_all, :], grad_ref[t_slice, vals])
+            key_part = dot(grad_weights[s_all, :], q_rows)
+            value_part = dot(weights[s_all, :], g_rows)
             key_out[t_slice, keys] = key_part[t_start:]
             value_out[t_slice, vals] = value_part[t_start:]
             if t_start:
@@ -209,16 +224,8 @@
         for part, where in ((three[0], low), (three[2], high)):
             for level, total in enumerate(diagonal_sums(part)):
                 coef_out[level : level + 1, where] = total * level_weight(level)
-        for level_idx, total in enumerate(cross_sums):
-            row = local_levels + level_idx
-            coef_out[row : row + 1, t_slice] = jnp.sum(total, axis=0, keepdims=True) * shard_bit(level_idx)
-
-    level_count = coef_out.shape[0]
-    if local_levels + cross_levels < level_count:
-        coef_out[local_levels + cross_levels :, :] = jnp.zeros(
-            (level_count - local_levels - cross_levels, tokens), jnp.float32
-        )
     rows = [local_levels + level_idx for level_idx in range(cross_levels - 1)]
+    chunks = chunk_rows(head_count, value_width)
     for head in range(head_count):
         if not rows:
             break
@@ -226,42 +233,85 @@
         stacked = state_gradients(rows, query_ref[:, keys], grad_t[head], gates_ref)
         for level_idx, row in enumerate(rows):
             part = stacked[level_idx * value_width : (level_idx + 1) * value_width]
-            state_outs[level_idx * head_count + head][...] = part * (shard_bit(level_idx) * level_weight(row))
-
-
-def apply_kernel(
-    head_count, key_ref, value_ref, key_local, value_local, coef_ref, coef_received, *refs,
+            refs = state_outs[level_idx * len(chunks) : (level_idx + 1) * len(chunks)]
+            store_rows(refs, chunks, head, part * (shard_bit(level_idx) * level_weight(row)))
+
+
+def query_kernel(
+    local_levels, cross_levels, head_count,
+    query_ref, key_ref, grad_ref, gates_ref, states_ref, grad_weights_ref, coef_ref, query_out, coef_out, key_t,
 ):
-    state_refs = refs[: 2 * head_count]
-    key_out, value_out, coef_out, key_total, value_total, coef_total, sems = refs[2 * head_count :]
+    tokens = query_ref.shape[0]
+    key_width = query_ref.shape[1] // head_count
+    value_width = grad_ref.shape[1] // head_count
+    wide = grad_weights_ref.shape[3]
+    coef_out[:local_levels, :] = coef_ref[:local_levels, :]
+    level_count = coef_out.shape[0]
+    if local_levels + cross_levels < level_count:
+        coef_out[local_levels + cross_levels :, :] = jnp.zeros(
+            (level_count - local_levels - cross_levels, tokens), jnp.float32
+        )
+    for t_start in range(0, tokens, wide):
+        t_end = t_start + wide
+        t_slice = slice(t_start, t_end)
+        cross_sums = [None] * cross_levels
+        for head in range(head_count):
+            keys = slice(head * key_width, (head + 1) * key_width)
+            vals = slice(head * value_width, (head + 1) * value_width)
+            key_t[head, :, t_slice] = key_ref[t_slice, keys].T
+            total = dot(key_t[head, :, :t_end], grad_weights_ref[head, t_start // wide, :t_end, :])
+            stacked = states_ref[0, :cross_levels, head].reshape(cross_levels * key_width, value_width)
+            projected = dot_t(stacked, grad_ref[t_slice, vals])
+            q_wide = query_ref[t_slice, keys].T.astype(jnp.float32)
+            for level_idx in range(cross_levels):
+                row = local_levels + level_idx
+                part = projected[level_idx * key_width : (level_idx + 1) * key_width]
+                total += (gates_ref[row : row + 1, t_slice] * shard_bit(level_idx)) * part
+                cross = jnp.sum((q_wide * part).reshape(-1, SUBLANES, wide), axis=0)
+                cross_sums[level_idx] = cross if head == 0 else cross_sums[level_idx] + cross
+            query_out[t_slice, keys] = total.astype(jnp.bfloat16).T
+        for level_idx, cross in enumerate(cross_sums):
+            row = local_levels + level_idx
+            coef_out[row : row + 1, t_slice] = jnp.sum(cross, axis=0, keepdims=True) * shard_bit(level_idx)
+
+
+def apply_kernel(head_count, heads, chunk_count, last, *refs):
+    key_ref, value_ref, key_local, value_local = refs[:4]
+    state_refs = refs[4 : 4 + chunk_count]
+    received_refs = refs[4 + chunk_count : 4 + 2 * chunk_count]
     tokens = key_ref.shape[0]
     key_width = key_ref.shape[1] // head_count
     value_width = value_ref.shape[1] // head_count
+    chunks = chunk_rows(head_count, value_width)[:chunk_count]
     wide = 2 * LANES
-    coef_total[...] = coef_ref[...] + coef_received[...]
-    copies = [pltpu.make_async_copy(coef_total, coef_out, sems.at[0])]
-    copies[0].start()
-    states = [
-        (state_refs[head][...] + state_refs[head_count + head][...]).astype(jnp.bfloat16) for head in range(head_count)
-    ]
-    flipped = [state.T for state in states]
-    for start in range(0, tokens, wide):
-        part = slice(start, start + wide)
-        for head in range(head_count):
-            keys = slice(head * key_width, (head + 1) * key_width)
-            vals = slice(head * value_width, (head + 1) * value_width)
-            key_total[part, keys] = (key_local[part, keys] + dot(value_ref[part, vals], states[head])).astype(
+    copies = []
+    if last:
+        coef_ref, coef_received = refs[-11:-9]
+        key_out, value_out, coef_out, key_total, value_total, coef_total, sems = refs[-7:]
+        coef_total[...] = coef_ref[...] + coef_received[...]
+        copies.append(pltpu.make_async_copy(coef_total, coef_out, sems.at[0]))
+        copies[0].start()
+    else:
+        query_ref = refs[4 + 2 * chunk_count]
+        query_out, key_out, value_out, key_total, value_total, sems = refs[-6:]
+        copies.append(pltpu.make_async_copy(query_ref, query_out, sems.at[0]))
+        copies[0].start()
+    for place, head in enumerate(heads):
+        keys = slice(head * key_width, (head + 1) * key_width)
+        vals = slice(head * value_width, (head + 1) * value_width)
+        state = load_rows(state_refs, chunks, head, value_width) + load_rows(received_refs, chunks, head, value_width)
+        state = state.astype(jnp.bfloat16)
+        flipped = state.T
+        for start in range(0, tokens, wide):
+            part = slice(start, start + wide)
+            key_total[place, part, :] = (key_local[part, keys] + dot(value_ref[part, vals], state)).astype(jnp.bfloat16)
+            value_total[place, part, :] = (value_local[part, vals] + dot(key_ref[part, keys], flipped)).astype(
                 jnp.bfloat16
             )
-            value_total[part, vals] = (value_local[part, vals] + dot(key_ref[part, keys], flipped[head])).astype(
-                jnp.bfloat16
-            )
-        for source, target in ((key_total, key_out), (value_total, value_out)):
-            copy = pltpu.make_async_copy(
-                source.at[start : start + wide, :], target.at[start : start + wide, :], sems.at[len(copies)]
-            )
-            copy.start()
-            copies.append(copy)
+            for source, target, cols in ((key_total, key_out, keys), (value_total, value_out, vals)):
+                copy = pltpu.make_async_copy(source.at[place, part, :], target.at[part, cols], sems.at[len(copies)])
+                copy.start()
+                copies.append(copy)
     for copy in copies:
         copy.wait()
 
@@ -279,58 +329,75 @@
     wide = 2 * block
     vmem = pl.BlockSpec(memory_space=pltpu.VMEM)
     hbm = pl.BlockSpec(memory_space=pltpu.HBM)
-    state_shape = jax.ShapeDtypeStruct((value_width, key_width), jnp.float32)
-    heads = range(head_count)
+    chunks = chunk_rows(head_count, value_width)
+    parts = range(len(chunks))
+    state_shapes = [jax.ShapeDtypeStruct((stop - start, key_width), jnp.float32) for start, stop in chunks]
 
     inputs = (queries, key_vectors, values, out_grad, level_coef, saved_states)
     count = len(inputs)
     results = pl.pallas_call(
         functools.partial(top_kernel, head_count, bit_count - 1, local_levels + bit_count - 1),
         in_specs=[hbm] * 6,
-        out_specs=[vmem] * (count + head_count),
-        out_shape=[jax.ShapeDtypeStruct(x.shape, x.dtype) for x in inputs] + [state_shape] * head_count,
+        out_specs=[vmem] * (count + 1 + len(chunks)),
+        out_shape=[jax.ShapeDtypeStruct(x.shape, x.dtype) for x in inputs]
+        + [jax.ShapeDtypeStruct((head_count, value_width, tokens), jnp.bfloat16)]
+        + state_shapes,
         scratch_shapes=[pltpu.SemaphoreType.DMA((2 * head_count + 4,))],
         compiler_params=pltpu.CompilerParams(vmem_limit_bytes=8 * MIB),
     )(*[pltpu.with_memory_space_constraint(x, pltpu.HBM) for x in inputs])
-    inputs, tops = results[:count], results[count:]
+    inputs, grad_t, tops = results[:count], results[count], results[count + 1 :]
 
     def exchange(value, axis, bit_pos):
         pairs = [(p, p ^ 2**bit_pos) for p in range(lax.axis_size(axis))]
         return lax.ppermute(value, axis, pairs)
 
-    received = [exchange(tops[head], "seq", bit_count - 1) for head in heads]
+    received = [exchange(tops[part], "seq", bit_count - 1) for part in parts]
 
     flops = 8 * head_count * tokens * tokens * key_width
+    blocks = tokens // wide
     local_call = pl.pallas_call(
         functools.partial(local_kernel, local_levels, bit_count, head_count),
         in_specs=[vmem] * 6,
-        out_specs=[vmem] * (4 + (bit_count - 1) * head_count),
+        out_specs=[vmem] * (4 + (bit_count - 1) * len(chunks)),
         out_shape=[
-            jax.ShapeDtypeStruct(queries.shape, jnp.bfloat16),
             jax.ShapeDtypeStruct(queries.shape, jnp.float32),
             jax.ShapeDtypeStruct(values.shape, jnp.float32),
             jax.ShapeDtypeStruct(level_coef.shape, jnp.float32),
+            jax.ShapeDtypeStruct((head_count, blocks, tokens, wide), jnp.bfloat16),
         ]
-        + [state_shape] * ((bit_count - 1) * head_count),
+        + state_shapes * (bit_count - 1),
         scratch_shapes=[
-            pltpu.VMEM((head_count, key_width, tokens), jnp.bfloat16),
-            pltpu.VMEM((head_count, value_width, tokens), jnp.bfloat16),
             pltpu.VMEM((tokens // block, block, block), jnp.float32),
             pltpu.VMEM((3, block, block), jnp.float32),
             pltpu.VMEM((tokens, wide), jnp.bfloat16),
-            pltpu.VMEM((tokens, wide), jnp.bfloat16),
         ],
-        compiler_params=pltpu.CompilerParams(vmem_limit_bytes=24 * MIB),
+        compiler_params=pltpu.CompilerParams(vmem_limit_bytes=20 * MIB),
         cost_estimate=pl.CostEstimate(flops=flops, bytes_accessed=8 * MIB, transcendentals=0),
     )
-    query_grad, key_local, value_local, coef_grad, *contrib = local_call(*inputs)
-
-    grad_state = [jnp.zeros(state_shape.shape, jnp.float32) for _ in heads]
+    query_call = pl.pallas_call(
+        functools.partial(query_kernel, local_levels, bit_count, head_count),
+        in_specs=[vmem] * 7,
+        out_specs=[vmem] * 2,
+        out_shape=[
+            jax.ShapeDtypeStruct(queries.shape, jnp.bfloat16),
+            jax.ShapeDtypeStruct(level_coef.shape, jnp.float32),
+        ],
+        scratch_shapes=[pltpu.VMEM((head_count, key_width, tokens), jnp.bfloat16)],
+        compiler_params=pltpu.CompilerParams(vmem_limit_bytes=12 * MIB),
+        cost_estimate=pl.CostEstimate(flops=flops // 4, bytes_accessed=6 * MIB, transcendentals=0),
+    )
+    query_in, key_in, value_in, grad_in, gates_in, states_in = inputs
+    key_local, value_local, coef_grad, grad_weights, *contrib = local_call(
+        query_in, key_in, value_in, grad_in, gates_in, grad_t
+    )
+    query_grad, coef_grad = query_call(query_in, key_in, grad_in, gates_in, states_in, grad_weights, coef_grad)
+
+    grad_state = [jnp.zeros(shape.shape, jnp.float32) for shape in state_shapes]
     for level_idx in reversed(range(bit_count - 1)):
-        for head in heads:
-            grad_state[head] = grad_state[head] + received[head]
-            own = contrib[level_idx * head_count + head]
-            received[head] = exchange(grad_state[head] + own, "seq", level_idx)
+        for part in parts:
+            grad_state[part] = grad_state[part] + received[part]
+            own = contrib[level_idx * len(chunks) + part]
+            received[part] = exchange(grad_state[part] + own, "seq", level_idx)
 
     head_bits = lax.axis_size("head").bit_length() - 1
     coef_received = jnp.zeros_like(coef_grad)
@@ -339,24 +406,38 @@
             coef_grad = coef_grad + coef_received
         coef_received = exchange(coef_grad, "head", bit_pos)
 
-    pieces = 2 * (tokens // wide) + 1
-    key_grad, value_grad, coef_grad = pl.pallas_call(
-        functools.partial(apply_kernel, head_count),
-        in_specs=[vmem] * (6 + 2 * head_count),
-        out_specs=[hbm] * 3,
-        out_shape=[
-            jax.ShapeDtypeStruct(queries.shape, jnp.bfloat16),
-            jax.ShapeDtypeStruct(values.shape, jnp.bfloat16),
-            jax.ShapeDtypeStruct(level_coef.shape, jnp.float32),
-        ],
-        scratch_shapes=[
-            pltpu.VMEM(queries.shape, jnp.bfloat16),
-            pltpu.VMEM(values.shape, jnp.bfloat16),
-            pltpu.VMEM(level_coef.shape, jnp.float32),
-            pltpu.SemaphoreType.DMA((pieces,)),
-        ],
-        compiler_params=pltpu.CompilerParams(vmem_limit_bytes=12 * MIB),
-    )(inputs[1], inputs[2], key_local, value_local, coef_grad, coef_received, *grad_state, *received)
+    shapes = [
+        jax.ShapeDtypeStruct(queries.shape, jnp.bfloat16),
+        jax.ShapeDtypeStruct(values.shape, jnp.bfloat16),
+    ]
+    coef_shape = jax.ShapeDtypeStruct(level_coef.shape, jnp.float32)
+    early = [head for head in range(head_count) if (head + 1) * value_width <= chunks[0][1]]
+    late = [head for head in range(head_count) if head not in early]
+    common = (inputs[1], inputs[2], key_local, value_local)
+
+    def apply_call(which, chunk_count, last):
+        pieces = 2 * len(which) * (tokens // wide) + 1
+        in_count = 4 + 2 * chunk_count + 1 + last
+        return pl.pallas_call(
+            functools.partial(apply_kernel, head_count, which, chunk_count, last),
+            in_specs=[vmem] * in_count + [hbm] * (2 * last),
+            out_specs=[hbm] * 3,
+            out_shape=shapes + [coef_shape] if last else shapes[:1] + shapes,
+            input_output_aliases={in_count: 0, in_count + 1: 1} if last else {},
+            scratch_shapes=[
+                pltpu.VMEM((len(which), tokens, key_width), jnp.bfloat16),
+                pltpu.VMEM((len(which), tokens, value_width), jnp.bfloat16),
+            ]
+            + [pltpu.VMEM(level_coef.shape, jnp.float32)] * last
+            + [pltpu.SemaphoreType.DMA((pieces,))],
+            compiler_params=pltpu.CompilerParams(vmem_limit_bytes=12 * MIB),
+        )
+
+    query_grad, *outs = apply_call(early, 1, False)(*common, grad_state[0], received[0], query_grad)
+    outs = [pltpu.with_memory_space_constraint(x, pltpu.HBM) for x in outs]
+    key_grad, value_grad, coef_grad = apply_call(late, 2, True)(
+        *common, *grad_state, *received, coef_grad, coef_received, *outs
+    )
     return (query_grad, key_grad, value_grad, coef_grad)
 
 

time: 28.7 us -> 27.7 us (0.965)
  waiting for transfers between devices: 7.1 us -> 6.07 us
    ppermute x8, waiting for transfers between devices: 7.1 us -> 6.07 us  [exchange(): return lax.ppermute(value, axis, pairs)]
    pallas_call x2 -> x4, Pallas kernels: 6.5 us -> 6.46 us  [the longest x1 3.39 us: shards(): local_call(query_in, key_in, value_in, grad_in, gates_in, grad_t)]
  transfers between devices with their start and end apart: 8 -> 8, of which waited for: 4 -> 4; matrix products, arithmetic and copies ran while one was open for 0% -> 0% of each run, Pallas kernels for 18% -> 20%
where the time goes in v5:
time: 27.7 us; the launch traced here: 27.5 us
  starting transfers between devices  12.5 us (45%)
  Pallas kernels  8.24 us (30%)
  waiting for transfers between devices  6.07 us (22%)
  between operations  0.71 us (3%)
    ppermute x8, starting transfers between devices, exchange(): return lax.ppermute(value, axis, pairs)  12.5 us
    ppermute x8, waiting for transfers between devices, exchange(): return lax.ppermute(value, axis, pairs)  6.07 us
    pallas_call x1, Pallas kernels, shards(): local_call(query_in, key_in, value_in, grad_in, gates_in, grad_t)  3.39 us
    pallas_call x1, Pallas kernels, shards(): pl.pallas_call(functools.partial(top_kernel, head_count, bit_count - 1, l...  1.77 us
    pallas_call x1, Pallas kernels, shards(): apply_call(early, 1, False)(*common, grad_state[0], received[0], query_grad)  1.03 us
    pallas_call x1, Pallas kernels, shards(): apply_call(late, 2, True)  1.03 us
    pallas_call x1, Pallas kernels, shards(): query_call(query_in, key_in, grad_in, gates_in, states_in, grad_weights,...  1.01 us
  transfers between devices with their start and end apart: 8, of which 4 were waited for; matrix products, arithmetic and copies ran while one was open for 0% of the time, Pallas kernels for 20%

profile of v5, /device:TPU:0, one launch (start us, length us, event | category | flops | bytes accessed | tf_op | source)
XLA Modules:
  0.0 27.5 jit_solution(4216933300517390337)
XLA Ops:
  0.6 1.8 %shard_map.93 = (bf16[1024,256]{1,0:T(8,128)(2,1)S(1)}, bf16[1024,256]{1,0:T(8,128)(2,1)S(1)}, bf16[1024,256]{1,0:T(8,128)(2,1)S(1)}, bf16[1024,256]{1,0:T(8,128...) custom-call(bf16[1024,256]{1,0:T(8,128)(2,1)} %refs_0_.1, ...), custom_call_target="tpu_custom_call" | custom-call | tf_op jit(solution)/shard_map/pallas_call | solution.py:338
  2.4 4.1 %collective-permute-start = (f32[128,128]{1,0:T(8,128)S(1)}, f32[128,128]{1,0:T(8,128)S(1)}, u32[]{:S(2)}, u32[]{:S(2)}) collective-permute-start(f32[128,128]{1,0:T(8,128)S(1)} %get-tuple-element.37), channel_id=1, source_target_pairs={{0,16},{4,20},{8,24},{12,28},{16,0},{20,4},{24,8},{28,12},{1,17},{... | collective-permute-start | bytes 196616 | tf_op jit(solution)/shard_map/ppermute | solution.py:352
  6.5 3.4 %shard_map.94 = (f32[1024,256]{1,0:T(8,128)S(1)}, f32[1024,256]{1,0:T(8,128)S(1)}, f32[17,1024]{1,0:T(8,128)S(1)}, bf16[2,4,1024,256]{3,2,1,0:T(8,128)(2,1)S(1)}...) custom-call(bf16[1024,256]{1,0:T(8,128)(2,1)S(1)} %get-tuple-element.31.quer, ...), custom_call_target="tpu_custom_call" | custom-call | flops 2147483648 | bytes 8388608 | tf_op jit(solution)/shard_map/pallas_call | solution.py:390
  9.9 1.0 %shard_map.95 = (bf16[1024,256]{1,0:T(8,128)(2,1)S(1)}, f32[17,1024]{1,0:T(8,128)S(1)}) custom-call(bf16[1024,256]{1,0:T(8,128)(2,1)S(1)} %get-tuple-element.31.query_ref, bf16[1024,256]{1,0:T(8,128)(2,1)S(1)} %get-tuple-element.29.key_ref.refs_0_, bf16[1024,256]{1,0:T(8,128)(2,1)S(1)} %get-tuple-element.32.grad_ref, ...), custom_call_target="tpu_custom_call" | custom-call | flops 536870912 | bytes 6291456 | tf_op jit(solution)/shard_map/pallas_call | solution.py:393
  11.0 1.6 %collective-permute-start.6 = (f32[17,1024]{1,0:T(8,128)S(1)}, f32[17,1024]{1,0:T(8,128)S(1)}, u32[]{:S(2)}, u32[]{:S(2)}) collective-permute-start(f32[17,1024]{1,0:T(8,128)S(1)} %get-tuple-element.48), channel_id=1, source_target_pairs={{0,2},{1,3},{2,0},{3,1},{4,6},{5,7},{6,4},{7,5},{8,10},{9,11},{10,... | collective-permute-start | bytes 208904 | tf_op jit(solution)/shard_map/ppermute | solution.py:352
  12.5 0.3 %collective-permute-start.3 = (f32[128,128]{1,0:T(8,128)S(1)}, f32[128,128]{1,0:T(8,128)S(1)}, u32[]{:S(2)}, u32[]{:S(2)}) collective-permute-start(f32[128,128]{1,0:T(8,128)S(1)} %get-tuple-element.45), channel_id=1, source_target_pairs={{0,16},{4,20},{8,24},{12,28},{16,0},{20,4},{24,8},{28,12},{1,17},{... | collective-permute-start | bytes 196616 | tf_op jit(solution)/shard_map/ppermute | solution.py:352
  12.9 0.0 collective-permute-done
  12.9 1.6 %collective-permute-start.1 = (f32[128,128]{1,0:T(8,128)S(1)}, f32[128,128]{1,0:T(8,128)S(1)}, u32[]{:S(2)}, u32[]{:S(2)}) collective-permute-start(f32[128,128]{1,0:T(8,128)S(1)} %add.21), channel_id=1, source_target_pairs={{0,8},{4,12},{8,0},{12,4},{16,24},{20,28},{24,16},{28,20},{1,9},{5... | collective-permute-start | bytes 196616 | tf_op jit(solution)/shard_map/ppermute | solution.py:352
  14.5 3.3 %collective-permute-done.3 = f32[128,128]{1,0:T(8,128)S(1)} collective-permute-done((f32[128,128]{1,0:T(8,128)S(1)}, f32[128,128]{1,0:T(8,128)S(1)}, u32[]{:S(2)}, u32[]{:S(2)}) %collective-permute-start.3) | collective-permute-done | bytes 65568 | tf_op jit(solution)/shard_map/ppermute | solution.py:352
  17.8 1.5 %collective-permute-start.4 = (f32[128,128]{1,0:T(8,128)S(1)}, f32[128,128]{1,0:T(8,128)S(1)}, u32[]{:S(2)}, u32[]{:S(2)}) collective-permute-start(f32[128,128]{1,0:T(8,128)S(1)} %add.24), channel_id=1, source_target_pairs={{0,8},{4,12},{8,0},{12,4},{16,24},{20,28},{24,16},{28,20},{1,9},{5... | collective-permute-start | bytes 196616 | tf_op jit(solution)/shard_map/ppermute | solution.py:352
  19.3 0.0 collective-permute-done.6
  19.4 0.1 collective-permute-start.7
  19.4 0.0 collective-permute-done.1
  19.5 1.6 %collective-permute-start.2 = (f32[128,128]{1,0:T(8,128)S(1)}, f32[128,128]{1,0:T(8,128)S(1)}, u32[]{:S(2)}, u32[]{:S(2)}) collective-permute-start(f32[128,128]{1,0:T(8,128)S(1)} %get-tuple-element.56), channel_id=1, source_target_pairs={{0,4},{4,0},{8,12},{12,8},{16,20},{20,16},{24,28},{28,24},{1,5},{5... | collective-permute-start | bytes 196616 | tf_op jit(solution)/shard_map/ppermute | solution.py:352
  21.1 1.1 %collective-permute-done.4 = f32[128,128]{1,0:T(8,128)S(1)} collective-permute-done((f32[128,128]{1,0:T(8,128)S(1)}, f32[128,128]{1,0:T(8,128)S(1)}, u32[]{:S(2)}, u32[]{:S(2)}) %collective-permute-start.4) | collective-permute-done | bytes 65568 | tf_op jit(solution)/shard_map/ppermute | solution.py:352
  22.2 1.6 %collective-permute-start.5 = (f32[128,128]{1,0:T(8,128)S(1)}, f32[128,128]{1,0:T(8,128)S(1)}, u32[]{:S(2)}, u32[]{:S(2)}) collective-permute-start(f32[128,128]{1,0:T(8,128)S(1)} %get-tuple-element.54), channel_id=1, source_target_pairs={{0,4},{4,0},{8,12},{12,8},{16,20},{20,16},{24,28},{28,24},{1,5},{5... | collective-permute-start | bytes 196616 | tf_op jit(solution)/shard_map/ppermute | solution.py:352
  23.7 0.3 %collective-permute-done.2.refs_5_.refs_6_ = f32[128,128]{1,0:T(8,128)S(1)} collective-permute-done((f32[128,128]{1,0:T(8,128)S(1)}, f32[128,128]{1,0:T(8,128)S(1)}, u32[]{:S(2)}, u32[]{:S(2)}) %collective-permute-start.2) | collective-permute-done | bytes 65568 | tf_op jit(solution)/shard_map/ppermute | solution.py:352
  24.1 1.0 %shard_map.96 = (bf16[1024,256]{1,0:T(8,128)(2,1)}, bf16[1024,256]{1,0:T(8,128)(2,1)}, bf16[1024,256]{1,0:T(8,128)(2,1)}) custom-call(bf16[1024,256]{1,0:T(8,128)(2,1)S(1)} %get-tuple-element.29.key_ref.refs_0_, bf16[1024,256]{1,0:T(8,128)(2,1)S(1)} %get-tuple-element.30.value_ref.refs_1_, f32[1024,256]{1,0:T(8,128)S(1)} %get-tuple-element.35.refs_2_, ...), custom_call_target="tpu_custom_call" | custom-call | tf_op jit(solution)/shard_map/pallas_call | solution.py:436
  25.1 0.0 collective-permute-done.7.refs_9_
  25.1 1.4 %collective-permute-done.5.refs_7_ = f32[128,128]{1,0:T(8,128)S(1)} collective-permute-done((f32[128,128]{1,0:T(8,128)S(1)}, f32[128,128]{1,0:T(8,128)S(1)}, u32[]{:S(2)}, u32[]{:S(2)}) %collective-permute-start.5) | collective-permute-done | bytes 65568 | tf_op jit(solution)/shard_map/ppermute | solution.py:352
  26.5 1.0 %shard_map.97 = (bf16[1024,256]{1,0:T(8,128)(2,1)}, bf16[1024,256]{1,0:T(8,128)(2,1)}, f32[17,1024]{1,0:T(8,128)}) custom-call(bf16[1024,256]{1,0:T(8,128)(2,1)S(1)} %get-tuple-element.29.key_ref.refs_0_, bf16[1024,256]{1,0:T(8,128)(2,1)S(1)} %get-tuple-element.30.value_ref.refs_1_, ...), custom_call_target="tpu_custom_call", output_to_operand_aliasing={{0}: (10, {}), {1}: (11, {})} | custom-call | tf_op jit(solution)/shard_map/pallas_call | solution.py:438
  (5 shorter events, 0.1 us)
Async XLA Ops:
  2.4 10.5 %collective-permute-start = (f32[128,128]{1,0:T(8,128)S(1)}, f32[128,128]{1,0:T(8,128)S(1)}, u32[]{:S(2)}, u32[]{:S(2)}) collective-permute-start(f32[128,128]{1,0:T(8,128)S(1)} %get-tuple-element.37), channel_id=1, source_target_pairs={{0,16},{4,20},{8,24},{12,28},{16,0},{20,4},{24,8},{28,12},{1,17},{... | collective-permute-start | bytes 196616 | tf_op jit(solution)/shard_map/ppermute | solution.py:352
  11.0 8.4 %collective-permute-start.6 = (f32[17,1024]{1,0:T(8,128)S(1)}, f32[17,1024]{1,0:T(8,128)S(1)}, u32[]{:S(2)}, u32[]{:S(2)}) collective-permute-start(f32[17,1024]{1,0:T(8,128)S(1)} %get-tuple-element.48), channel_id=1, source_target_pairs={{0,2},{1,3},{2,0},{3,1},{4,6},{5,7},{6,4},{7,5},{8,10},{9,11},{10,... | collective-permute-start | bytes 208904 | tf_op jit(solution)/shard_map/ppermute | solution.py:352
  12.5 5.3 %collective-permute-start.3 = (f32[128,128]{1,0:T(8,128)S(1)}, f32[128,128]{1,0:T(8,128)S(1)}, u32[]{:S(2)}, u32[]{:S(2)}) collective-permute-start(f32[128,128]{1,0:T(8,128)S(1)} %get-tuple-element.45), channel_id=1, source_target_pairs={{0,16},{4,20},{8,24},{12,28},{16,0},{20,4},{24,8},{28,12},{1,17},{... | collective-permute-start | bytes 196616 | tf_op jit(solution)/shard_map/ppermute | solution.py:352
  12.9 6.6 %collective-permute-start.1 = (f32[128,128]{1,0:T(8,128)S(1)}, f32[128,128]{1,0:T(8,128)S(1)}, u32[]{:S(2)}, u32[]{:S(2)}) collective-permute-start(f32[128,128]{1,0:T(8,128)S(1)} %add.21), channel_id=1, source_target_pairs={{0,8},{4,12},{8,0},{12,4},{16,24},{20,28},{24,16},{28,20},{1,9},{5... | collective-permute-start | bytes 196616 | tf_op jit(solution)/shard_map/ppermute | solution.py:352
  17.8 4.3 %collective-permute-start.4 = (f32[128,128]{1,0:T(8,128)S(1)}, f32[128,128]{1,0:T(8,128)S(1)}, u32[]{:S(2)}, u32[]{:S(2)}) collective-permute-start(f32[128,128]{1,0:T(8,128)S(1)} %add.24), channel_id=1, source_target_pairs={{0,8},{4,12},{8,0},{12,4},{16,24},{20,28},{24,16},{28,20},{1,9},{5... | collective-permute-start | bytes 196616 | tf_op jit(solution)/shard_map/ppermute | solution.py:352
  19.4 5.8 %collective-permute-start.7 = (f32[17,1024]{1,0:T(8,128)S(1)}, f32[17,1024]{1,0:T(8,128)S(1)}, u32[]{:S(2)}, u32[]{:S(2)}) collective-permute-start(f32[17,1024]{1,0:T(8,128)S(1)} %add.27.refs_8_), channel_id=1, source_target_pairs={{0,1},{1,0},{2,3},{3,2},{4,5},{5,4},{6,7},{7,6},{8,9},{9,8},{10,11... | collective-permute-start | bytes 208904 | tf_op jit(solution)/shard_map/ppermute | solution.py:352
  19.5 4.6 %collective-permute-start.2 = (f32[128,128]{1,0:T(8,128)S(1)}, f32[128,128]{1,0:T(8,128)S(1)}, u32[]{:S(2)}, u32[]{:S(2)}) collective-permute-start(f32[128,128]{1,0:T(8,128)S(1)} %get-tuple-element.56), channel_id=1, source_target_pairs={{0,4},{4,0},{8,12},{12,8},{16,20},{20,16},{24,28},{28,24},{1,5},{5... | collective-permute-start | bytes 196616 | tf_op jit(solution)/shard_map/ppermute | solution.py:352
  22.2 4.3 %collective-permute-start.5 = (f32[128,128]{1,0:T(8,128)S(1)}, f32[128,128]{1,0:T(8,128)S(1)}, u32[]{:S(2)}, u32[]{:S(2)}) collective-permute-start(f32[128,128]{1,0:T(8,128)S(1)} %get-tuple-element.54), channel_id=1, source_target_pairs={{0,4},{4,0},{8,12},{12,8},{16,20},{20,16},{24,28},{28,24},{1,5},{5... | collective-permute-start | bytes 196616 | tf_op jit(solution)/shard_map/ppermute | solution.py:352

commit v6 on v5

--- a/solution.py
+++ b/solution.py
@@ -9,6 +9,7 @@
 
 
 LANES = 128
+TOP_PIECES = 2
 SUBLANES = 8
 MIB = 2**20
 
@@ -66,25 +67,30 @@
     key_width = query.shape[1] // head_count
     value_width = grad.shape[1] // head_count
     chunks = chunk_rows(head_count, value_width)
-    first = [pltpu.make_async_copy(gates_hbm, gates, sems.at[0])]
-    for head in range(head_count):
-        for source, target, width in ((grad_hbm, grad, value_width), (query_hbm, query, key_width)):
-            cols = slice(head * width, (head + 1) * width)
-            first.append(pltpu.make_async_copy(source.at[:, cols], target.at[:, cols], sems.at[len(first)]))
-    later = []
-    for source, target in ((key_hbm, key), (value_hbm, value), (states_hbm, states)):
-        later.append(pltpu.make_async_copy(source, target, sems.at[len(first) + len(later)]))
-    for copy in first + later:
+    size = query.shape[0] // TOP_PIECES
+    spans = [slice(part * size, (part + 1) * size) for part in range(TOP_PIECES)]
+    levels = slice(0, level_idx + 1)
+    pairs = [(gates_hbm, gates)]
+    for span in spans:
+        pairs += [(grad_hbm.at[span, :], grad.at[span, :]), (query_hbm.at[span, :], query.at[span, :])]
+    pairs += [(key_hbm, key), (value_hbm, value), (states_hbm.at[:, levels], states.at[:, levels])]
+    copies = [pltpu.make_async_copy(source, target, sems.at[k]) for k, (source, target) in enumerate(pairs)]
+    for copy in copies:
         copy.start()
-    first[0].wait()
+    copies[0].wait()
+    totals = [0.0] * head_count
+    for part, span in enumerate(spans):
+        copies[1 + 2 * part].wait()
+        copies[2 + 2 * part].wait()
+        for head in range(head_count):
+            keys = slice(head * key_width, (head + 1) * key_width)
+            flipped = grad[span, head * value_width : (head + 1) * value_width].T
+            grad_t[head, :, span] = flipped
+            totals[head] += state_gradients([row], query[span, keys], flipped, gates.at[:, span])
     scale = shard_bit(level_idx) * level_weight(row)
-    for head in range(head_count):
-        first[2 * head + 1].wait()
-        grad_t[head] = grad[:, head * value_width : (head + 1) * value_width].T
-        first[2 * head + 2].wait()
-        keys = slice(head * key_width, (head + 1) * key_width)
-        store_rows(out_refs, chunks, head, state_gradients([row], query[:, keys], grad_t[head], gates) * scale)
-    for copy in later:
+    for head, total in enumerate(totals):
+        store_rows(out_refs, chunks, head, total * scale)
+    for copy in copies[1 + 2 * len(spans) :]:
         copy.wait()
 
 
@@ -301,11 +307,10 @@
         vals = slice(head * value_width, (head + 1) * value_width)
         state = load_rows(state_refs, chunks, head, value_width) + load_rows(received_refs, chunks, head, value_width)
         state = state.astype(jnp.bfloat16)
-        flipped = state.T
         for start in range(0, tokens, wide):
             part = slice(start, start + wide)
             key_total[place, part, :] = (key_local[part, keys] + dot(value_ref[part, vals], state)).astype(jnp.bfloat16)
-            value_total[place, part, :] = (value_local[part, vals] + dot(key_ref[part, keys], flipped)).astype(
+            value_total[place, part, :] = (value_local[part, vals] + dot_t(key_ref[part, keys], state)).astype(
                 jnp.bfloat16
             )
             for source, target, cols in ((key_total, key_out, keys), (value_total, value_out, vals)):
@@ -342,7 +347,7 @@
         out_shape=[jax.ShapeDtypeStruct(x.shape, x.dtype) for x in inputs]
         + [jax.ShapeDtypeStruct((head_count, value_width, tokens), jnp.bfloat16)]
         + state_shapes,
-        scratch_shapes=[pltpu.SemaphoreType.DMA((2 * head_count + 4,))],
+        scratch_shapes=[pltpu.SemaphoreType.DMA((2 * TOP_PIECES + 4,))],
         compiler_params=pltpu.CompilerParams(vmem_limit_bytes=8 * MIB),
     )(*[pltpu.with_memory_space_constraint(x, pltpu.HBM) for x in inputs])
     inputs, grad_t, tops = results[:count], results[count], results[count + 1 :]

time: 27.7 us -> 27.6 us (level)
  no operation moved by 1% of the time
where the time goes in v6:
time: 27.6 us; the launch traced here: 27.4 us
  starting transfers between devices  12.4 us (45%)
  Pallas kernels  8.16 us (30%)
  waiting for transfers between devices  6.05 us (22%)
  between operations  0.71 us (3%)
    ppermute x8, starting transfers between devices, exchange(): return lax.ppermute(value, axis, pairs)  12.4 us
    ppermute x8, waiting for transfers between devices, exchange(): return lax.ppermute(value, axis, pairs)  6.05 us
    pallas_call x1, Pallas kernels, shards(): local_call(query_in, key_in, value_in, grad_in, gates_in, grad_t)  3.39 us
    pallas_call x1, Pallas kernels, shards(): pl.pallas_call(functools.partial(top_kernel, head_count, bit_count - 1, l...  1.68 us
    pallas_call x1, Pallas kernels, shards(): apply_call(late, 2, True)  1.03 us
    pallas_call x1, Pallas kernels, shards(): apply_call(early, 1, False)(*common, grad_state[0], received[0], query_grad)  1.03 us
    pallas_call x1, Pallas kernels, shards(): query_call(query_in, key_in, grad_in, gates_in, states_in, grad_weights,...  1.02 us
  transfers between devices with their start and end apart: 8, of which 4 were waited for; matrix products, arithmetic and copies ran while one was open for 0% of the time, Pallas kernels for 20%

profile of v6, /device:TPU:0, one launch (start us, length us, event | category | flops | bytes accessed | tf_op | source)
XLA Modules:
  0.0 27.4 jit_solution(15174285150262633841)
XLA Ops:
  0.6 1.7 %shard_map.93 = (bf16[1024,256]{1,0:T(8,128)(2,1)S(1)}, bf16[1024,256]{1,0:T(8,128)(2,1)S(1)}, bf16[1024,256]{1,0:T(8,128)(2,1)S(1)}, bf16[1024,256]{1,0:T(8,128...) custom-call(bf16[1024,256]{1,0:T(8,128)(2,1)} %refs_0_.1, ...), custom_call_target="tpu_custom_call" | custom-call | tf_op jit(solution)/shard_map/pallas_call | solution.py:343
  2.3 4.1 %collective-permute-start = (f32[128,128]{1,0:T(8,128)S(1)}, f32[128,128]{1,0:T(8,128)S(1)}, u32[]{:S(2)}, u32[]{:S(2)}) collective-permute-start(f32[128,128]{1,0:T(8,128)S(1)} %get-tuple-element.37), channel_id=1, source_target_pairs={{0,16},{4,20},{8,24},{12,28},{16,0},{20,4},{24,8},{28,12},{1,17},{... | collective-permute-start | bytes 196616 | tf_op jit(solution)/shard_map/ppermute | solution.py:357
  6.5 3.4 %shard_map.94 = (f32[1024,256]{1,0:T(8,128)S(1)}, f32[1024,256]{1,0:T(8,128)S(1)}, f32[17,1024]{1,0:T(8,128)S(1)}, bf16[2,4,1024,256]{3,2,1,0:T(8,128)(2,1)S(1)}...) custom-call(bf16[1024,256]{1,0:T(8,128)(2,1)S(1)} %get-tuple-element.31.quer, ...), custom_call_target="tpu_custom_call" | custom-call | flops 2147483648 | bytes 8388608 | tf_op jit(solution)/shard_map/pallas_call | solution.py:395
  9.8 1.0 %shard_map.95 = (bf16[1024,256]{1,0:T(8,128)(2,1)S(1)}, f32[17,1024]{1,0:T(8,128)S(1)}) custom-call(bf16[1024,256]{1,0:T(8,128)(2,1)S(1)} %get-tuple-element.31.query_ref, bf16[1024,256]{1,0:T(8,128)(2,1)S(1)} %get-tuple-element.29.key_ref.refs_0_, bf16[1024,256]{1,0:T(8,128)(2,1)S(1)} %get-tuple-element.32.grad_ref, ...), custom_call_target="tpu_custom_call" | custom-call | flops 536870912 | bytes 6291456 | tf_op jit(solution)/shard_map/pallas_call | solution.py:398
  10.9 1.6 %collective-permute-start.6 = (f32[17,1024]{1,0:T(8,128)S(1)}, f32[17,1024]{1,0:T(8,128)S(1)}, u32[]{:S(2)}, u32[]{:S(2)}) collective-permute-start(f32[17,1024]{1,0:T(8,128)S(1)} %get-tuple-element.48), channel_id=1, source_target_pairs={{0,2},{1,3},{2,0},{3,1},{4,6},{5,7},{6,4},{7,5},{8,10},{9,11},{10,... | collective-permute-start | bytes 208904 | tf_op jit(solution)/shard_map/ppermute | solution.py:357
  12.4 0.3 %collective-permute-start.3 = (f32[128,128]{1,0:T(8,128)S(1)}, f32[128,128]{1,0:T(8,128)S(1)}, u32[]{:S(2)}, u32[]{:S(2)}) collective-permute-start(f32[128,128]{1,0:T(8,128)S(1)} %get-tuple-element.45), channel_id=1, source_target_pairs={{0,16},{4,20},{8,24},{12,28},{16,0},{20,4},{24,8},{28,12},{1,17},{... | collective-permute-start | bytes 196616 | tf_op jit(solution)/shard_map/ppermute | solution.py:357
  12.8 0.0 collective-permute-done
  12.8 1.6 %collective-permute-start.1 = (f32[128,128]{1,0:T(8,128)S(1)}, f32[128,128]{1,0:T(8,128)S(1)}, u32[]{:S(2)}, u32[]{:S(2)}) collective-permute-start(f32[128,128]{1,0:T(8,128)S(1)} %add.21), channel_id=1, source_target_pairs={{0,8},{4,12},{8,0},{12,4},{16,24},{20,28},{24,16},{28,20},{1,9},{5... | collective-permute-start | bytes 196616 | tf_op jit(solution)/shard_map/ppermute | solution.py:357
  14.4 3.3 %collective-permute-done.3 = f32[128,128]{1,0:T(8,128)S(1)} collective-permute-done((f32[128,128]{1,0:T(8,128)S(1)}, f32[128,128]{1,0:T(8,128)S(1)}, u32[]{:S(2)}, u32[]{:S(2)}) %collective-permute-start.3) | collective-permute-done | bytes 65568 | tf_op jit(solution)/shard_map/ppermute | solution.py:357
  17.7 1.5 %collective-permute-start.4 = (f32[128,128]{1,0:T(8,128)S(1)}, f32[128,128]{1,0:T(8,128)S(1)}, u32[]{:S(2)}, u32[]{:S(2)}) collective-permute-start(f32[128,128]{1,0:T(8,128)S(1)} %add.24), channel_id=1, source_target_pairs={{0,8},{4,12},{8,0},{12,4},{16,24},{20,28},{24,16},{28,20},{1,9},{5... | collective-permute-start | bytes 196616 | tf_op jit(solution)/shard_map/ppermute | solution.py:357
  19.3 0.0 collective-permute-done.6
  19.3 0.1 collective-permute-start.7
  19.4 0.0 collective-permute-done.1
  19.4 1.6 %collective-permute-start.2 = (f32[128,128]{1,0:T(8,128)S(1)}, f32[128,128]{1,0:T(8,128)S(1)}, u32[]{:S(2)}, u32[]{:S(2)}) collective-permute-start(f32[128,128]{1,0:T(8,128)S(1)} %get-tuple-element.56), channel_id=1, source_target_pairs={{0,4},{4,0},{8,12},{12,8},{16,20},{20,16},{24,28},{28,24},{1,5},{5... | collective-permute-start | bytes 196616 | tf_op jit(solution)/shard_map/ppermute | solution.py:357
  21.0 1.1 %collective-permute-done.4 = f32[128,128]{1,0:T(8,128)S(1)} collective-permute-done((f32[128,128]{1,0:T(8,128)S(1)}, f32[128,128]{1,0:T(8,128)S(1)}, u32[]{:S(2)}, u32[]{:S(2)}) %collective-permute-start.4) | collective-permute-done | bytes 65568 | tf_op jit(solution)/shard_map/ppermute | solution.py:357
  22.1 1.6 %collective-permute-start.5 = (f32[128,128]{1,0:T(8,128)S(1)}, f32[128,128]{1,0:T(8,128)S(1)}, u32[]{:S(2)}, u32[]{:S(2)}) collective-permute-start(f32[128,128]{1,0:T(8,128)S(1)} %get-tuple-element.54), channel_id=1, source_target_pairs={{0,4},{4,0},{8,12},{12,8},{16,20},{20,16},{24,28},{28,24},{1,5},{5... | collective-permute-start | bytes 196616 | tf_op jit(solution)/shard_map/ppermute | solution.py:357
  23.7 0.4 %collective-permute-done.2.refs_5_.refs_6_ = f32[128,128]{1,0:T(8,128)S(1)} collective-permute-done((f32[128,128]{1,0:T(8,128)S(1)}, f32[128,128]{1,0:T(8,128)S(1)}, u32[]{:S(2)}, u32[]{:S(2)}) %collective-permute-start.2) | collective-permute-done | bytes 65568 | tf_op jit(solution)/shard_map/ppermute | solution.py:357
  24.0 1.0 %shard_map.96 = (bf16[1024,256]{1,0:T(8,128)(2,1)}, bf16[1024,256]{1,0:T(8,128)(2,1)}, bf16[1024,256]{1,0:T(8,128)(2,1)}) custom-call(bf16[1024,256]{1,0:T(8,128)(2,1)S(1)} %get-tuple-element.29.key_ref.refs_0_, bf16[1024,256]{1,0:T(8,128)(2,1)S(1)} %get-tuple-element.30.value_ref.refs_1_, f32[1024,256]{1,0:T(8,128)S(1)} %get-tuple-element.35.refs_2_, ...), custom_call_target="tpu_custom_call" | custom-call | tf_op jit(solution)/shard_map/pallas_call | solution.py:441
  25.1 0.0 collective-permute-done.7.refs_9_
  25.1 1.3 %collective-permute-done.5.refs_7_ = f32[128,128]{1,0:T(8,128)S(1)} collective-permute-done((f32[128,128]{1,0:T(8,128)S(1)}, f32[128,128]{1,0:T(8,128)S(1)}, u32[]{:S(2)}, u32[]{:S(2)}) %collective-permute-start.5) | collective-permute-done | bytes 65568 | tf_op jit(solution)/shard_map/ppermute | solution.py:357
  26.4 1.0 %shard_map.97 = (bf16[1024,256]{1,0:T(8,128)(2,1)}, bf16[1024,256]{1,0:T(8,128)(2,1)}, f32[17,1024]{1,0:T(8,128)}) custom-call(bf16[1024,256]{1,0:T(8,128)(2,1)S(1)} %get-tuple-element.29.key_ref.refs_0_, bf16[1024,256]{1,0:T(8,128)(2,1)S(1)} %get-tuple-element.30.value_ref.refs_1_, ...), custom_call_target="tpu_custom_call", output_to_operand_aliasing={{0}: (10, {}), {1}: (11, {})} | custom-call | tf_op jit(solution)/shard_map/pallas_call | solution.py:443
  (5 shorter events, 0.1 us)
Async XLA Ops:
  2.3 10.4 %collective-permute-start = (f32[128,128]{1,0:T(8,128)S(1)}, f32[128,128]{1,0:T(8,128)S(1)}, u32[]{:S(2)}, u32[]{:S(2)}) collective-permute-start(f32[128,128]{1,0:T(8,128)S(1)} %get-tuple-element.37), channel_id=1, source_target_pairs={{0,16},{4,20},{8,24},{12,28},{16,0},{20,4},{24,8},{28,12},{1,17},{... | collective-permute-start | bytes 196616 | tf_op jit(solution)/shard_map/ppermute | solution.py:357
  10.9 8.4 %collective-permute-start.6 = (f32[17,1024]{1,0:T(8,128)S(1)}, f32[17,1024]{1,0:T(8,128)S(1)}, u32[]{:S(2)}, u32[]{:S(2)}) collective-permute-start(f32[17,1024]{1,0:T(8,128)S(1)} %get-tuple-element.48), channel_id=1, source_target_pairs={{0,2},{1,3},{2,0},{3,1},{4,6},{5,7},{6,4},{7,5},{8,10},{9,11},{10,... | collective-permute-start | bytes 208904 | tf_op jit(solution)/shard_map/ppermute | solution.py:357
  12.4 5.3 %collective-permute-start.3 = (f32[128,128]{1,0:T(8,128)S(1)}, f32[128,128]{1,0:T(8,128)S(1)}, u32[]{:S(2)}, u32[]{:S(2)}) collective-permute-start(f32[128,128]{1,0:T(8,128)S(1)} %get-tuple-element.45), channel_id=1, source_target_pairs={{0,16},{4,20},{8,24},{12,28},{16,0},{20,4},{24,8},{28,12},{1,17},{... | collective-permute-start | bytes 196616 | tf_op jit(solution)/shard_map/ppermute | solution.py:357
  12.8 6.6 %collective-permute-start.1 = (f32[128,128]{1,0:T(8,128)S(1)}, f32[128,128]{1,0:T(8,128)S(1)}, u32[]{:S(2)}, u32[]{:S(2)}) collective-permute-start(f32[128,128]{1,0:T(8,128)S(1)} %add.21), channel_id=1, source_target_pairs={{0,8},{4,12},{8,0},{12,4},{16,24},{20,28},{24,16},{28,20},{1,9},{5... | collective-permute-start | bytes 196616 | tf_op jit(solution)/shard_map/ppermute | solution.py:357
  17.7 4.3 %collective-permute-start.4 = (f32[128,128]{1,0:T(8,128)S(1)}, f32[128,128]{1,0:T(8,128)S(1)}, u32[]{:S(2)}, u32[]{:S(2)}) collective-permute-start(f32[128,128]{1,0:T(8,128)S(1)} %add.24), channel_id=1, source_target_pairs={{0,8},{4,12},{8,0},{12,4},{16,24},{20,28},{24,16},{28,20},{1,9},{5... | collective-permute-start | bytes 196616 | tf_op jit(solution)/shard_map/ppermute | solution.py:357
  19.3 5.8 %collective-permute-start.7 = (f32[17,1024]{1,0:T(8,128)S(1)}, f32[17,1024]{1,0:T(8,128)S(1)}, u32[]{:S(2)}, u32[]{:S(2)}) collective-permute-start(f32[17,1024]{1,0:T(8,128)S(1)} %add.27.refs_8_), channel_id=1, source_target_pairs={{0,1},{1,0},{2,3},{3,2},{4,5},{5,4},{6,7},{7,6},{8,9},{9,8},{10,11... | collective-permute-start | bytes 208904 | tf_op jit(solution)/shard_map/ppermute | solution.py:357
  19.4 4.6 %collective-permute-start.2 = (f32[128,128]{1,0:T(8,128)S(1)}, f32[128,128]{1,0:T(8,128)S(1)}, u32[]{:S(2)}, u32[]{:S(2)}) collective-permute-start(f32[128,128]{1,0:T(8,128)S(1)} %get-tuple-element.56), channel_id=1, source_target_pairs={{0,4},{4,0},{8,12},{12,8},{16,20},{20,16},{24,28},{28,24},{1,5},{5... | collective-permute-start | bytes 196616 | tf_op jit(solution)/shard_map/ppermute | solution.py:357
  22.1 4.3 %collective-permute-start.5 = (f32[128,128]{1,0:T(8,128)S(1)}, f32[128,128]{1,0:T(8,128)S(1)}, u32[]{:S(2)}, u32[]{:S(2)}) collective-permute-start(f32[128,128]{1,0:T(8,128)S(1)} %get-tuple-element.54), channel_id=1, source_target_pairs={{0,4},{4,0},{8,12},{12,8},{16,20},{20,16},{24,28},{28,24},{1,5},{5... | collective-permute-start | bytes 196616 | tf_op jit(solution)/shard_map/ppermute | solution.py:357

commit v7 on v6

--- a/solution.py
+++ b/solution.py
@@ -252,11 +252,6 @@
     value_width = grad_ref.shape[1] // head_count
     wide = grad_weights_ref.shape[3]
     coef_out[:local_levels, :] = coef_ref[:local_levels, :]
-    level_count = coef_out.shape[0]
-    if local_levels + cross_levels < level_count:
-        coef_out[local_levels + cross_levels :, :] = jnp.zeros(
-            (level_count - local_levels - cross_levels, tokens), jnp.float32
-        )
     for t_start in range(0, tokens, wide):
         t_end = t_start + wide
         t_slice = slice(t_start, t_end)
@@ -294,7 +289,10 @@
     if last:
         coef_ref, coef_received = refs[-11:-9]
         key_out, value_out, coef_out, key_total, value_total, coef_total, sems = refs[-7:]
-        coef_total[...] = coef_ref[...] + coef_received[...]
+        used = coef_ref.shape[0]
+        coef_total[:used, :] = coef_ref[...] + coef_received[...]
+        if used < coef_total.shape[0]:
+            coef_total[used:, :] = jnp.zeros((coef_total.shape[0] - used, tokens), jnp.float32)
         copies.append(pltpu.make_async_copy(coef_total, coef_out, sems.at[0]))
         copies[0].start()
     else:
@@ -385,7 +383,7 @@
         out_specs=[vmem] * 2,
         out_shape=[
             jax.ShapeDtypeStruct(queries.shape, jnp.bfloat16),
-            jax.ShapeDtypeStruct(level_coef.shape, jnp.float32),
+            jax.ShapeDtypeStruct((local_levels + bit_count, tokens), jnp.float32),
         ],
         scratch_shapes=[pltpu.VMEM((head_count, key_width, tokens), jnp.bfloat16)],
         compiler_params=pltpu.CompilerParams(vmem_limit_bytes=12 * MIB),

time: 27.6 us -> 24.7 us (0.89)
  waiting for transfers between devices: 6.05 us -> 4.06 us
  starting transfers between devices: 12.4 us -> 11.6 us
    ppermute x8, waiting for transfers between devices: 6.05 us -> 4.06 us  [exchange(): return lax.ppermute(value, axis, pairs)]
    ppermute x8, starting transfers between devices: 12.4 us -> 11.6 us  [exchange(): return lax.ppermute(value, axis, pairs)]
  transfers between devices with their start and end apart: 8 -> 8, of which waited for: 4 -> 4; matrix products, arithmetic and copies ran while one was open for 0% -> 0% of each run, Pallas kernels for 20% -> 22%
where the time goes in v7:
time: 24.7 us; the launch traced here: 24.6 us
  starting transfers between devices  11.6 us (47%)
  Pallas kernels  8.15 us (33%)
  waiting for transfers between devices  4.06 us (16%)
  between operations  0.7 us (3%)
    ppermute x8, starting transfers between devices, exchange(): return lax.ppermute(value, axis, pairs)  11.6 us
    ppermute x8, waiting for transfers between devices, exchange(): return lax.ppermute(value, axis, pairs)  4.06 us
    pallas_call x1, Pallas kernels, shards(): local_call(query_in, key_in, value_in, grad_in, gates_in, grad_t)  3.39 us
    pallas_call x1, Pallas kernels, shards(): pl.pallas_call(functools.partial(top_kernel, head_count, bit_count - 1, l...  1.68 us
    pallas_call x1, Pallas kernels, shards(): apply_call(early, 1, False)(*common, grad_state[0], received[0], query_grad)  1.03 us
    pallas_call x1, Pallas kernels, shards(): apply_call(late, 2, True)  1.03 us
    pallas_call x1, Pallas kernels, shards(): query_call(query_in, key_in, grad_in, gates_in, states_in, grad_weights,...  1.02 us
  transfers between devices with their start and end apart: 8, of which 4 were waited for; matrix products, arithmetic and copies ran while one was open for 0% of the time, Pallas kernels for 22%

profile of v7, /device:TPU:0, one launch (start us, length us, event | category | flops | bytes accessed | tf_op | source)
XLA Modules:
  0.0 24.6 jit_solution(15503313324591964928)
XLA Ops:
  0.6 1.7 %shard_map.93 = (bf16[1024,256]{1,0:T(8,128)(2,1)S(1)}, bf16[1024,256]{1,0:T(8,128)(2,1)S(1)}, bf16[1024,256]{1,0:T(8,128)(2,1)S(1)}, bf16[1024,256]{1,0:T(8,128...) custom-call(bf16[1024,256]{1,0:T(8,128)(2,1)} %refs_0_.1, ...), custom_call_target="tpu_custom_call" | custom-call | tf_op jit(solution)/shard_map/pallas_call | solution.py:341
  2.3 4.1 %collective-permute-start = (f32[128,128]{1,0:T(8,128)S(1)}, f32[128,128]{1,0:T(8,128)S(1)}, u32[]{:S(2)}, u32[]{:S(2)}) collective-permute-start(f32[128,128]{1,0:T(8,128)S(1)} %get-tuple-element.37), channel_id=1, source_target_pairs={{0,16},{4,20},{8,24},{12,28},{16,0},{20,4},{24,8},{28,12},{1,17},{... | collective-permute-start | bytes 196616 | tf_op jit(solution)/shard_map/ppermute | solution.py:355
  6.5 0.1 collective-permute-start.3
  6.5 3.4 %shard_map.94 = (f32[1024,256]{1,0:T(8,128)S(1)}, f32[1024,256]{1,0:T(8,128)S(1)}, f32[17,1024]{1,0:T(8,128)S(1)}, bf16[2,4,1024,256]{3,2,1,0:T(8,128)(2,1)S(1)}...) custom-call(bf16[1024,256]{1,0:T(8,128)(2,1)S(1)} %get-tuple-element.31.quer, ...), custom_call_target="tpu_custom_call" | custom-call | flops 2147483648 | bytes 8388608 | tf_op jit(solution)/shard_map/pallas_call | solution.py:393
  9.9 0.2 collective-permute-done
  10.2 2.1 %collective-permute-start.1 = (f32[128,128]{1,0:T(8,128)S(1)}, f32[128,128]{1,0:T(8,128)S(1)}, u32[]{:S(2)}, u32[]{:S(2)}) collective-permute-start(f32[128,128]{1,0:T(8,128)S(1)} %add.21), channel_id=1, source_target_pairs={{0,8},{4,12},{8,0},{12,4},{16,24},{20,28},{24,16},{28,20},{1,9},{5... | collective-permute-start | bytes 196616 | tf_op jit(solution)/shard_map/ppermute | solution.py:355
  12.2 1.0 %shard_map.95 = (bf16[1024,256]{1,0:T(8,128)(2,1)S(1)}, f32[14,1024]{1,0:T(8,128)S(1)}) custom-call(bf16[1024,256]{1,0:T(8,128)(2,1)S(1)} %get-tuple-element.31.query_ref, bf16[1024,256]{1,0:T(8,128)(2,1)S(1)} %get-tuple-element.29.key_ref.refs_0_, bf16[1024,256]{1,0:T(8,128)(2,1)S(1)} %get-tuple-element.32.grad_ref, ...), custom_call_target="tpu_custom_call" | custom-call | flops 536870912 | bytes 6291456 | tf_op jit(solution)/shard_map/pallas_call | solution.py:396
  13.3 1.6 %collective-permute-start.6 = (f32[14,1024]{1,0:T(8,128)S(1)}, f32[14,1024]{1,0:T(8,128)S(1)}, u32[]{:S(2)}, u32[]{:S(2)}) collective-permute-start(f32[14,1024]{1,0:T(8,128)S(1)} %get-tuple-element.48), channel_id=1, source_target_pairs={{0,2},{1,3},{2,0},{3,1},{4,6},{5,7},{6,4},{7,5},{8,10},{9,11},{10,... | collective-permute-start | bytes 172040 | tf_op jit(solution)/shard_map/ppermute | solution.py:355
  14.8 0.0 collective-permute-done.3
  14.8 0.5 %collective-permute-start.4 = (f32[128,128]{1,0:T(8,128)S(1)}, f32[128,128]{1,0:T(8,128)S(1)}, u32[]{:S(2)}, u32[]{:S(2)}) collective-permute-start(f32[128,128]{1,0:T(8,128)S(1)} %add.24), channel_id=1, source_target_pairs={{0,8},{4,12},{8,0},{12,4},{16,24},{20,28},{24,16},{28,20},{1,9},{5... | collective-permute-start | bytes 196616 | tf_op jit(solution)/shard_map/ppermute | solution.py:355
  15.4 0.0 collective-permute-done.1
  15.4 1.6 %collective-permute-start.2 = (f32[128,128]{1,0:T(8,128)S(1)}, f32[128,128]{1,0:T(8,128)S(1)}, u32[]{:S(2)}, u32[]{:S(2)}) collective-permute-start(f32[128,128]{1,0:T(8,128)S(1)} %get-tuple-element.56), channel_id=1, source_target_pairs={{0,4},{4,0},{8,12},{12,8},{16,20},{20,16},{24,28},{28,24},{1,5},{5... | collective-permute-start | bytes 196616 | tf_op jit(solution)/shard_map/ppermute | solution.py:355
  17.0 2.2 %collective-permute-done.4 = f32[128,128]{1,0:T(8,128)S(1)} collective-permute-done((f32[128,128]{1,0:T(8,128)S(1)}, f32[128,128]{1,0:T(8,128)S(1)}, u32[]{:S(2)}, u32[]{:S(2)}) %collective-permute-start.4) | collective-permute-done | bytes 65568 | tf_op jit(solution)/shard_map/ppermute | solution.py:355
  19.2 1.6 %collective-permute-start.5 = (f32[128,128]{1,0:T(8,128)S(1)}, f32[128,128]{1,0:T(8,128)S(1)}, u32[]{:S(2)}, u32[]{:S(2)}) collective-permute-start(f32[128,128]{1,0:T(8,128)S(1)} %get-tuple-element.54), channel_id=1, source_target_pairs={{0,4},{4,0},{8,12},{12,8},{16,20},{20,16},{24,28},{28,24},{1,5},{5... | collective-permute-start | bytes 196616 | tf_op jit(solution)/shard_map/ppermute | solution.py:355
  20.8 0.0 collective-permute-done.6
  20.8 0.1 collective-permute-start.7
  20.9 0.0 collective-permute-done.2.refs_5_.refs_6_
  20.9 1.0 %shard_map.96 = (bf16[1024,256]{1,0:T(8,128)(2,1)}, bf16[1024,256]{1,0:T(8,128)(2,1)}, bf16[1024,256]{1,0:T(8,128)(2,1)}) custom-call(bf16[1024,256]{1,0:T(8,128)(2,1)S(1)} %get-tuple-element.29.key_ref.refs_0_, bf16[1024,256]{1,0:T(8,128)(2,1)S(1)} %get-tuple-element.30.value_ref.refs_1_, f32[1024,256]{1,0:T(8,128)S(1)} %get-tuple-element.35.refs_2_, ...), custom_call_target="tpu_custom_call" | custom-call | tf_op jit(solution)/shard_map/pallas_call | solution.py:439
  21.9 0.2 collective-permute-done.7.refs_9_
  22.1 1.4 %collective-permute-done.5.refs_7_ = f32[128,128]{1,0:T(8,128)S(1)} collective-permute-done((f32[128,128]{1,0:T(8,128)S(1)}, f32[128,128]{1,0:T(8,128)S(1)}, u32[]{:S(2)}, u32[]{:S(2)}) %collective-permute-start.5) | collective-permute-done | bytes 65568 | tf_op jit(solution)/shard_map/ppermute | solution.py:355
  23.5 1.0 %shard_map.97 = (bf16[1024,256]{1,0:T(8,128)(2,1)}, bf16[1024,256]{1,0:T(8,128)(2,1)}, f32[17,1024]{1,0:T(8,128)}) custom-call(bf16[1024,256]{1,0:T(8,128)(2,1)S(1)} %get-tuple-element.29.key_ref.refs_0_, bf16[1024,256]{1,0:T(8,128)(2,1)S(1)} %get-tuple-element.30.value_ref.refs_1_, ...), custom_call_target="tpu_custom_call", output_to_operand_aliasing={{0}: (10, {}), {1}: (11, {})} | custom-call | tf_op jit(solution)/shard_map/pallas_call | solution.py:441
  (5 shorter events, 0.1 us)
Async XLA Ops:
  2.3 7.8 %collective-permute-start = (f32[128,128]{1,0:T(8,128)S(1)}, f32[128,128]{1,0:T(8,128)S(1)}, u32[]{:S(2)}, u32[]{:S(2)}) collective-permute-start(f32[128,128]{1,0:T(8,128)S(1)} %get-tuple-element.37), channel_id=1, source_target_pairs={{0,16},{4,20},{8,24},{12,28},{16,0},{20,4},{24,8},{28,12},{1,17},{... | collective-permute-start | bytes 196616 | tf_op jit(solution)/shard_map/ppermute | solution.py:355
  6.5 8.4 %collective-permute-start.3 = (f32[128,128]{1,0:T(8,128)S(1)}, f32[128,128]{1,0:T(8,128)S(1)}, u32[]{:S(2)}, u32[]{:S(2)}) collective-permute-start(f32[128,128]{1,0:T(8,128)S(1)} %get-tuple-element.45), channel_id=1, source_target_pairs={{0,16},{4,20},{8,24},{12,28},{16,0},{20,4},{24,8},{28,12},{1,17},{... | collective-permute-start | bytes 196616 | tf_op jit(solution)/shard_map/ppermute | solution.py:355
  10.2 5.2 %collective-permute-start.1 = (f32[128,128]{1,0:T(8,128)S(1)}, f32[128,128]{1,0:T(8,128)S(1)}, u32[]{:S(2)}, u32[]{:S(2)}) collective-permute-start(f32[128,128]{1,0:T(8,128)S(1)} %add.21), channel_id=1, source_target_pairs={{0,8},{4,12},{8,0},{12,4},{16,24},{20,28},{24,16},{28,20},{1,9},{5... | collective-permute-start | bytes 196616 | tf_op jit(solution)/shard_map/ppermute | solution.py:355
  13.3 7.5 %collective-permute-start.6 = (f32[14,1024]{1,0:T(8,128)S(1)}, f32[14,1024]{1,0:T(8,128)S(1)}, u32[]{:S(2)}, u32[]{:S(2)}) collective-permute-start(f32[14,1024]{1,0:T(8,128)S(1)} %get-tuple-element.48), channel_id=1, source_target_pairs={{0,2},{1,3},{2,0},{3,1},{4,6},{5,7},{6,4},{7,5},{8,10},{9,11},{10,... | collective-permute-start | bytes 172040 | tf_op jit(solution)/shard_map/ppermute | solution.py:355
  14.8 4.3 %collective-permute-start.4 = (f32[128,128]{1,0:T(8,128)S(1)}, f32[128,128]{1,0:T(8,128)S(1)}, u32[]{:S(2)}, u32[]{:S(2)}) collective-permute-start(f32[128,128]{1,0:T(8,128)S(1)} %add.24), channel_id=1, source_target_pairs={{0,8},{4,12},{8,0},{12,4},{16,24},{20,28},{24,16},{28,20},{1,9},{5... | collective-permute-start | bytes 196616 | tf_op jit(solution)/shard_map/ppermute | solution.py:355
  15.4 5.5 %collective-permute-start.2 = (f32[128,128]{1,0:T(8,128)S(1)}, f32[128,128]{1,0:T(8,128)S(1)}, u32[]{:S(2)}, u32[]{:S(2)}) collective-permute-start(f32[128,128]{1,0:T(8,128)S(1)} %get-tuple-element.56), channel_id=1, source_target_pairs={{0,4},{4,0},{8,12},{12,8},{16,20},{20,16},{24,28},{28,24},{1,5},{5... | collective-permute-start | bytes 196616 | tf_op jit(solution)/shard_map/ppermute | solution.py:355
  19.2 4.3 %collective-permute-start.5 = (f32[128,128]{1,0:T(8,128)S(1)}, f32[128,128]{1,0:T(8,128)S(1)}, u32[]{:S(2)}, u32[]{:S(2)}) collective-permute-start(f32[128,128]{1,0:T(8,128)S(1)} %get-tuple-element.54), channel_id=1, source_target_pairs={{0,4},{4,0},{8,12},{12,8},{16,20},{20,16},{24,28},{28,24},{1,5},{5... | collective-permute-start | bytes 196616 | tf_op jit(solution)/shard_map/ppermute | solution.py:355
  20.8 1.3 %collective-permute-start.7 = (f32[14,1024]{1,0:T(8,128)S(1)}, f32[14,1024]{1,0:T(8,128)S(1)}, u32[]{:S(2)}, u32[]{:S(2)}) collective-permute-start(f32[14,1024]{1,0:T(8,128)S(1)} %add.27.refs_8_), channel_id=1, source_target_pairs={{0,1},{1,0},{2,3},{3,2},{4,5},{5,4},{6,7},{7,6},{8,9},{9,8},{10,11... | collective-permute-start | bytes 172040 | tf_op jit(solution)/shard_map/ppermute | solution.py:355
